TPU v7x, 32 devices: a whole 2x2x4 slice. The times are simulated.
32 devices in a mesh: rep: 2 (over core), dp: 4 (over y, x), seq: 4 (over z).
Axes of the slice: x: 2, y: 2, z: 4, core: 2. Of those that a mesh axis runs over, the one named last changes fastest.
Arguments:
- tokens: bfloat16 [2, 4, 2048, 2048], P(None, 'dp', ('rep', 'seq')), may hold values from -6 to 6
- lengths: int32 [2, 4], P(None, 'dp'), may hold values from 512 to 2048, as said below
- memory: float32 [2, 4, 16, 128, 128], P(None, 'dp'), may hold values from -48 to 48
- normalizer: float32 [2, 4, 16, 128], P(None, 'dp'), may hold values from 0.5 to 4
- qkv_weight: bfloat16 [6144, 2048], P(('dp', 'seq')), may hold values from -0.1875 to 0.1875
- out_weight: bfloat16 [2048, 2048], P(('dp', 'seq')), may hold values from -0.375 to 0.375
- norm_gains: bfloat16 [2, 2048], P(None, ('dp', 'seq')), may hold values from 0.5 to 1.5
- gate_logit: float32 [16], replicated, may hold values from -2 to 2
- inner_weight: bfloat16 [8192, 4096], P(('dp', 'seq')), may hold values from -0.125 to 0.125
- down_weight: bfloat16 [8192, 2048], P(('dp', 'seq')), may hold values from -0.125 to 0.125
- cotangent: bfloat16 [2, 4, 2048, 2048], P(None, 'dp', ('rep', 'seq')), may hold values from -6 to 6
Outputs:
- output: bfloat16 [2, 4, 2048, 2048], P(None, 'dp', ('rep', 'seq'))
- new_memory: float32 [2, 4, 16, 128, 128], P(None, 'dp', ('rep', 'seq'))
- new_normalizer: float32 [2, 4, 16, 128], P(None, 'dp', ('rep', 'seq'))
- grad_tokens: bfloat16 [2, 4, 2048, 2048], P(None, 'dp', ('rep', 'seq'))
- grad_qkv: float32 [6144, 2048], P(('dp', 'seq'))
- grad_out: float32 [2048, 2048], P(('dp', 'seq'))
- grad_gains: float32 [2, 2048], P(None, ('dp', 'seq'))
- grad_gate: float32 [16], replicated
- grad_inner: float32 [8192, 4096], P(('dp', 'seq'))
- grad_down: float32 [8192, 2048], P(('dp', 'seq'))
Inputs may be any that keep to these rules, and one draw needn't show every extreme that they name: `lengths`: in every draw some sequence has length 2048 and some has 512.
All inputs are finite; a program needn't handle non-finite values.
Results may differ from a plain program's by a relative error of at most 0.018.
The roundings to bfloat16 on the way count: a program that leaves them out, or rounds other values in their place, can miss the bound.
Values may be sent and summed in bfloat16 or wider, within the bound.
A program may use at most 640 MiB of HBM per device.

v0:
```python
import jax
import jax.numpy as jnp
from jax import lax
from jax.sharding import PartitionSpec as P

EPSILON = 1e-05
HIGHEST = lax.Precision.HIGHEST


def contract(left_side, right_side):
    return lax.dot_general(
        left_side, right_side, (((1,), (1,)), ((), ())), preferred_element_type=jnp.float32
    )


def across(left_side, right_side):
    return lax.dot_general(
        left_side, right_side, (((0,), (0,)), ((), ())), preferred_element_type=jnp.float32
    )


def inverse_rms(values):
    return lax.rsqrt(jnp.mean(values * values, axis=-1, keepdims=True) + EPSILON)


def norm_back(grad_normed, normed, scale):
    return scale * (grad_normed - normed * jnp.mean(grad_normed * normed, axis=-1, keepdims=True))


def silu_back(grad_hidden, gates, up_values):
    sigmoid = jax.nn.sigmoid(gates)
    grad_gate = grad_hidden * up_values * sigmoid * (1.0 + gates * (1.0 - sigmoid))
    grad_up = grad_hidden * jax.nn.silu(gates)
    return (grad_gate.astype(jnp.bfloat16), grad_up.astype(jnp.bfloat16))


def spread_terms(attn_terms):
    return (
        lax.psum_scatter(attn_terms[0], ("dp", "seq"), scatter_dimension=0, tiled=True),
        lax.psum_scatter(attn_terms[1], ("dp", "seq"), scatter_dimension=0, tiled=True),
        lax.psum_scatter(attn_terms[2], ("dp", "seq"), scatter_dimension=1, tiled=True),
    )


def shards(
    tokens,
    lengths,
    memory,
    normalizer,
    qkv_weight,
    out_weight,
    norm_gains,
    gate_logit,
    inner_weight,
    down_weight,
    cotangent,
):
    span_rows = tokens.shape[2]
    model_width = tokens.shape[3]
    head_count = gate_logit.shape[0]
    head_dim = model_width // head_count
    seq_parts = lax.axis_size(("rep", "seq"))
    full_length = span_rows * seq_parts
    local_units = inner_weight.shape[0]
    heads_here = head_count // seq_parts
    score_scale = head_dim ** (-0.5)
    qkv_all, out_all, gains_all = (
        lax.all_gather(qkv_weight, ("dp", "seq"), axis=0, tiled=True),
        lax.all_gather(out_weight, ("dp", "seq"), axis=0, tiled=True),
        lax.all_gather(norm_gains, ("dp", "seq"), axis=1, tiled=True),
    )
    gain_one = gains_all[0].astype(jnp.float32)
    gain_two = gains_all[1].astype(jnp.float32)
    span_index = lax.axis_index(("rep", "seq"))
    positions = span_index * span_rows + jnp.arange(span_rows)
    key_positions = jnp.arange(full_length)
    gate_share = jax.nn.sigmoid(gate_logit)
    mixing = gate_share[None, :, None]
    gate_local = inner_weight[:, :model_width]
    up_local = inner_weight[:, model_width:]
    head_start = span_index * heads_here

    def one_micro(micro_carry, inputs):
        total_attn, total_inner, total_gate = micro_carry
        rows_in, length, mem_state, norm_state, grad_rows = inputs
        rows_float = rows_in.astype(jnp.float32)
        scale_one = inverse_rms(rows_float)
        normed_one = rows_float * scale_one
        hidden_one = (normed_one * gain_one).astype(jnp.bfloat16)
        projected = contract(hidden_one, qkv_all).astype(jnp.bfloat16)
        queries = projected[:, :model_width].reshape(span_rows, head_count, head_dim)
        key_rows = projected[:, model_width : 2 * model_width].reshape(
            span_rows, head_count, head_dim
        )
        value_rows = projected[:, 2 * model_width :].reshape(span_rows, head_count, head_dim)
        query_float = queries.astype(jnp.float32)
        query_sig = jax.nn.elu(query_float) + 1.0
        numerator = jnp.einsum("thd,hde->the", query_sig, mem_state, precision=HIGHEST)
        denominator = jnp.einsum("thd,hd->th", query_sig, norm_state, precision=HIGHEST)
        mem_read = numerator / denominator[..., None]
        keys_all, values_all = (
            lax.all_gather(key_rows, ("rep", "seq"), axis=0, tiled=True),
            lax.all_gather(value_rows, ("rep", "seq"), axis=0, tiled=True),
        )
        allowed = (key_positions[None, :] <= positions[:, None]) & (key_positions[None, :] < length)

        def attention_scores():
            raw_scores = (
                jnp.einsum("qhd,khd->hqk", queries, keys_all, preferred_element_type=jnp.float32)
                * score_scale
            )
            return jnp.where(allowed[None], raw_scores, -1e30)

        scores = attention_scores()
        row_max = jnp.max(scores, axis=-1, keepdims=True)
        shifted = jnp.exp(scores - row_max)
        row_total = jnp.sum(shifted, axis=-1, keepdims=True)
        probs_low = (shifted / row_total).astype(jnp.bfloat16)
        dot_read = jnp.einsum(
            "hqk,khd->qhd", probs_low, values_all, preferred_element_type=jnp.float32
        )
        mixed_low = (
            (mixing * mem_read + (1.0 - mixing) * dot_read)
            .reshape(span_rows, model_width)
            .astype(jnp.bfloat16)
        )
        after_attn = rows_float + contract(mixed_low, out_all)
        scale_two = inverse_rms(after_attn)
        normed_two = after_attn * scale_two
        hidden_two = (normed_two * gain_two).astype(jnp.bfloat16)
        rows_all = lax.all_gather(hidden_two, ("dp", "seq"), axis=0, tiled=True)
        gates_kept = contract(rows_all, gate_local)
        ups_kept = contract(rows_all, up_local)
        hidden_kept = (jax.nn.silu(gates_kept) * ups_kept).astype(jnp.bfloat16)
        mlp_out = lax.psum_scatter(
            jnp.dot(hidden_kept, down_weight, preferred_element_type=jnp.float32),
            ("dp", "seq"),
            scatter_dimension=0,
            tiled=True,
        )
        output_rows = (after_attn + mlp_out).astype(jnp.bfloat16)
        key_sig = jax.nn.elu(key_rows.astype(jnp.float32)) + 1.0
        recalled = (
            jnp.einsum("thd,hde->the", key_sig, mem_state, precision=HIGHEST)
            / jnp.einsum("thd,hd->th", key_sig, norm_state, precision=HIGHEST)[..., None]
        )
        live_rows = (positions < length).astype(jnp.float32)
        kept_sig = key_sig * live_rows[:, None, None]
        memory_term = jnp.einsum(
            "thd,the->hde", kept_sig, value_rows.astype(jnp.float32) - recalled, precision=HIGHEST
        )
        norm_term = jnp.sum(kept_sig, axis=0)
        memory_add, norm_add = (
            lax.psum_scatter(
                memory_term.astype(jnp.bfloat16), ("rep", "seq"), scatter_dimension=0, tiled=True
            ).astype(jnp.float32),
            lax.psum_scatter(
                norm_term.astype(jnp.bfloat16), ("rep", "seq"), scatter_dimension=0, tiled=True
            ).astype(jnp.float32),
        )
        new_state = lax.dynamic_slice_in_dim(mem_state, head_start, heads_here, 0) + memory_add
        new_norm = lax.dynamic_slice_in_dim(norm_state, head_start, heads_here, 0) + norm_add
        cot_live = grad_rows.astype(jnp.float32) * live_rows[:, None]
        grad_mlp = cot_live.astype(jnp.bfloat16)
        grad_all = lax.all_gather(grad_mlp, ("dp", "seq"), axis=0, tiled=True)
        grad_hidden = contract(grad_all, down_weight)
        grad_gates, grad_ups = silu_back(grad_hidden, gates_kept, ups_kept)
        inner_term = jnp.concatenate(
            [
                across(grad_gates, rows_all),
                across(grad_ups, rows_all),
                across(hidden_kept, grad_all),
            ],
            axis=1,
        )
        grad_two = lax.psum_scatter(
            jnp.dot(grad_gates, gate_local, preferred_element_type=jnp.float32)
            + jnp.dot(grad_ups, up_local, preferred_element_type=jnp.float32),
            ("dp", "seq"),
            scatter_dimension=0,
            tiled=True,
        )
        grad_after = cot_live + norm_back(grad_two * gain_two, normed_two, scale_two)
        grad_branch = grad_after.astype(jnp.bfloat16)
        grad_mixed = jnp.dot(grad_branch, out_all, preferred_element_type=jnp.float32).astype(
            jnp.bfloat16
        )
        grad_mixed_float = grad_mixed.astype(jnp.float32).reshape(span_rows, head_count, head_dim)
        grad_dot = (grad_mixed_float * (1.0 - mixing)).astype(jnp.bfloat16)
        gate_term = (
            jnp.sum(grad_mixed_float * (mem_read - dot_read), axis=(0, 2))
            * gate_share
            * (1.0 - gate_share)
        )
        probabilities = jnp.exp(attention_scores() - row_max) / row_total
        grad_probs = jnp.einsum(
            "qhd,khd->hqk", grad_dot, values_all, preferred_element_type=jnp.float32
        )
        inner_sum = jnp.sum(probabilities * grad_probs, axis=-1, keepdims=True)
        grad_scores = (probabilities * (grad_probs - inner_sum) * score_scale).astype(jnp.bfloat16)
        grad_query_dot = jnp.einsum(
            "hqk,khd->qhd", grad_scores, keys_all, preferred_element_type=jnp.float32
        )
        grad_keys_all = jnp.einsum(
            "hqk,qhd->khd", grad_scores, queries, preferred_element_type=jnp.float32
        )
        grad_values_all = jnp.einsum(
            "hqk,qhd->khd", probs_low, grad_dot, preferred_element_type=jnp.float32
        )
        grad_keys, grad_values = (
            lax.psum_scatter(
                grad_keys_all.astype(jnp.bfloat16), ("rep", "seq"), scatter_dimension=0, tiled=True
            ).astype(jnp.float32),
            lax.psum_scatter(
                grad_values_all.astype(jnp.bfloat16),
                ("rep", "seq"),
                scatter_dimension=0,
                tiled=True,
            ).astype(jnp.float32),
        )
        grad_read = grad_mixed_float * mixing
        grad_numer = grad_read / denominator[..., None]
        grad_denom = -jnp.sum(grad_read * numerator, axis=-1) / (denominator * denominator)
        grad_sig = (
            jnp.einsum("the,hde->thd", grad_numer, mem_state, precision=HIGHEST)
            + grad_denom[..., None] * norm_state[None]
        )
        elu_slope = jnp.where(query_float > 0.0, 1.0, jnp.exp(jnp.minimum(query_float, 0.0)))
        grad_queries = grad_query_dot + grad_sig * elu_slope
        grad_projected = jnp.concatenate(
            [
                grad_queries.reshape(span_rows, model_width),
                grad_keys.reshape(span_rows, model_width),
                grad_values.reshape(span_rows, model_width),
            ],
            axis=1,
        ).astype(jnp.bfloat16)
        grad_one = jnp.dot(grad_projected, qkv_all, preferred_element_type=jnp.float32)
        grad_tokens_rows = (
            grad_after + norm_back(grad_one * gain_one, normed_one, scale_one)
        ).astype(jnp.bfloat16)
        qkv_term = across(grad_projected, hidden_one)
        out_term = across(grad_branch, mixed_low)
        gains_term = jnp.stack(
            [jnp.sum(grad_one * normed_one, axis=0), jnp.sum(grad_two * normed_two, axis=0)]
        )
        attn_terms = (qkv_term, out_term, gains_term)
        total_attn = tuple((running + share for running, share in zip(total_attn, attn_terms)))
        total_inner = total_inner + inner_term
        total_gate = total_gate + gate_term
        return (
            (total_attn, total_inner, total_gate),
            (output_rows, new_state, new_norm, grad_tokens_rows),
        )

    attn_start = (
        jnp.zeros(qkv_all.shape, jnp.float32),
        jnp.zeros(out_all.shape, jnp.float32),
        jnp.zeros(gains_all.shape, jnp.float32),
    )
    carry_start = (
        attn_start,
        jnp.zeros((local_units, 3 * model_width), jnp.float32),
        jnp.zeros((head_count,), jnp.float32),
    )
    carry_end, stacked = lax.scan(
        one_micro,
        carry_start,
        (tokens[:, 0], lengths[:, 0], memory[:, 0], normalizer[:, 0], cotangent[:, 0]),
    )
    total_attn, total_inner, total_gate = carry_end
    total_attn = spread_terms(total_attn)
    grad_qkv, grad_out, grad_gains, grad_units = (
        lax.psum(total_attn[0].astype(jnp.bfloat16), "rep").astype(jnp.float32),
        lax.psum(total_attn[1].astype(jnp.bfloat16), "rep").astype(jnp.float32),
        lax.psum(total_attn[2].astype(jnp.bfloat16), "rep").astype(jnp.float32),
        lax.psum(total_inner.astype(jnp.bfloat16), "rep").astype(jnp.float32),
    )
    grad_gate = lax.psum(total_gate, ("rep", "dp", "seq"))
    outputs, memories, norm_states, grad_tokens = stacked
    return (
        outputs[:, None],
        memories[:, None],
        norm_states[:, None],
        grad_tokens[:, None],
        grad_qkv,
        grad_out,
        grad_gains,
        grad_gate,
        grad_units[:, : 2 * model_width],
        grad_units[:, 2 * model_width :],
    )


def solution(mesh):
    placed = (
        P(None, "dp", ("rep", "seq"), None),
        P(None, "dp"),
        P(None, "dp", None, None, None),
        P(None, "dp", None, None),
        P(("dp", "seq"), None),
        P(("dp", "seq"), None),
        P(None, ("dp", "seq")),
        P(),
        P(("dp", "seq"), None),
        P(("dp", "seq"), None),
        P(None, "dp", ("rep", "seq"), None),
    )
    return jax.shard_map(
        shards,
        mesh=mesh,
        in_specs=placed,
        out_specs=(
            P(None, "dp", ("rep", "seq"), None),
            P(None, "dp", ("rep", "seq"), None, None),
            P(None, "dp", ("rep", "seq"), None),
            P(None, "dp", ("rep", "seq"), None),
            P(("dp", "seq"), None),
            P(("dp", "seq"), None),
            P(None, ("dp", "seq")),
            P(),
            P(("dp", "seq"), None),
            P(("dp", "seq"), None),
        ),
        check_vma=False,
    )
```

profile of v0, /device:TPU:17, one launch (start us, length us, event | category | flops | bytes accessed | tf_op | source)
XLA Modules:
  0.0 6498.0 jit_solution(5619045800706865099)
XLA Ops:
  10.7 28.8 all_gather.37
  46.0 77.5 %all-gather.9.cloned.1.call-done = bf16[2048,2048]{1,0:T(8,128)(2,1)} async-done(((bf16[128,2048]{1,0:T(8,128)(2,1)}), bf16[2048,2048]{1,0:T(8,128)(2,1)}) %all-gather.9.cloned.1.call-update) | async-done | bytes 8388624 | tf_op jit(solution)/shard_map/all_gather | solution.py:69
  123.5 272.3 %all-gather.7.cloned.1.call-done = bf16[6144,2048]{1,0:T(8,128)(2,1)} async-done(((bf16[384,2048]{1,0:T(8,128)(2,1)}), bf16[6144,2048]{1,0:T(8,128)(2,1)}) %all-gather.7.cloned.1.call-update) | async-done | bytes 25165840 | tf_op jit(solution)/shard_map/all_gather | solution.py:68
  395.8 4903.2 %while.31 = (s32[]{:T(128)}, f32[6144,2048]{1,0:T(8,128)}, f32[2048,2048]{1,0:T(8,128)}, f32[2,2048]{1,0:T(2,128)}, f32[512,6144]{1,0:T(8,128)}, /*index=5*/f32[...) while((s32[]{:T(128)}, f32[6144,2048]{1,0:T(8,128)}, ...), condition=%wide.region_19.20_spmd.clone.clone, body=%wide.region_0.19_spmd.clone.clone.sunk | while | flops 119561093120 | bytes 1664443648 | solution.py:266
  428.7 65.7 %all-gather.13.cloned.1.call-done = bf16[2048,16,128]{2,0,1:T(8,128)(2,1)} async-done(((bf16[256,16,128]{2,0,1:T(8,128)(2,1)}), bf16[2048,16,128]{2,0,1:T(8,128)(2,1)}) %all-gather.13.cloned.1.call-update) | async-done | bytes 8388624 | tf_op jit(solution)/shard_map/while/body/eval_jaxpr/all_gather | solution.py:102
  513.3 63.9 all-gather.11.cloned.1.call-done
  603.9 165.8 %all-gather.17.cloned.1.call-done = bf16[4096,2048]{1,0:T(8,128)(2,1)} async-done(((bf16[256,2048]{1,0:T(8,128)(2,1)}), bf16[4096,2048]{1,0:T(8,128)(2,1)}) %all-gather.17.cloned.1.call-update) | async-done | bytes 16777232 | tf_op jit(solution)/shard_map/while/body/eval_jaxpr/all_gather | solution.py:165
  784.1 178.5 %all-gather.15.cloned.1.call-done = bf16[4096,2048]{1,0:T(8,128)(2,1)} async-done(((bf16[256,2048]{1,0:T(8,128)(2,1)}), bf16[4096,2048]{1,0:T(8,128)(2,1)}) %all-gather.15.cloned.1.call-update) | async-done | bytes 16777232 | tf_op jit(solution)/shard_map/while/body/eval_jaxpr/all_gather | solution.py:131
  978.0 24.1 multiply_convert_fusion.15
  1020.0 26.5 convolution_add_fusion.2
  1077.9 657.0 %reduce-scatter.17.cloned.1.call-done = f32[256,2048]{1,0:T(8,128)} async-done(((f32[4096,2048]{1,0:T(8,128)}), f32[256,2048]{1,0:T(8,128)}) %reduce-scatter.17.cloned.1.call-update) | async-done | bytes 2097168 | tf_op jit(solution)/shard_map/while/body/eval_jaxpr/reduce_scatter | solution.py:176
  1785.1 46.4 convert_bitcast_fusion.6
  1902.3 558.5 %reduce-scatter.23.cloned.1.call-done = f32[256,2048]{1,0:T(8,128)} async-done(((f32[4096,2048]{1,0:T(8,128)}), f32[256,2048]{1,0:T(8,128)}) %reduce-scatter.23.cloned.1.call-update) | async-done | bytes 2097168 | tf_op jit(solution)/shard_map/while/body/eval_jaxpr/reduce_scatter | solution.py:135
  2473.2 48.4 fusion.336
  2521.5 109.9 %reduce-scatter.19.cloned.1.call-done = bf16[256,16,128]{0,2,1:T(8,128)(2,1)} async-done(((bf16[2048,16,128]{0,2,1:T(8,128)(2,1)}), bf16[256,16,128]{0,2,1:T(8,128)(2,1)}) %reduce-scatter.19.cloned.1.call-update) | async-done | bytes 1048592 | tf_op jit(solution)/shard_map/while/body/eval_jaxpr/reduce_scatter | solution.py:214
  2631.5 170.3 %reduce-scatter.21.cloned.1.call-done = bf16[256,16,128]{0,2,1:T(8,128)(2,1)} async-done(((bf16[2048,16,128]{0,2,1:T(8,128)(2,1)}), bf16[256,16,128]{0,2,1:T(8,128)(2,1)}) %reduce-scatter.21.cloned.1.call-update) | async-done | bytes 1048592 | tf_op jit(solution)/shard_map/while/body/eval_jaxpr/reduce_scatter | solution.py:211
  2872.5 65.8 %all-gather.13.cloned.1.call-done = bf16[2048,16,128]{2,0,1:T(8,128)(2,1)} async-done(((bf16[256,16,128]{2,0,1:T(8,128)(2,1)}), bf16[2048,16,128]{2,0,1:T(8,128)(2,1)}) %all-gather.13.cloned.1.call-update) | async-done | bytes 8388624 | tf_op jit(solution)/shard_map/while/body/eval_jaxpr/all_gather | solution.py:102
  2957.1 64.1 all-gather.11.cloned.1.call-done
  3047.8 165.8 %all-gather.17.cloned.1.call-done = bf16[4096,2048]{1,0:T(8,128)(2,1)} async-done(((bf16[256,2048]{1,0:T(8,128)(2,1)}), bf16[4096,2048]{1,0:T(8,128)(2,1)}) %all-gather.17.cloned.1.call-update) | async-done | bytes 16777232 | tf_op jit(solution)/shard_map/while/body/eval_jaxpr/all_gather | solution.py:165
  3228.2 178.5 %all-gather.15.cloned.1.call-done = bf16[4096,2048]{1,0:T(8,128)(2,1)} async-done(((bf16[256,2048]{1,0:T(8,128)(2,1)}), bf16[4096,2048]{1,0:T(8,128)(2,1)}) %all-gather.15.cloned.1.call-update) | async-done | bytes 16777232 | tf_op jit(solution)/shard_map/while/body/eval_jaxpr/all_gather | solution.py:131
  3463.8 26.8 convolution_add_fusion.2
  3521.9 657.1 %reduce-scatter.17.cloned.1.call-done = f32[256,2048]{1,0:T(8,128)} async-done(((f32[4096,2048]{1,0:T(8,128)}), f32[256,2048]{1,0:T(8,128)}) %reduce-scatter.17.cloned.1.call-update) | async-done | bytes 2097168 | tf_op jit(solution)/shard_map/while/body/eval_jaxpr/reduce_scatter | solution.py:176
  4229.0 46.4 convert_bitcast_fusion.6
  4352.0 552.6 %reduce-scatter.23.cloned.1.call-done = f32[256,2048]{1,0:T(8,128)} async-done(((f32[4096,2048]{1,0:T(8,128)}), f32[256,2048]{1,0:T(8,128)}) %reduce-scatter.23.cloned.1.call-update) | async-done | bytes 2097168 | tf_op jit(solution)/shard_map/while/body/eval_jaxpr/reduce_scatter | solution.py:135
  4922.2 48.6 fusion.336
  4970.8 104.6 %reduce-scatter.19.cloned.1.call-done = bf16[256,16,128]{0,2,1:T(8,128)(2,1)} async-done(((bf16[2048,16,128]{0,2,1:T(8,128)(2,1)}), bf16[256,16,128]{0,2,1:T(8,128)(2,1)}) %reduce-scatter.19.cloned.1.call-update) | async-done | bytes 1048592 | tf_op jit(solution)/shard_map/while/body/eval_jaxpr/reduce_scatter | solution.py:214
  5075.4 170.1 %reduce-scatter.21.cloned.1.call-done = bf16[256,16,128]{0,2,1:T(8,128)(2,1)} async-done(((bf16[2048,16,128]{0,2,1:T(8,128)(2,1)}), bf16[256,16,128]{0,2,1:T(8,128)(2,1)}) %reduce-scatter.21.cloned.1.call-update) | async-done | bytes 1048592 | tf_op jit(solution)/shard_map/while/body/eval_jaxpr/reduce_scatter | solution.py:211
  5259.4 32.8 select_add_fusion.4
  5310.4 340.8 %reduce-scatter.13.cloned.1.call-done = f32[128,2048]{1,0:T(8,128)} async-done(((f32[2048,2048]{1,0:T(8,128)}), f32[128,2048]{1,0:T(8,128)}) %reduce-scatter.13.cloned.1.call-update) | async-done | bytes 1048592 | tf_op jit(solution)/shard_map/reduce_scatter | solution.py:40
  5653.2 702.7 %reduce-scatter.11.cloned.1.call-done = f32[384,2048]{1,0:T(8,128)} async-done(((f32[6144,2048]{1,0:T(8,128)}), f32[384,2048]{1,0:T(8,128)}) %reduce-scatter.11.cloned.1.call-update) | async-done | bytes 3145744 | tf_op jit(solution)/shard_map/reduce_scatter | solution.py:39
  6359.8 39.6 psum.38
  6437.8 40.5 all-reduce.6.cloned.1.call-done
  (446 shorter events, 746.9 us)
Async XLA Ops:
  7.2 116.3 %all-gather.9.cloned.1.call-start = ((), (), s32[]{:S(2)}) async-start(), calls=%async_computation.9 | async-start | bytes 8912896 | tf_op jit(solution)/shard_map/all_gather | solution.py:69
  7.9 387.9 %all-gather.7.cloned.1.call-start = ((), (), s32[]{:S(2)}) async-start(), calls=%async_computation.8 | async-start | bytes 26738688 | tf_op jit(solution)/shard_map/all_gather | solution.py:68
  395.8 98.6 %all-gather.13.cloned.1.call-start = ((), (), s32[]{:S(2)}) async-start(), calls=%async_computation.15 | async-start | bytes 9437184 | tf_op jit(solution)/shard_map/while/body/eval_jaxpr/all_gather | solution.py:102
  413.7 163.5 %all-gather.11.cloned.1.call-start = ((), (), s32[]{:S(2)}) async-start(), calls=%async_computation.14 | async-start | bytes 9437184 | tf_op jit(solution)/shard_map/while/body/eval_jaxpr/all_gather | solution.py:103
  415.6 354.0 %all-gather.17.cloned.1.call-start = ((), (), s32[]{:S(2)}) async-start(), calls=%async_computation.17 | async-start | bytes 17825792 | tf_op jit(solution)/shard_map/while/body/eval_jaxpr/all_gather | solution.py:165
  419.5 543.2 %all-gather.15.cloned.1.call-start = ((), (), s32[]{:S(2)}) async-start(), calls=%async_computation.16 | async-start | bytes 17825792 | tf_op jit(solution)/shard_map/while/body/eval_jaxpr/all_gather | solution.py:131
  603.8 1131.0 %reduce-scatter.17.cloned.1.call-start = ((), (), s32[]{:S(2)}) async-start(), calls=%async_computation.18 | async-start | bytes 35651584 | tf_op jit(solution)/shard_map/while/body/eval_jaxpr/reduce_scatter | solution.py:176
  1046.5 788.0 %reduce-scatter.25.cloned.1.call-start = ((), (), s32[]{:S(2)}) async-start(), calls=%async_computation.22 | async-start | bytes 589824 | tf_op jit(solution)/shard_map/while/body/eval_jaxpr/reduce_scatter | solution.py:154
  1059.6 1401.2 %reduce-scatter.23.cloned.1.call-start = ((), (), s32[]{:S(2)}) async-start(), calls=%async_computation.21 | async-start | bytes 35651584 | tf_op jit(solution)/shard_map/while/body/eval_jaxpr/reduce_scatter | solution.py:135
  1077.8 657.1 %copy-start.1 = (f32[256,2048]{1,0:T(8,128)S(1)}, f32[256,2048]{1,0:T(8,128)}, u32[]{:S(2)}) copy-start(f32[256,2048]{1,0:T(8,128)} %copy-done) | copy-start | bytes 6291460 | tf_op jit(solution)/shard_map/while
  1077.8 657.1 %copy-start.27 = (f32[2048]{0:T(1024)S(1)}, f32[2048]{0:T(1024)}, u32[]{:S(2)}) copy-start(f32[2048]{0:T(1024)} %copy-done.26) | copy-start | bytes 24580 | tf_op jit(solution)/shard_map/while
  1077.8 657.1 %copy-start.43 = (f32[256]{0:T(256)S(1)}, f32[256]{0:T(256)}, u32[]{:S(2)}) copy-start(f32[256]{0:T(256)} %copy-done.42) | copy-start | bytes 3076 | tf_op jit(solution)/shard_map/while
  1077.8 1553.7 %reduce-scatter.19.cloned.1.call-start = ((), (), s32[]{:S(2)}) async-start(), calls=%async_computation.19 | async-start | bytes 9437184 | tf_op jit(solution)/shard_map/while/body/eval_jaxpr/reduce_scatter | solution.py:214
  1767.4 1034.4 %reduce-scatter.21.cloned.1.call-start = ((), (), s32[]{:S(2)}) async-start(), calls=%async_computation.20 | async-start | bytes 9437184 | tf_op jit(solution)/shard_map/while/body/eval_jaxpr/reduce_scatter | solution.py:211
  2473.1 328.6 %copy-start.35 = (f32[2048]{0:T(1024)S(1)}, f32[2048]{0:T(1024)}, u32[]{:S(2)}) copy-start(f32[2048]{0:T(1024)} %copy-done.34) | copy-start | bytes 24580 | tf_op jit(solution)/shard_map/while
  2473.1 328.6 %copy-start.47 = (f32[256]{0:T(256)S(1)}, f32[256]{0:T(256)}, u32[]{:S(2)}) copy-start(f32[256]{0:T(256)} %copy-done.46) | copy-start | bytes 3076 | tf_op jit(solution)/shard_map/while
  2839.2 99.0 %all-gather.13.cloned.1.call-start = ((), (), s32[]{:S(2)}) async-start(), calls=%async_computation.15 | async-start | bytes 9437184 | tf_op jit(solution)/shard_map/while/body/eval_jaxpr/all_gather | solution.py:102
  2857.2 164.0 %all-gather.11.cloned.1.call-start = ((), (), s32[]{:S(2)}) async-start(), calls=%async_computation.14 | async-start | bytes 9437184 | tf_op jit(solution)/shard_map/while/body/eval_jaxpr/all_gather | solution.py:103
  2859.1 354.6 %all-gather.17.cloned.1.call-start = ((), (), s32[]{:S(2)}) async-start(), calls=%async_computation.17 | async-start | bytes 17825792 | tf_op jit(solution)/shard_map/while/body/eval_jaxpr/all_gather | solution.py:165
  2862.9 543.8 %all-gather.15.cloned.1.call-start = ((), (), s32[]{:S(2)}) async-start(), calls=%async_computation.16 | async-start | bytes 17825792 | tf_op jit(solution)/shard_map/while/body/eval_jaxpr/all_gather | solution.py:131
  3047.8 1131.1 %reduce-scatter.17.cloned.1.call-start = ((), (), s32[]{:S(2)}) async-start(), calls=%async_computation.18 | async-start | bytes 35651584 | tf_op jit(solution)/shard_map/while/body/eval_jaxpr/reduce_scatter | solution.py:176
  3490.6 787.8 %reduce-scatter.25.cloned.1.call-start = ((), (), s32[]{:S(2)}) async-start(), calls=%async_computation.22 | async-start | bytes 589824 | tf_op jit(solution)/shard_map/while/body/eval_jaxpr/reduce_scatter | solution.py:154
  3503.6 1401.0 %reduce-scatter.23.cloned.1.call-start = ((), (), s32[]{:S(2)}) async-start(), calls=%async_computation.21 | async-start | bytes 35651584 | tf_op jit(solution)/shard_map/while/body/eval_jaxpr/reduce_scatter | solution.py:135
  3521.8 657.1 %copy-start.1 = (f32[256,2048]{1,0:T(8,128)S(1)}, f32[256,2048]{1,0:T(8,128)}, u32[]{:S(2)}) copy-start(f32[256,2048]{1,0:T(8,128)} %copy-done) | copy-start | bytes 6291460 | tf_op jit(solution)/shard_map/while
  3521.8 657.1 %copy-start.27 = (f32[2048]{0:T(1024)S(1)}, f32[2048]{0:T(1024)}, u32[]{:S(2)}) copy-start(f32[2048]{0:T(1024)} %copy-done.26) | copy-start | bytes 24580 | tf_op jit(solution)/shard_map/while
  3521.8 657.1 %copy-start.43 = (f32[256]{0:T(256)S(1)}, f32[256]{0:T(256)}, u32[]{:S(2)}) copy-start(f32[256]{0:T(256)} %copy-done.42) | copy-start | bytes 3076 | tf_op jit(solution)/shard_map/while
  3521.8 1553.6 %reduce-scatter.19.cloned.1.call-start = ((), (), s32[]{:S(2)}) async-start(), calls=%async_computation.19 | async-start | bytes 9437184 | tf_op jit(solution)/shard_map/while/body/eval_jaxpr/reduce_scatter | solution.py:214
  4211.5 1034.1 %reduce-scatter.21.cloned.1.call-start = ((), (), s32[]{:S(2)}) async-start(), calls=%async_computation.20 | async-start | bytes 9437184 | tf_op jit(solution)/shard_map/while/body/eval_jaxpr/reduce_scatter | solution.py:211
  5299.0 352.1 %reduce-scatter.13.cloned.1.call-start = ((), (), s32[]{:S(2)}) async-start(), calls=%async_computation.11 | async-start | bytes 17825792 | tf_op jit(solution)/shard_map/reduce_scatter | solution.py:40
  5299.7 1056.2 %reduce-scatter.11.cloned.1.call-start = ((), (), s32[]{:S(2)}) async-start(), calls=%async_computation.10 | async-start | bytes 53477376 | tf_op jit(solution)/shard_map/reduce_scatter | solution.py:39
  5300.5 1122.1 %reduce-scatter.15.cloned.1.call-start = ((), (), s32[]{:S(2)}) async-start(), calls=%async_computation.12 | async-start | bytes 1114112
  5301.9 1176.4 %all-reduce.6.cloned.1.call-start = ((), (), s32[]{:S(2)}) async-start(), calls=%async_computation.13 | async-start | bytes 16777216 | tf_op jit(solution)/shard_map/psum | solution.py:274
  (114 other events, 3294.7 us)
Sparse Core Ops, SparseCore 0:
  10.8 112.6 all-gather.8
  126.3 269.4 all-gather.6
  413.8 80.4 all-gather.12
  496.4 80.7 all-gather.10
  579.8 189.8 all-gather.16
  772.8 189.7 all-gather.14
  1046.7 688.1 reduce-scatter.16
  1737.7 30.9 reduce-scatter.24
  1771.2 689.5 reduce-scatter.22
  2463.6 167.8 reduce-scatter.18
  2633.9 167.8 reduce-scatter.20
  2857.3 80.9 all-gather.12
  2940.4 80.7 all-gather.10
  3023.8 189.8 all-gather.16
  3216.9 189.7 all-gather.14
  3490.7 688.1 reduce-scatter.16
  4181.6 31.1 reduce-scatter.24
  4215.1 689.4 reduce-scatter.22
  4907.6 167.7 reduce-scatter.18
  5077.7 167.8 reduce-scatter.20
  5302.1 348.9 reduce-scatter.12
  5657.1 698.7 reduce-scatter.10
  6358.8 63.6 reduce-scatter.14
  6426.3 52.0 all-reduce.5
where the time goes:
time: 6500 us
  waiting for transfers between devices  5390 us (83%)
  matrix products  829 us (13%)
  blocking collectives  115 us (2%)
  other arithmetic  86.2 us (1%)
    reduce_scatter x2, waiting for transfers between devices, one_micro(): lax.psum_scatter(jnp.dot(grad_gates, gate_local, preferred_element_type=j...  1310 us
    reduce_scatter x2, waiting for transfers between devices, one_micro(): lax.psum_scatter(jnp.dot(hidden_kept, down_weight, preferred_element_type...  1110 us
    reduce_scatter x1, waiting for transfers between devices, spread_terms(): lax.psum_scatter(attn_terms[0], ('dp', 'seq'), scatter_dimension=0, tiled...  703 us
    all_gather x2, waiting for transfers between devices, one_micro(): rows_all = lax.all_gather(hidden_two, ('dp', 'seq'), axis=0, tiled=True)  357 us
    reduce_scatter x1, waiting for transfers between devices, spread_terms(): lax.psum_scatter(attn_terms[1], ('dp', 'seq'), scatter_dimension=0, tiled...  341 us
    reduce_scatter x2, waiting for transfers between devices, one_micro(): lax.psum_scatter(grad_keys_all.astype(jnp.bfloat16), ('rep', 'seq'), scat...  340 us
    all_gather x2, waiting for transfers between devices, one_micro(): grad_all = lax.all_gather(grad_mlp, ('dp', 'seq'), axis=0, tiled=True)  332 us
    all_gather x1, waiting for transfers between devices, shards(): lax.all_gather(qkv_weight, ('dp', 'seq'), axis=0, tiled=True)  272 us
  transfers between devices with their start and end apart: 24, of which 22 were waited for; matrix products, arithmetic and copies ran while one was open for 10% of the time, Pallas kernels for 0%

commit v1 on v0

v1 whole, which is shorter than its diff:
```python
import functools
import math

import jax
import jax.numpy as jnp
from jax import lax
from jax.experimental import pallas as pl
from jax.experimental.pallas import tpu as pltpu
from jax.sharding import PartitionSpec as P

EPSILON = 1e-05
LOG2E = 1.4426950408889634
NEG = -1e30
F32 = jnp.float32
BF16 = jnp.bfloat16
ALL = ("rep", "dp", "seq")


def nt(left_side, right_side):
    return lax.dot_general(
        left_side, right_side, (((1,), (1,)), ((), ())), preferred_element_type=F32
    )


def nn(left_side, right_side):
    return lax.dot_general(
        left_side, right_side, (((1,), (0,)), ((), ())), preferred_element_type=F32
    )


def tn(left_side, right_side):
    return lax.dot_general(
        left_side, right_side, (((0,), (0,)), ((), ())), preferred_element_type=F32
    )


def elu_one(values):
    return jnp.where(values > 0.0, values + 1.0, jnp.exp(jnp.minimum(values, 0.0)))


def project_kernel(rows_ref, gain_ref, weight_ref, hidden_ref, projected_ref):
    rows = rows_ref[...].astype(F32)
    scale = lax.rsqrt(jnp.mean(rows * rows, axis=-1, keepdims=True) + EPSILON)
    hidden = (rows * scale * gain_ref[...]).astype(BF16)
    hidden_ref[...] = hidden
    projected_ref[...] = nt(hidden, weight_ref[...]).astype(BF16)


def project(rows, gain, weight):
    count, width = rows.shape
    outs = weight.shape[0]
    block = min(256, count)
    return pl.pallas_call(
        project_kernel,
        grid=(count // block,),
        in_specs=[
            pl.BlockSpec((block, width), lambda i: (i, 0)),
            pl.BlockSpec((1, width), lambda i: (0, 0)),
            pl.BlockSpec((outs, width), lambda i: (0, 0)),
        ],
        out_specs=[
            pl.BlockSpec((block, width), lambda i: (i, 0)),
            pl.BlockSpec((block, outs), lambda i: (i, 0)),
        ],
        out_shape=[
            jax.ShapeDtypeStruct((count, width), BF16),
            jax.ShapeDtypeStruct((count, outs), BF16),
        ],
        compiler_params=pltpu.CompilerParams(vmem_limit_bytes=32 << 20),
        cost_estimate=pl.CostEstimate(
            flops=2 * count * width * outs,
            bytes_accessed=4 * count * width + 2 * outs * (width + count),
            transcendentals=count,
        ),
        name="project",
    )(rows, gain, weight)


def attend_kernel(
    block,
    length_ref,
    gate_ref,
    q_ref,
    k_ref,
    v_ref,
    mem_ref,
    norm_ref,
    mixed_ref,
    dot_ref,
    lse_ref,
    new_mem_ref,
    new_norm_ref,
    v_turned,
):
    head, step = pl.program_id(0), pl.program_id(1)
    length = length_ref[0]
    total, width = k_ref.shape
    memory = mem_ref[0]
    norm_row = norm_ref[0]
    memory_low = memory.astype(BF16)

    @pl.when(step == 0)
    def _():
        v_turned[...] = v_ref[...].T
        key_sig = elu_one(k_ref[...].astype(F32))
        below = jnp.sum(key_sig * norm_row, axis=-1, keepdims=True)
        recalled = nn(key_sig.astype(BF16), memory_low) / below
        change = v_ref[...].astype(F32) - recalled
        live = lax.broadcasted_iota(jnp.int32, (total, width), 0) < length
        kept = jnp.where(live, key_sig, 0.0)
        new_mem_ref[0] = memory + tn(kept.astype(BF16), change.astype(BF16))
        new_norm_ref[0] = norm_row + jnp.sum(kept, axis=0, keepdims=True)

    queries = q_ref[...]
    factor = LOG2E * width ** (-0.5)

    def visit(at, carry, masked):
        high, mass, acc = carry
        start = pl.multiple_of(at * block, block)
        scores = nt(k_ref[pl.ds(start, block), :], queries) * factor
        if masked:
            key_at = start + lax.broadcasted_iota(jnp.int32, (block, block), 0)
            query_at = step * block + lax.broadcasted_iota(jnp.int32, (block, block), 1)
            scores = jnp.where((key_at <= query_at) & (key_at < length), scores, NEG)
        higher = jnp.maximum(high, jnp.max(scores, axis=0, keepdims=True))
        weights = jnp.exp2(scores - higher)
        shrink = jnp.exp2(high - higher)
        mass = mass * shrink + jnp.sum(weights, axis=0, keepdims=True)
        acc = acc * shrink + nn(v_turned[:, pl.ds(start, block)], weights.astype(BF16))
        return higher, mass, acc

    full = jnp.minimum(step, length // block)
    end = jnp.minimum(step + 1, (length + block - 1) // block)
    carry = (
        jnp.full((1, block), NEG, F32),
        jnp.zeros((1, block), F32),
        jnp.zeros((width, block), F32),
    )
    carry = lax.fori_loop(0, full, functools.partial(visit, masked=False), carry)
    high, mass, acc = lax.fori_loop(full, end, functools.partial(visit, masked=True), carry)
    dot_read = (acc / mass).T
    query_sig = elu_one(queries.astype(F32))
    below = jnp.sum(query_sig * norm_row, axis=-1, keepdims=True)
    mem_read = nn(query_sig.astype(BF16), memory_low) / below
    gate = gate_ref[head]
    mixed_ref[...] = (gate * mem_read + (1.0 - gate) * dot_read).astype(BF16)
    dot_ref[...] = dot_read
    lse_ref[0] = high + jnp.log2(mass)


def attend(length, gate, projected, memory, normalizer):
    total = projected.shape[0]
    heads, width = normalizer.shape[0], normalizer.shape[2]
    block = min(512, total)
    smem = pl.BlockSpec(memory_space=pltpu.SMEM)
    return pl.pallas_call(
        functools.partial(attend_kernel, block),
        grid=(heads, total // block),
        in_specs=[
            smem,
            smem,
            pl.BlockSpec((block, width), lambda h, i: (i, h)),
            pl.BlockSpec((total, width), lambda h, i: (0, heads + h)),
            pl.BlockSpec((total, width), lambda h, i: (0, 2 * heads + h)),
            pl.BlockSpec((1, width, width), lambda h, i: (h, 0, 0)),
            pl.BlockSpec((1, 1, width), lambda h, i: (h, 0, 0)),
        ],
        out_specs=[
            pl.BlockSpec((block, width), lambda h, i: (i, h)),
            pl.BlockSpec((block, width), lambda h, i: (i, h)),
            pl.BlockSpec((1, 1, block), lambda h, i: (h, 0, i)),
            pl.BlockSpec((1, width, width), lambda h, i: (h, 0, 0)),
            pl.BlockSpec((1, 1, width), lambda h, i: (h, 0, 0)),
        ],
        out_shape=[
            jax.ShapeDtypeStruct((total, heads * width), BF16),
            jax.ShapeDtypeStruct((total, heads * width), F32),
            jax.ShapeDtypeStruct((heads, 1, total), F32),
            jax.ShapeDtypeStruct((heads, width, width), F32),
            jax.ShapeDtypeStruct((heads, 1, width), F32),
        ],
        scratch_shapes=[pltpu.VMEM((width, total), BF16)],
        compiler_params=pltpu.CompilerParams(vmem_limit_bytes=40 << 20),
        cost_estimate=pl.CostEstimate(
            flops=4 * heads * total * total * width,
            bytes_accessed=heads * total * width * 12,
            transcendentals=heads * total * total,
        ),
        name="attend",
    )(length, gate, projected, projected, projected, memory, normalizer)


def attend_back_kernel(
    block,
    length_ref,
    gate_ref,
    q_ref,
    k_ref,
    v_ref,
    mem_ref,
    norm_ref,
    dot_ref,
    lse_ref,
    grad_ref,
    out_ref,
    gate_sum_ref,
    k_turned,
    k_sum,
    v_sum,
):
    head, step = pl.program_id(0), pl.program_id(1)
    heads, steps = pl.num_programs(0), pl.num_programs(1)
    length = length_ref[0]
    total, width = k_ref.shape
    gate = gate_ref[head]

    @pl.when(step == 0)
    def _():
        k_turned[...] = k_ref[...].T
        k_sum[...] = jnp.zeros_like(k_sum)
        v_sum[...] = jnp.zeros_like(v_sum)
        gate_sum_ref[...] = jnp.zeros_like(gate_sum_ref)

    queries = q_ref[...]
    query_float = queries.astype(F32)
    grad_mixed = grad_ref[...].astype(F32)
    grad_dot = ((1.0 - gate) * grad_mixed).astype(BF16)
    dot_read = dot_ref[...]
    offset = jnp.sum((grad_dot.astype(F32) * dot_read).T, axis=0, keepdims=True)
    lse = lse_ref[0]
    scale = width ** (-0.5)
    factor = LOG2E * scale

    def visit(at, acc, masked):
        start = pl.multiple_of(at * block, block)
        here = pl.ds(start, block)
        scores = nt(k_ref[here, :], queries) * factor
        weights = jnp.exp2(scores - lse)
        if masked:
            key_at = start + lax.broadcasted_iota(jnp.int32, (block, block), 0)
            query_at = step * block + lax.broadcasted_iota(jnp.int32, (block, block), 1)
            weights = jnp.where((key_at <= query_at) & (key_at < length), weights, 0.0)
        grad_probs = nt(v_ref[here, :], grad_dot)
        grad_scores = (weights * (grad_probs - offset) * scale).astype(BF16)
        v_sum[here, :] += nn(weights.astype(BF16), grad_dot)
        k_sum[here, :] += nn(grad_scores, queries)
        return acc + nn(k_turned[:, here], grad_scores)

    full = jnp.minimum(step, length // block)
    end = jnp.minimum(step + 1, (length + block - 1) // block)
    acc = jnp.zeros((width, block), F32)
    acc = lax.fori_loop(0, full, functools.partial(visit, masked=False), acc)
    acc = lax.fori_loop(full, end, functools.partial(visit, masked=True), acc)

    memory_low = mem_ref[0].astype(BF16)
    norm_row = norm_ref[0]
    query_sig = elu_one(query_float)
    below = jnp.sum(query_sig * norm_row, axis=-1, keepdims=True)
    numerator = nn(query_sig.astype(BF16), memory_low)
    inverse = 1.0 / below
    grad_read = gate * grad_mixed
    grad_below = -jnp.sum(grad_read * numerator, axis=-1, keepdims=True) * inverse * inverse
    grad_sig = nt((grad_read * inverse).astype(BF16), memory_low) + grad_below * norm_row
    slope = jnp.where(query_float > 0.0, 1.0, jnp.exp(jnp.minimum(query_float, 0.0)))
    rows = pl.ds(pl.multiple_of(step * block, block), block)
    out_ref[rows, pl.ds(pl.multiple_of(head * width, width), width)] = (
        acc.T + grad_sig * slope
    ).astype(BF16)
    gate_sum_ref[0] += jnp.sum(
        grad_mixed * (numerator * inverse - dot_read), axis=0, keepdims=True
    )

    @pl.when(step == steps - 1)
    def _():
        k_at = pl.multiple_of((heads + head) * width, width)
        v_at = pl.multiple_of((2 * heads + head) * width, width)
        out_ref[:, pl.ds(k_at, width)] = k_sum[...].astype(BF16)
        out_ref[:, pl.ds(v_at, width)] = v_sum[...].astype(BF16)


def attend_back(length, gate, projected, memory, normalizer, dot_read, lse, grad_mixed):
    total = projected.shape[0]
    heads, width = normalizer.shape[0], normalizer.shape[2]
    block = min(512, total)
    smem = pl.BlockSpec(memory_space=pltpu.SMEM)
    return pl.pallas_call(
        functools.partial(attend_back_kernel, block),
        grid=(heads, total // block),
        in_specs=[
            smem,
            smem,
            pl.BlockSpec((block, width), lambda h, i: (i, h)),
            pl.BlockSpec((total, width), lambda h, i: (0, heads + h)),
            pl.BlockSpec((total, width), lambda h, i: (0, 2 * heads + h)),
            pl.BlockSpec((1, width, width), lambda h, i: (h, 0, 0)),
            pl.BlockSpec((1, 1, width), lambda h, i: (h, 0, 0)),
            pl.BlockSpec((block, width), lambda h, i: (i, h)),
            pl.BlockSpec((1, 1, block), lambda h, i: (h, 0, i)),
            pl.BlockSpec((block, width), lambda h, i: (i, h)),
        ],
        out_specs=[
            pl.BlockSpec((total, 3 * heads * width), lambda h, i: (0, 0)),
            pl.BlockSpec((1, 1, width), lambda h, i: (h, 0, 0)),
        ],
        out_shape=[
            jax.ShapeDtypeStruct((total, 3 * heads * width), BF16),
            jax.ShapeDtypeStruct((heads, 1, width), F32),
        ],
        scratch_shapes=[
            pltpu.VMEM((width, total), BF16),
            pltpu.VMEM((total, width), F32),
            pltpu.VMEM((total, width), F32),
        ],
        compiler_params=pltpu.CompilerParams(vmem_limit_bytes=40 << 20),
        cost_estimate=pl.CostEstimate(
            flops=10 * heads * total * total * width,
            bytes_accessed=heads * total * width * 20,
            transcendentals=heads * total * total,
        ),
        name="attend_back",
    )(length, gate, projected, projected, projected, memory, normalizer, dot_read, lse, grad_mixed)


def mlp_kernel(
    tiles,
    rows_ref,
    grad_ref,
    inner_a,
    inner_b,
    down_a,
    down_b,
    out_ref,
    grad_two_ref,
    hidden_ref,
    grad_gate_ref,
    grad_up_ref,
    out_acc,
    grad_acc,
):
    step = pl.program_id(0)
    width = rows_ref.shape[1]

    @pl.when(step == 0)
    def _():
        out_acc[...] = jnp.zeros_like(out_acc)
        grad_acc[...] = jnp.zeros_like(grad_acc)

    def visit(inner_ref, down_ref):
        gate_weight = inner_ref[:, :width]
        up_weight = inner_ref[:, width:]
        down = down_ref[...]
        rows = rows_ref[...]
        gates = nt(rows, gate_weight)
        ups = nt(rows, up_weight)
        sigmoid = 1.0 / (1.0 + jnp.exp(-gates))
        silu = gates * sigmoid
        hidden = (silu * ups).astype(BF16)
        hidden_ref[...] = hidden
        out_acc[...] += nn(hidden, down)
        grad_hidden = nt(grad_ref[...], down)
        grad_gates = (grad_hidden * ups * (sigmoid * (1.0 + gates * (1.0 - sigmoid)))).astype(BF16)
        grad_ups = (grad_hidden * silu).astype(BF16)
        grad_gate_ref[...] = grad_gates
        grad_up_ref[...] = grad_ups
        grad_acc[...] += nn(grad_gates, gate_weight) + nn(grad_ups, up_weight)

    @pl.when(step < tiles)
    def _():
        visit(inner_a, down_a)

    @pl.when(step >= tiles)
    def _():
        visit(inner_b, down_b)

    @pl.when(step == 2 * tiles - 1)
    def _():
        out_ref[...] = out_acc[...].astype(BF16)
        grad_two_ref[...] = grad_acc[...].astype(BF16)


def mlp(rows, grads, inner_a, inner_b, down_a, down_b):
    count, width = rows.shape
    units = inner_a.shape[0]
    tile = min(256, units)
    tiles = units // tile
    first = lambda t: (jnp.minimum(t, tiles - 1), 0)
    second = lambda t: (jnp.maximum(t - tiles, 0), 0)
    whole = lambda t: (0, 0)
    once = pl.Buffered(1)
    column = pl.BlockSpec((count, tile), lambda t: (0, t))
    unit_shape = jax.ShapeDtypeStruct((count, 2 * units), BF16)
    row_shape = jax.ShapeDtypeStruct((count, width), BF16)
    return pl.pallas_call(
        functools.partial(mlp_kernel, tiles),
        grid=(2 * tiles,),
        in_specs=[
            pl.BlockSpec((count, width), whole, pipeline_mode=once),
            pl.BlockSpec((count, width), whole, pipeline_mode=once),
            pl.BlockSpec((tile, 2 * width), first),
            pl.BlockSpec((tile, 2 * width), second),
            pl.BlockSpec((tile, width), first),
            pl.BlockSpec((tile, width), second),
        ],
        out_specs=[
            pl.BlockSpec((count, width), whole, pipeline_mode=once),
            pl.BlockSpec((count, width), whole, pipeline_mode=once),
            column,
            column,
            column,
        ],
        out_shape=[row_shape, row_shape, unit_shape, unit_shape, unit_shape],
        scratch_shapes=[pltpu.VMEM((count, width), F32), pltpu.VMEM((count, width), F32)],
        compiler_params=pltpu.CompilerParams(vmem_limit_bytes=60 << 20),
        cost_estimate=pl.CostEstimate(
            flops=2 * 6 * count * width * 2 * units,
            bytes_accessed=2 * units * (6 * width + 6 * count) + 8 * count * width,
            transcendentals=count * 2 * units,
        ),
        name="feed_forward",
    )(rows, grads, inner_a, inner_b, down_a, down_b)


def swap(values):
    return lax.ppermute(values, "rep", [(0, 1), (1, 0)])


def add_low(left_side, right_side):
    return (left_side.astype(F32) + right_side.astype(F32)).astype(BF16)


def line_gather(values, axis):
    count = lax.axis_size(axis)
    here = lax.axis_index(axis)
    rows = values.shape[0]
    table = jnp.zeros(((3 * count - 2) * rows,) + values.shape[1:], values.dtype)

    def put(table, piece, origin):
        return lax.dynamic_update_slice_in_dim(table, piece, (origin + count - 1) * rows, 0)

    table = put(table, values, here)
    rising = falling = values
    for hop in range(1, count):
        rising = lax.ppermute(
            rising, axis, [(a, a + 1) for a in range(count - 1) if a >= hop - 1]
        )
        falling = lax.ppermute(
            falling, axis, [(a, a - 1) for a in range(1, count) if a + hop - 1 < count]
        )
        table = put(table, rising, here - hop)
        table = put(table, falling, here + hop)
    return table[(count - 1) * rows : (2 * count - 1) * rows]


def line_scatter(values, axis):
    count = lax.axis_size(axis)
    here = lax.axis_index(axis)
    rows = values.shape[0] // count

    def block(owner):
        start = jnp.clip(owner, 0, count - 1) * rows
        return lax.dynamic_slice_in_dim(values, start, rows, 0).astype(F32)

    rising = falling = None
    for hop in range(1, count):
        reach = count - hop
        up, down = block(here + reach), block(here - reach)
        if rising is not None:
            up, down = up + rising.astype(F32), down + falling.astype(F32)
        rising = lax.ppermute(
            up.astype(BF16), axis, [(a, a + 1) for a in range(count) if a + reach < count]
        )
        falling = lax.ppermute(
            down.astype(BF16), axis, [(a, a - 1) for a in range(count) if a - reach >= 0]
        )
    return block(here) + rising.astype(F32) + falling.astype(F32)


def cube_bits(count):
    bits = [1 << b for b in range(count.bit_length() - 1)]
    return bits, bits[::-1]


def cube_order(bits):
    order = [0]
    for bit in reversed(bits):
        order = order + [k | bit for k in order]
    return order


def cube_gather(values, axis):
    count = lax.axis_size(axis)
    half = values.shape[0] // 2
    parts = []
    for bits, start in zip(cube_bits(count), (0, half)):
        held = {0: values[start : start + half]}
        for bit in bits:
            pairs = [(a, a ^ bit) for a in range(count)]
            held.update({k ^ bit: lax.ppermute(v, axis, pairs) for k, v in list(held.items())})
        parts += [held[k] for k in cube_order(bits)]
    return jnp.concatenate(parts, axis=0)


def cube_scatter(values, axis):
    count = lax.axis_size(axis)
    half = values.shape[0] // 2
    parts = []
    for bits, start in zip(cube_bits(count), (0, half)):
        held = values[start : start + half]
        for bit in bits:
            pairs = [(a, a ^ bit) for a in range(count)]
            keep = held.shape[0] // 2
            got = lax.ppermute(held[keep:].astype(BF16), axis, pairs)
            held = held[:keep].astype(F32) + got.astype(F32)
        parts.append(held)
    return jnp.concatenate(parts, axis=0)


def heads_plan(shard_rows, block_rows, dp_count, seq_count, span_count):
    unit = math.gcd(shard_rows, block_rows)
    per_shard, per_block = shard_rows // unit, block_rows // unit
    per_column = 3 * span_count // dp_count
    edges = []
    for u in range(dp_count * seq_count * per_shard):
        shard, block = u // per_shard, u // per_block
        column, source = divmod(shard, seq_count)
        core, target = divmod(block % span_count, seq_count)
        edges.append((core, column, source, target, u % per_shard, u % per_block))
    rounds = []
    for edge in edges:
        core, column, source, target = edge[:4]
        for group in rounds:
            if all(
                (core, column) != e[:2] or (source != e[2] and target != e[3]) for e in group
            ):
                group.append(edge)
                break
        else:
            rounds.append([edge])
    return unit, per_shard, per_block, per_column, rounds


def device_number(core, column, place, dp_count, seq_count):
    return (core * dp_count + column) * seq_count + place


def pick(table, number):
    return jnp.asarray(table, jnp.int32)[number]


def shards(
    tokens,
    lengths,
    memory,
    normalizer,
    qkv_weight,
    out_weight,
    norm_gains,
    gate_logit,
    inner_weight,
    down_weight,
    cotangent,
):
    micros, _, span_rows, width = tokens.shape
    head_count = gate_logit.shape[0]
    head_dim = width // head_count
    dp_count, seq_count = lax.axis_size("dp"), lax.axis_size("seq")
    span_count = 2 * seq_count
    total = span_rows * span_count
    half_total = total // 2
    heads_here = head_count // span_count
    block_rows = heads_here * head_dim
    core, column, place = lax.axis_index("rep"), lax.axis_index("dp"), lax.axis_index("seq")
    span = core * seq_count + place
    number = device_number(core, column, place, dp_count, seq_count)
    inner_half = inner_weight.shape[0] // 2

    own_rows = [tokens[m, 0] for m in range(micros)]
    near = [line_gather(rows, "seq") for rows in own_rows]
    far = [swap(rows) for rows in near]

    unit, per_shard, per_block, per_column, rounds = heads_plan(
        qkv_weight.shape[0], block_rows, dp_count, seq_count, span_count
    )
    landed = jnp.zeros(((per_block + 1) * unit, width), BF16)
    devices = 2 * dp_count * seq_count
    for group in rounds:
        send, slot, pairs = [0] * devices, [per_block] * devices, []
        for c, col, source, target, from_unit, to_unit in group:
            a = device_number(c, col, source, dp_count, seq_count)
            b = device_number(c, col, target, dp_count, seq_count)
            send[a], slot[b] = from_unit, to_unit
            pairs.append((a, b))
        piece = lax.dynamic_slice_in_dim(qkv_weight, pick(send, number) * unit, unit, 0)
        piece = lax.ppermute(piece, ALL, pairs)
        landed = lax.dynamic_update_slice_in_dim(landed, piece, pick(slot, number) * unit, 0)
    forward_bits = cube_bits(dp_count)
    blocks = cube_gather(landed[:block_rows], "dp")
    half_block = block_rows // 2
    orders = [cube_order(bits) for bits in forward_bits]
    spots = [[order.index(k) for k in range(dp_count)] for order in orders]
    head_weights = []
    for part in range(3):
        distance = ((part * span_count + span) // per_column) ^ column
        for side in range(2):
            spot = pick(spots[side], distance) + side * dp_count
            head_weights.append(
                lax.dynamic_slice_in_dim(blocks, spot * half_block, half_block, 0)
            )
    head_weight = jnp.concatenate(head_weights, axis=0)

    gains_all = lax.all_gather(norm_gains, ("dp", "seq"), axis=1, tiled=True).astype(F32)
    gain_one, gain_two = gains_all[0:1], gains_all[1:2]
    half_width = width // 2
    out_near = lax.all_gather(
        lax.dynamic_slice_in_dim(out_weight, core * half_width, half_width, 1),
        ("dp", "seq"),
        axis=0,
        tiled=True,
    )
    inner_near = lax.all_gather(
        lax.dynamic_slice_in_dim(inner_weight, core * inner_half, inner_half, 0),
        "seq",
        axis=0,
        tiled=True,
    )
    down_near = lax.all_gather(
        lax.dynamic_slice_in_dim(down_weight, core * inner_half, inner_half, 0),
        "seq",
        axis=0,
        tiled=True,
    )
    out_far, inner_far, down_far = swap(out_near), swap(inner_near), swap(down_near)

    positions = span * span_rows + jnp.arange(span_rows)
    gate_share = jax.nn.sigmoid(gate_logit)
    gate_here = lax.dynamic_slice_in_dim(gate_share, span * heads_here, heads_here, 0)
    near_at, far_at = core * half_width, (1 - core) * half_width

    live_cots, grad_lows, grad_rows = [], [], []
    for m in range(micros):
        live_rows = (positions < lengths[m, 0]).astype(F32)
        live = cotangent[m, 0].astype(F32) * live_rows[:, None]
        live_cots.append(live)
        grad_lows.append(live.astype(BF16))
        grad_rows.append(cube_gather(grad_lows[m], "dp"))

    saved = []
    outputs, new_memories, new_norms = [], [], []
    for m in range(micros):
        hidden_near, projected_near = project(near[m], gain_one, head_weight)
        hidden_far, projected_far = project(far[m], gain_one, head_weight)
        low_first = core == 0
        projected = jnp.concatenate(
            [
                jnp.where(low_first, projected_near, projected_far),
                jnp.where(low_first, projected_far, projected_near),
            ],
            axis=0,
        )
        memory_here = lax.dynamic_slice_in_dim(memory[m, 0], span * heads_here, heads_here, 0)
        norm_here = lax.dynamic_slice_in_dim(
            normalizer[m, 0], span * heads_here, heads_here, 0
        ).reshape(heads_here, 1, head_dim)
        length = lengths[m]
        mixed_heads, dot_read, lse, new_memory, new_norm = attend(
            length, gate_here, projected, memory_here, norm_here
        )
        new_memories.append(new_memory)
        new_norms.append(new_norm.reshape(heads_here, head_dim))
        mixed = lax.all_to_all(
            mixed_heads.reshape(span_count, span_rows, block_rows),
            ("rep", "seq"),
            0,
            0,
            tiled=True,
        )
        mixed = jnp.swapaxes(mixed, 0, 1).reshape(span_rows, width)
        mixed_near = lax.dynamic_slice_in_dim(mixed, near_at, half_width, 1)
        mixed_far = lax.dynamic_slice_in_dim(mixed, far_at, half_width, 1)
        after_attn = (
            own_rows[m].astype(F32) + nt(mixed_near, out_near) + nt(mixed_far, out_far)
        )
        scale_two = lax.rsqrt(jnp.mean(after_attn * after_attn, axis=-1, keepdims=True) + EPSILON)
        normed_two = after_attn * scale_two
        hidden_two = (normed_two * gain_two).astype(BF16)
        rows_all = cube_gather(hidden_two, "dp")
        mlp_part, grad_two_part, hidden, grad_gates, grad_ups = mlp(
            rows_all, grad_rows[m], inner_near, inner_far, down_near, down_far
        )
        grad_two = cube_scatter(grad_two_part, "dp")
        mlp_out = cube_scatter(mlp_part, "dp")
        outputs.append((after_attn + mlp_out).astype(BF16))
        grad_scaled = grad_two * gain_two
        grad_after = live_cots[m] + scale_two * (
            grad_scaled
            - normed_two * jnp.mean(grad_scaled * normed_two, axis=-1, keepdims=True)
        )
        grad_branch = grad_after.astype(BF16)
        grad_mixed_near = nn(grad_branch, out_near).astype(BF16)
        grad_mixed_far = nn(grad_branch, out_far).astype(BF16)
        grad_mixed = jnp.concatenate(
            [
                jnp.where(low_first, grad_mixed_near, grad_mixed_far),
                jnp.where(low_first, grad_mixed_far, grad_mixed_near),
            ],
            axis=1,
        )
        grad_heads = lax.all_to_all(
            jnp.swapaxes(grad_mixed.reshape(span_rows, span_count, block_rows), 0, 1),
            ("rep", "seq"),
            0,
            0,
            tiled=True,
        ).reshape(total, block_rows)
        grad_projected, gate_sums = attend_back(
            length, gate_here, projected, memory_here, norm_here, dot_read, lse, grad_heads
        )
        grad_near = lax.dynamic_slice_in_dim(grad_projected, core * half_total, half_total, 0)
        grad_far = lax.dynamic_slice_in_dim(
            grad_projected, (1 - core) * half_total, half_total, 0
        )
        grad_one_far = swap(nn(grad_far, head_weight).astype(BF16))
        grad_one_near = (nn(grad_near, head_weight) + grad_one_far.astype(F32)).astype(BF16)
        grad_one = line_scatter(grad_one_near, "seq")
        rows_float = own_rows[m].astype(F32)
        scale_one = lax.rsqrt(jnp.mean(rows_float * rows_float, axis=-1, keepdims=True) + EPSILON)
        normed_one = rows_float * scale_one
        grad_scaled_one = grad_one * gain_one
        grad_tokens = (
            grad_after
            + scale_one
            * (
                grad_scaled_one
                - normed_one * jnp.mean(grad_scaled_one * normed_one, axis=-1, keepdims=True)
            )
        ).astype(BF16)
        saved.append(
            dict(
                grad_tokens=grad_tokens,
                gains_one=jnp.sum(grad_one * normed_one, axis=0),
                gains_two=jnp.sum(grad_two * normed_two, axis=0),
                gate=jnp.sum(gate_sums, axis=(1, 2)),
                qkv=tn(grad_near, hidden_near) + tn(grad_far, hidden_far),
                out_near=tn(grad_branch, mixed_near),
                out_far=tn(grad_branch, mixed_far),
                rows=rows_all,
                grads=grad_rows[m],
                hidden=hidden,
                grad_gates=grad_gates,
                grad_ups=grad_ups,
            )
        )

    def joined(name):
        return functools.reduce(jnp.add, [s[name] for s in saved])

    units = inner_near.shape[0]

    def unit_grads(left, right):
        def part(start):
            return functools.reduce(
                jnp.add, [tn(s[left][:, start : start + units], s[right]) for s in saved]
            )

        far_part = swap(part(units).astype(BF16))
        near_part = (part(0) + far_part.astype(F32)).astype(BF16)
        mine = line_scatter(near_part, "seq").astype(BF16)
        other = swap(mine)
        return jnp.concatenate(
            [jnp.where(core == 0, mine, other), jnp.where(core == 0, other, mine)], axis=0
        ).astype(F32)

    grad_down = unit_grads("hidden", "grads")
    grad_inner = jnp.concatenate(
        [unit_grads("grad_gates", "rows"), unit_grads("grad_ups", "rows")], axis=1
    )

    out_other = swap(joined("out_far").astype(BF16))
    out_mine = (joined("out_near") + out_other.astype(F32)).astype(BF16)
    shard_out = out_weight.shape[0]
    out_mine = out_mine.reshape(dp_count, seq_count * shard_out, half_width)
    pieces = []
    side_rows = seq_count * shard_out // 2
    for side in range(2):
        for k in orders[side]:
            owned = lax.dynamic_index_in_dim(out_mine, column ^ k, 0, keepdims=False)
            pieces.append(owned[side * side_rows : (side + 1) * side_rows])
    out_column = cube_scatter(jnp.concatenate(pieces, axis=0), "dp").astype(BF16)
    out_mine = line_scatter(out_column, "seq").astype(BF16)
    out_other = swap(out_mine)
    grad_out = jnp.concatenate(
        [jnp.where(core == 0, out_mine, out_other), jnp.where(core == 0, out_other, out_mine)],
        axis=1,
    ).astype(F32)

    qkv_low = joined("qkv").astype(BF16).reshape(3, block_rows, width)
    qkv_low = jnp.concatenate([qkv_low, jnp.zeros((1, block_rows, width), BF16)], axis=0)
    which = [
        [3] * (span_count * dp_count) for _ in range(1)
    ][0]
    for part in range(3):
        for owner in range(span_count):
            col = (part * span_count + owner) // per_column
            which[owner * dp_count + col] = part
    pieces = []
    for side in range(2):
        for k in orders[side]:
            part = pick(which, span * dp_count + (column ^ k))
            block = lax.dynamic_index_in_dim(qkv_low, part, 0, keepdims=False)
            pieces.append(block[side * half_block : (side + 1) * half_block])
    qkv_block = cube_scatter(jnp.concatenate(pieces, axis=0), "dp").astype(BF16)
    returned = jnp.zeros(((per_shard + 1) * unit, width), BF16)
    for group in rounds:
        send, slot, pairs = [0] * devices, [per_shard] * devices, []
        for c, col, source, target, from_unit, to_unit in group:
            a = device_number(c, col, target, dp_count, seq_count)
            b = device_number(c, col, source, dp_count, seq_count)
            send[a], slot[b] = to_unit, from_unit
            pairs.append((a, b))
        piece = lax.dynamic_slice_in_dim(qkv_block, pick(send, number) * unit, unit, 0)
        piece = lax.ppermute(piece, ALL, pairs)
        returned = lax.dynamic_update_slice_in_dim(returned, piece, pick(slot, number) * unit, 0)
    returned = returned[: per_shard * unit]
    grad_qkv = returned.astype(F32) + swap(returned).astype(F32)

    gate_terms = joined("gate") * gate_here * (1.0 - gate_here)
    gate_row = lax.dynamic_update_slice_in_dim(
        jnp.zeros((head_count,), F32), gate_terms, span * heads_here, 0
    )
    small = jnp.concatenate([joined("gains_one"), joined("gains_two"), gate_row])
    small = jnp.sum(lax.all_gather(small, ALL, axis=0), axis=0)
    shard_gain = norm_gains.shape[1]
    gain_at = (column * seq_count + place) * shard_gain
    grad_gains = lax.dynamic_slice_in_dim(
        small[: 2 * width].reshape(2, width), gain_at, shard_gain, 1
    )
    grad_gate = small[2 * width :]
    return (
        jnp.stack(outputs)[:, None],
        jnp.stack(new_memories)[:, None],
        jnp.stack(new_norms)[:, None],
        jnp.stack([s["grad_tokens"] for s in saved])[:, None],
        grad_qkv,
        grad_out,
        grad_gains,
        grad_gate,
        grad_inner,
        grad_down,
    )


def solution(mesh):
    placed = (
        P(None, "dp", ("rep", "seq"), None),
        P(None, "dp"),
        P(None, "dp", None, None, None),
        P(None, "dp", None, None),
        P(("dp", "seq"), None),
        P(("dp", "seq"), None),
        P(None, ("dp", "seq")),
        P(),
        P(("dp", "seq"), None),
        P(("dp", "seq"), None),
        P(None, "dp", ("rep", "seq"), None),
    )
    return jax.shard_map(
        shards,
        mesh=mesh,
        in_specs=placed,
        out_specs=(
            P(None, "dp", ("rep", "seq"), None),
            P(None, "dp", ("rep", "seq"), None, None),
            P(None, "dp", ("rep", "seq"), None),
            P(None, "dp", ("rep", "seq"), None),
            P(("dp", "seq"), None),
            P(("dp", "seq"), None),
            P(None, ("dp", "seq")),
            P(),
            P(("dp", "seq"), None),
            P(("dp", "seq"), None),
        ),
        check_vma=False,
    )
```

time: 6500 us -> 1960 us (0.30)
  waiting for transfers between devices: 5390 us -> 835 us
  matrix products: 829 us -> 185 us
  Pallas kernels: 0 us -> 307 us
  starting transfers between devices: 1.62 us -> 266 us
  local copies, waits for them, and re-layouts: 56.9 us -> 133 us
  blocking collectives: 115 us -> 46.9 us
    reduce_scatter x12 -> x0, waiting for transfers between devices: 4020 us -> none  [the longest x2 1310 us: one_micro(): lax.psum_scatter(jnp.dot(grad_gates, gate_local, preferred_element_type=j...]
    all_gather x10 -> x3, waiting for transfers between devices: 1300 us -> 0.01 us  [the longest x1 0.01 us: shards(): lax.all_gather(lax.dynamic_slice_in_dim(out_weight, core * half_width, ha...]
    ppermute x0 -> x124, waiting for transfers between devices: none -> 698 us  [the longest x6 217 us: line_gather(): lax.ppermute(rising, axis, [(a, a + 1) for a in range(count - 1) if a >=...]
    dot_general x52 -> x32, matrix products: 791 us -> 185 us  [the longest x20 137 us: tn(): lax.dot_general(left_side, right_side, (((0,), (0,)), ((), ())), preferre...]
    pallas_call x0 -> x10, Pallas kernels: none -> 307 us  [the longest x2 200 us: mlp(): pl.pallas_call(functools.partial(mlp_kernel, tiles), grid=(2 * tiles,), i...]
    ppermute x0 -> x124, starting transfers between devices: none -> 240 us  [the longest x18 48.2 us: line_scatter(): lax.ppermute(down.astype(BF16), axis, [(a, a - 1) for a in range(count) i...]
    unnamed x7 -> x5, waiting for transfers between devices: 25.9 us -> 121 us
  transfers between devices with their start and end apart: 24 -> 132, of which waited for: 22 -> 54; matrix products, arithmetic and copies ran while one was open for 10% -> 19% of each run, Pallas kernels for 0% -> 6%
where the time goes in v1:
time: 1960 us; the launch traced here: 1940 us
  waiting for transfers between devices  835 us (43%)
  Pallas kernels  307 us (16%)
  starting transfers between devices  266 us (14%)
  matrix products  185 us (9%)
  other arithmetic  135 us (7%)
  local copies, waits for them, and re-layouts  133 us (7%)
  blocking collectives  46.9 us (2%)
  between operations  34.4 us (2%)
    ppermute x6, waiting for transfers between devices, line_gather(): lax.ppermute(rising, axis, [(a, a + 1) for a in range(count - 1) if a >=...  217 us
    pallas_call x2, Pallas kernels, mlp(): pl.pallas_call(functools.partial(mlp_kernel, tiles), grid=(2 * tiles,), i...  200 us
    dot_general x20, matrix products, tn(): lax.dot_general(left_side, right_side, (((0,), (0,)), ((), ())), preferre...  137 us
    ppermute x18, waiting for transfers between devices, line_scatter(): lax.ppermute(up.astype(BF16), axis, [(a, a + 1) for a in range(count) if...  131 us
    unnamed x5, waiting for transfers between devices  121 us
    ppermute x18, waiting for transfers between devices, line_scatter(): lax.ppermute(down.astype(BF16), axis, [(a, a - 1) for a in range(count) i...  116 us
    ppermute x30, waiting for transfers between devices, cube_gather(): lax.ppermute(v, axis, pairs)  101 us
    ppermute x24, waiting for transfers between devices, cube_scatter(): got = lax.ppermute(held[keep:].astype(BF16), axis, pairs)  95.9 us
  transfers between devices with their start and end apart: 132, of which 54 were waited for; matrix products, arithmetic and copies ran while one was open for 19% of the time, Pallas kernels for 6%

profile of v1, /device:TPU:17, one launch (start us, length us, event | category | flops | bytes accessed | tf_op | source)
XLA Modules:
  0.0 1942.5 jit_solution(3657004819642583267)
XLA Ops:
  42.1 46.9 %all_gather.18 = bf16[2,2048]{1,0:T(2,128)(2,1)S(1)} all-gather(bf16[2,128]{1,0:T(2,128)(2,1)S(1)} %copy-done.105), channel_id=1, replica_groups=mesh['rep'=2,'dp'=4,'seq'=4] {'dp','seq'}, dimensions={1}, use_global_device_ids=true | all-gather | bytes 8704 | tf_op jit(solution)/shard_map/all_gather | solution.py:611
  161.8 41.0 %collective-permute-done = bf16[256,2048]{1,0:T(8,128)(2,1)S(1)} collective-permute-done((bf16[256,2048]{1,0:T(8,128)(2,1)S(1)}, bf16[256,2048]{1,0:T(8,128)(2,1)S(1)}, u32[]{:S(2)}, u32[]{:S(2)}) %collective-permute-start) | collective-permute-done | bytes 1048608 | tf_op jit(solution)/shard_map/ppermute | solution.py:443
  202.7 16.4 collective-permute-start.2
  221.5 46.7 %collective-permute-done.35 = bf16[256,2048]{1,0:T(8,128)(2,1)S(1)} collective-permute-done((bf16[256,2048]{1,0:T(8,128)(2,1)S(1)}, bf16[256,2048]{1,0:T(8,128)(2,1)S(1)}, u32[]{:S(2)}, u32[]{:S(2)}) %collective-permute-start.35) | collective-permute-done | bytes 1048608 | tf_op jit(solution)/shard_map/ppermute | solution.py:443
  268.2 17.1 collective-permute-start.37
  300.9 13.8 collective-permute-done.2
  318.5 65.3 %collective-permute-done.37 = bf16[256,2048]{1,0:T(8,128)(2,1)S(1)} collective-permute-done((bf16[256,2048]{1,0:T(8,128)(2,1)S(1)}, bf16[256,2048]{1,0:T(8,128)(2,1)S(1)}, u32[]{:S(2)}, u32[]{:S(2)}) %collective-permute-start.37) | collective-permute-done | bytes 1048608 | tf_op jit(solution)/shard_map/ppermute | solution.py:443
  389.8 36.0 %collective-permute-done.4 = bf16[256,2048]{1,0:T(8,128)(2,1)S(1)} collective-permute-done((bf16[256,2048]{1,0:T(8,128)(2,1)S(1)}, bf16[256,2048]{1,0:T(8,128)(2,1)S(1)}, u32[]{:S(2)}, u32[]{:S(2)}) %collective-permute-start.4) | collective-permute-done | bytes 1048608 | tf_op jit(solution)/shard_map/ppermute | solution.py:443
  434.2 14.1 collective-permute-done.39
  465.5 14.5 collective-permute-done.12
  536.2 17.0 attend.2
  572.4 19.8 %attend.3 = (bf16[2048,256]{1,0:T(8,128)(2,1)S(1)}, f32[2048,256]{1,0:T(8,128)S(1)}, f32[2,1,2048]{2,1,0:T(1,128)S(1)}, f32[2,128,128]{2,1,0:T(8,128)S(1)}, f32[2,1,128]{2,1,0:T(1,128)S(1)}) custom-call(s32[1]{0:T(128)} %bitcast.22.length_ref, f32[2]{0:T(128)S(1)} %dynamic_slice.337.gate_ref, bf16[2048,768]{1,0:T(8,128)(2,1)S(1)} %pad_maximum_fusion.1.q_ref.k_ref.v_ref, ...), custom_call_target="tpu_custom_call" | custom-call | flops 4294967296 | bytes 6291456 | tf_op jit(solution)/shard_map/attend/pallas_call | solution.py:156
  670.5 99.9 %feed_forward.2 = (bf16[1024,2048]{1,0:T(8,128)(2,1)}, bf16[1024,2048]{1,0:T(8,128)(2,1)}, bf16[1024,2048]{1,0:T(8,128)(2,1)}, bf16[1024,2048]{1,0:T(8,128)(2,1)}, bf16[1024,2048]{1,0:T(8,128)(2,1)}) custom-call(bf16[1024,2048]{1,0:T(8,128)(2,1)} %copy-done.91, bf16[1024,2048]{1,0:T(8,128)(2,1)} %constant_dynamic-update-slice_fusion.16.grad_ref, ...), custom_call_target="tpu_custom_call" | custom-call | flops 51539607552 | bytes 54525952 | tf_op jit(solution)/shard_map/feed_forward/pallas_call | solution.py:393
  801.2 15.9 collective-permute-done.31
  877.4 99.8 %feed_forward.3 = (bf16[1024,2048]{1,0:T(8,128)(2,1)}, bf16[1024,2048]{1,0:T(8,128)(2,1)}, bf16[1024,2048]{1,0:T(8,128)(2,1)}, bf16[1024,2048]{1,0:T(8,128)(2,1)}, bf16[1024,2048]{1,0:T(8,128)(2,1)}) custom-call(bf16[1024,2048]{1,0:T(8,128)(2,1)} %constant_dynamic-update-slice_fusion.24.rows_ref, ...), custom_call_target="tpu_custom_call" | custom-call | flops 51539607552 | bytes 54525952 | tf_op jit(solution)/shard_map/feed_forward/pallas_call | solution.py:393
  1079.9 18.1 collective-permute-done.54
  1174.5 21.1 %attend_back.2 = (bf16[2048,768]{1,0:T(8,128)(2,1)S(1)}, f32[2,1,128]{2,1,0:T(1,128)S(1)}) custom-call(s32[1]{0:T(128)} %bitcast.1.length_ref, f32[2]{0:T(128)S(1)} %dynamic_slice.337.gate_ref, bf16[2048,768]{1,0:T(8,128)(2,1)S(1)} %copy-done.3, bf16[2048,768]{1,0:T(8,128)(2,1)S(1)} %copy-done.3, bf16[2048,768]{1,0:T(8,128)(2,1)S(1)} %copy-done.3, ...), custom_call_target="tpu_custom_call" | custom-call | flops 10737418240 | bytes 10485760 | tf_op jit(solution)/shard_map/attend_back/pallas_call | solution.py:286
  1208.1 24.1 %attend_back.3 = (bf16[2048,768]{1,0:T(8,128)(2,1)S(1)}, f32[2,1,128]{2,1,0:T(1,128)S(1)}) custom-call(s32[1]{0:T(128)} %bitcast.22.length_ref, f32[2]{0:T(128)S(1)} %dynamic_slice.337.gate_ref, bf16[2048,768]{1,0:T(8,128)(2,1)S(1)} %copy-done.5, bf16[2048,768]{1,0:T(8,128)(2,1)S(1)} %copy-done.5, bf16[2048,768]{1,0:T(8,128)(2,1)S(1)} %copy-done.5, ...), custom_call_target="tpu_custom_call" | custom-call | flops 10737418240 | bytes 10485760 | tf_op jit(solution)/shard_map/attend_back/pallas_call | solution.py:286
  1345.3 35.6 %collective-permute-done.84 = bf16[128,2048]{1,0:T(8,128)(2,1)S(1)} collective-permute-done((bf16[128,2048]{1,0:T(8,128)(2,1)S(1)}, bf16[128,2048]{1,0:T(8,128)(2,1)S(1)}, u32[]{:S(2)}, u32[]{:S(2)}) %collective-permute-start.84) | collective-permute-done | bytes 524320 | tf_op jit(solution)/shard_map/ppermute | solution.py:821
  1396.0 21.1 %collective-permute-done.118 = bf16[256,2048]{1,0:T(8,128)(2,1)} collective-permute-done((bf16[256,2048]{1,0:T(8,128)(2,1)}, bf16[256,2048]{1,0:T(8,128)(2,1)}, u32[]{:S(2)}, u32[]{:S(2)}) %collective-permute-start.118) | collective-permute-done | bytes 1048608 | tf_op jit(solution)/shard_map/ppermute | solution.py:469
  1442.9 17.6 collective-permute-done.110
  1501.2 14.1 collective-permute-done.105
  1517.3 20.4 %collective-permute-done.113 = bf16[256,2048]{1,0:T(8,128)(2,1)S(1)} collective-permute-done((bf16[256,2048]{1,0:T(8,128)(2,1)S(1)}, bf16[256,2048]{1,0:T(8,128)(2,1)S(1)}, u32[]{:S(2)}, u32[]{:S(2)}) %collective-permute-start.113) | collective-permute-done | bytes 1048608 | tf_op jit(solution)/shard_map/ppermute | solution.py:472
  1595.9 16.6 collective-permute-done.98
  1624.3 13.8 collective-permute-done.111
  1650.0 12.8 collective-permute-done.77
  1665.9 40.9 %collective-permute-done.75 = bf16[256,2048]{1,0:T(8,128)(2,1)S(1)} collective-permute-done((bf16[256,2048]{1,0:T(8,128)(2,1)S(1)}, bf16[256,2048]{1,0:T(8,128)(2,1)S(1)}, u32[]{:S(2)}, u32[]{:S(2)}) %collective-permute-start.75) | collective-permute-done | bytes 1048608 | tf_op jit(solution)/shard_map/ppermute | solution.py:469
  1711.7 17.6 collective-permute-done.64
  1742.4 12.8 collective-permute-done.67
  1761.5 18.4 maximum_convert_fusion
  1780.7 19.5 %collective-permute-done.68 = bf16[256,2048]{1,0:T(8,128)(2,1)S(1)} collective-permute-done((bf16[256,2048]{1,0:T(8,128)(2,1)S(1)}, bf16[256,2048]{1,0:T(8,128)(2,1)S(1)}, u32[]{:S(2)}, u32[]{:S(2)}) %collective-permute-start.68) | collective-permute-done | bytes 1048608 | tf_op jit(solution)/shard_map/ppermute | solution.py:472
  1811.9 121.4 %all-reduce.4.cloned.1.call-done = f32[131584]{0:T(1024)} async-done(((f32[131584]{0:T(1024)}), f32[131584]{0:T(1024)}) %all-reduce.4.cloned.1.call-update) | async-done | bytes 526352
  (766 shorter events, 898.2 us)
Async XLA Ops:
  7.2 494.6 %all-gather.5.cloned.1.call-start = ((), (), s32[]{:S(2)}) async-start(), calls=%async_computation.4 | async-start | bytes 4456448 | tf_op jit(solution)/shard_map/all_gather | solution.py:614
  9.1 515.2 %all-gather.7.cloned.1.call-start = ((), (), s32[]{:S(2)}) async-start(), calls=%async_computation.5 | async-start | bytes 10485760 | tf_op jit(solution)/shard_map/all_gather | solution.py:620
  12.3 557.6 %all-gather.9.cloned.1.call-start = ((), (), s32[]{:S(2)}) async-start(), calls=%async_computation.6 | async-start | bytes 5242880 | tf_op jit(solution)/shard_map/all_gather | solution.py:626
  18.6 115.5 %collective-permute-start.23 = (bf16[128,2048]{1,0:T(8,128)(2,1)}, bf16[128,2048]{1,0:T(8,128)(2,1)}, u32[]{:S(2)}, u32[]{:S(2)}) collective-permute-start(bf16[128,2048]{1,0:T(8,128)(2,1)} %get-tuple-element.215), channel_id=1, source_target_pairs={{0,8},{4,12},{8,0},{12,4},{1,9},{5,13},{9,1},{13,5},{2,10},{6,14},... | collective-permute-start | bytes 1572872 | tf_op jit(solution)/shard_map/ppermute | solution.py:498
  19.8 116.8 %collective-permute-start.24 = (bf16[128,2048]{1,0:T(8,128)(2,1)}, bf16[128,2048]{1,0:T(8,128)(2,1)}, u32[]{:S(2)}, u32[]{:S(2)}) collective-permute-start(bf16[128,2048]{1,0:T(8,128)(2,1)} %get-tuple-element.215), channel_id=1, source_target_pairs={{0,4},{4,0},{8,12},{12,8},{1,5},{5,1},{9,13},{13,9},{2,6},{6,2},{1... | collective-permute-start | bytes 1572872 | tf_op jit(solution)/shard_map/ppermute | solution.py:498
  27.4 98.5 %collective-permute-start.6 = (bf16[128,2048]{1,0:T(8,128)(2,1)}, bf16[128,2048]{1,0:T(8,128)(2,1)}, u32[]{:S(2)}, u32[]{:S(2)}) collective-permute-start(bf16[128,2048]{1,0:T(8,128)(2,1)} %get-tuple-element.198), channel_id=1, source_target_pairs={{0,0},{1,1},{2,3},{18,16},{19,17},{20,22},{21,23},{5,4},{6,5},{7,6... | collective-permute-start | bytes 1572872 | tf_op jit(solution)/shard_map/ppermute | solution.py:594
  34.3 92.9 %collective-permute-start.7 = (bf16[128,2048]{1,0:T(8,128)(2,1)}, bf16[128,2048]{1,0:T(8,128)(2,1)}, u32[]{:S(2)}, u32[]{:S(2)}) collective-permute-start(bf16[128,2048]{1,0:T(8,128)(2,1)} %get-tuple-element.199), channel_id=1, source_target_pairs={{0,0},{1,2},{2,3},{19,16},{20,22},{5,4},{6,5},{7,7},{24,24},{25,26... | collective-permute-start | bytes 1572872 | tf_op jit(solution)/shard_map/ppermute | solution.py:594
  35.8 93.1 %collective-permute-start.8 = (bf16[128,2048]{1,0:T(8,128)(2,1)}, bf16[128,2048]{1,0:T(8,128)(2,1)}, u32[]{:S(2)}, u32[]{:S(2)}) collective-permute-start(bf16[128,2048]{1,0:T(8,128)(2,1)} %get-tuple-element.197), channel_id=1, source_target_pairs={{0,1},{1,2},{19,17},{20,23},{6,6},{7,7},{24,25},{25,26},{11,9},{12... | collective-permute-start | bytes 1572872 | tf_op jit(solution)/shard_map/ppermute | solution.py:594
  141.5 126.7 %collective-permute-start.35 = (bf16[256,2048]{1,0:T(8,128)(2,1)S(1)}, bf16[256,2048]{1,0:T(8,128)(2,1)S(1)}, u32[]{:S(2)}, u32[]{:S(2)}) collective-permute-start(bf16[256,2048]{1,0:T(8,128)(2,1)S(1)} %copy-done.81), channel_id=1, source_target_pairs={{0,1},{1,2},{2,3},{4,5},{5,6},{6,7},{8,9},{9,10},{10,11},{12,13},{... | collective-permute-start | bytes 3145736 | tf_op jit(solution)/shard_map/ppermute | solution.py:443
  147.6 141.3 %collective-permute-start.36 = (bf16[256,2048]{1,0:T(8,128)(2,1)S(1)}, bf16[256,2048]{1,0:T(8,128)(2,1)S(1)}, u32[]{:S(2)}, u32[]{:S(2)}) collective-permute-start(bf16[256,2048]{1,0:T(8,128)(2,1)S(1)} %copy-done.81), channel_id=1, source_target_pairs={{1,0},{2,1},{3,2},{5,4},{6,5},{7,6},{9,8},{10,9},{11,10},{13,12},{... | collective-permute-start | bytes 3145736 | tf_op jit(solution)/shard_map/ppermute | solution.py:446
  159.0 127.5 %collective-permute-start.9 = (bf16[128,2048]{1,0:T(8,128)(2,1)S(1)}, bf16[128,2048]{1,0:T(8,128)(2,1)S(1)}, u32[]{:S(2)}, u32[]{:S(2)}) collective-permute-start(bf16[128,2048]{1,0:T(8,128)(2,1)S(1)} %get-tuple-element.196), channel_id=1, source_target_pairs={{0,8},{4,12},{8,0},{12,4},{1,9},{5,13},{9,1},{13,5},{2,10},{6,14},... | collective-permute-start | bytes 1572872 | tf_op jit(solution)/shard_map/ppermute | solution.py:498
  202.7 112.0 %collective-permute-start.2 = (bf16[256,2048]{1,0:T(8,128)(2,1)S(1)}, bf16[256,2048]{1,0:T(8,128)(2,1)S(1)}, u32[]{:S(2)}, u32[]{:S(2)}) collective-permute-start(bf16[256,2048]{1,0:T(8,128)(2,1)S(1)} %collective-permute-done), channel_id=1, source_target_pairs={{1,2},{2,3},{5,6},{6,7},{9,10},{10,11},{13,14},{14,15},{17,18},{18... | collective-permute-start | bytes 3145736 | tf_op jit(solution)/shard_map/ppermute | solution.py:443
  219.2 98.5 %collective-permute-start.3 = (bf16[256,2048]{1,0:T(8,128)(2,1)S(1)}, bf16[256,2048]{1,0:T(8,128)(2,1)S(1)}, u32[]{:S(2)}, u32[]{:S(2)}) collective-permute-start(bf16[256,2048]{1,0:T(8,128)(2,1)S(1)} %collective-permute-done.1), channel_id=1, source_target_pairs={{1,0},{2,1},{5,4},{6,5},{9,8},{10,9},{13,12},{14,13},{17,16},{18,1... | collective-permute-start | bytes 3145736 | tf_op jit(solution)/shard_map/ppermute | solution.py:446
  268.2 115.5 %collective-permute-start.37 = (bf16[256,2048]{1,0:T(8,128)(2,1)S(1)}, bf16[256,2048]{1,0:T(8,128)(2,1)S(1)}, u32[]{:S(2)}, u32[]{:S(2)}) collective-permute-start(bf16[256,2048]{1,0:T(8,128)(2,1)S(1)} %collective-permute-done.35), channel_id=1, source_target_pairs={{1,2},{2,3},{5,6},{6,7},{9,10},{10,11},{13,14},{14,15},{17,18},{18... | collective-permute-start | bytes 3145736 | tf_op jit(solution)/shard_map/ppermute | solution.py:443
  288.9 98.9 %collective-permute-start.38 = (bf16[256,2048]{1,0:T(8,128)(2,1)S(1)}, bf16[256,2048]{1,0:T(8,128)(2,1)S(1)}, u32[]{:S(2)}, u32[]{:S(2)}) collective-permute-start(bf16[256,2048]{1,0:T(8,128)(2,1)S(1)} %collective-permute-done.36), channel_id=1, source_target_pairs={{1,0},{2,1},{5,4},{6,5},{9,8},{10,9},{13,12},{14,13},{17,16},{18,1... | collective-permute-start | bytes 3145736 | tf_op jit(solution)/shard_map/ppermute | solution.py:446
  299.7 154.5 %collective-permute-start.26 = (bf16[128,2048]{1,0:T(8,128)(2,1)S(1)}, bf16[128,2048]{1,0:T(8,128)(2,1)S(1)}, u32[]{:S(2)}, u32[]{:S(2)}) collective-permute-start(bf16[128,2048]{1,0:T(8,128)(2,1)S(1)} %copy-done.84), channel_id=1, source_target_pairs={{0,4},{4,0},{8,12},{12,8},{1,5},{5,1},{9,13},{13,9},{2,6},{6,2},{1... | collective-permute-start | bytes 1572872 | tf_op jit(solution)/shard_map/ppermute | solution.py:498
  314.7 111.1 %collective-permute-start.4 = (bf16[256,2048]{1,0:T(8,128)(2,1)S(1)}, bf16[256,2048]{1,0:T(8,128)(2,1)S(1)}, u32[]{:S(2)}, u32[]{:S(2)}) collective-permute-start(bf16[256,2048]{1,0:T(8,128)(2,1)S(1)} %collective-permute-done.2), channel_id=1, source_target_pairs={{2,3},{6,7},{10,11},{14,15},{18,19},{22,23},{26,27},{30,31}} | collective-permute-start | bytes 3145736 | tf_op jit(solution)/shard_map/ppermute | solution.py:443
  317.7 110.3 %collective-permute-start.5 = (bf16[256,2048]{1,0:T(8,128)(2,1)S(1)}, bf16[256,2048]{1,0:T(8,128)(2,1)S(1)}, u32[]{:S(2)}, u32[]{:S(2)}) collective-permute-start(bf16[256,2048]{1,0:T(8,128)(2,1)S(1)} %collective-permute-done.3), channel_id=1, source_target_pairs={{1,0},{5,4},{9,8},{13,12},{17,16},{21,20},{25,24},{29,28}} | collective-permute-start | bytes 3145736 | tf_op jit(solution)/shard_map/ppermute | solution.py:446
  455.3 107.0 %collective-permute-start.51 = (bf16[128,2048]{1,0:T(8,128)(2,1)}, bf16[128,2048]{1,0:T(8,128)(2,1)}, u32[]{:S(2)}, u32[]{:S(2)}) collective-permute-start(bf16[128,2048]{1,0:T(8,128)(2,1)} %get-tuple-element.219), channel_id=1, source_target_pairs={{0,4},{4,0},{8,12},{12,8},{1,5},{5,1},{9,13},{13,9},{2,6},{6,2},{1... | collective-permute-start | bytes 1572872 | tf_op jit(solution)/shard_map/ppermute | solution.py:498
  501.8 103.0 %collective-permute-start.16 = (bf16[2048,1024]{1,0:T(8,128)(2,1)}, bf16[2048,1024]{1,0:T(8,128)(2,1)}, u32[]{:S(2)}, u32[]{:S(2)}) collective-permute-start(bf16[2048,1024]{1,0:T(8,128)(2,1)} %all-gather.5.cloned.1.call-done), channel_id=1, source_target_pairs={{0,16},{16,0},{1,17},{17,1},{2,18},{18,2},{3,19},{19,3},{4,20},{20... | collective-permute-start | bytes 12582920 | tf_op jit(solution)/shard_map/ppermute | solution.py:424
  524.3 146.3 %collective-permute-start.29 = (bf16[1024,4096]{1,0:T(8,128)(2,1)}, bf16[1024,4096]{1,0:T(8,128)(2,1)}, u32[]{:S(2)}, u32[]{:S(2)}) collective-permute-start(bf16[1024,4096]{1,0:T(8,128)(2,1)} %all-gather.7.cloned.1.call-done.inner_a), channel_id=1, source_target_pairs={{0,16},{16,0},{1,17},{17,1},{2,18},{18,2},{3,19},{19,3},{4,20},{20... | collective-permute-start | bytes 25165832 | tf_op jit(solution)/shard_map/ppermute | solution.py:424
  569.9 100.7 %collective-permute-start.30 = (bf16[1024,2048]{1,0:T(8,128)(2,1)}, bf16[1024,2048]{1,0:T(8,128)(2,1)}, u32[]{:S(2)}, u32[]{:S(2)}) collective-permute-start(bf16[1024,2048]{1,0:T(8,128)(2,1)} %all-gather.9.cloned.1.call-done.down_a), channel_id=1, source_target_pairs={{0,16},{16,0},{1,17},{17,1},{2,18},{18,2},{3,19},{19,3},{4,20},{20... | collective-permute-start | bytes 12582920 | tf_op jit(solution)/shard_map/ppermute | solution.py:424
  1020.0 246.7 %collective-permute-start.116 = (bf16[1024,2048]{1,0:T(8,128)(2,1)}, bf16[1024,2048]{1,0:T(8,128)(2,1)}, u32[]{:S(2)}, u32[]{:S(2)}) collective-permute-start(bf16[1024,2048]{1,0:T(8,128)(2,1)} %add_convert_fusion.1), channel_id=1, source_target_pairs={{0,16},{16,0},{1,17},{17,1},{2,18},{18,2},{3,19},{19,3},{4,20},{20... | collective-permute-start | bytes 12582920 | tf_op jit(solution)/shard_map/ppermute | solution.py:424
  1075.6 205.7 %collective-permute-start.100 = (bf16[1024,2048]{1,0:T(8,128)(2,1)}, bf16[1024,2048]{1,0:T(8,128)(2,1)}, u32[]{:S(2)}, u32[]{:S(2)}) collective-permute-start(bf16[1024,2048]{1,0:T(8,128)(2,1)} %add_convert_fusion.5), channel_id=1, source_target_pairs={{0,16},{16,0},{1,17},{17,1},{2,18},{18,2},{3,19},{19,3},{4,20},{20... | collective-permute-start | bytes 12582920 | tf_op jit(solution)/shard_map/ppermute | solution.py:424
  1077.6 216.9 %collective-permute-start.108 = (bf16[1024,2048]{1,0:T(8,128)(2,1)}, bf16[1024,2048]{1,0:T(8,128)(2,1)}, u32[]{:S(2)}, u32[]{:S(2)}) collective-permute-start(bf16[1024,2048]{1,0:T(8,128)(2,1)} %add_convert_fusion.3), channel_id=1, source_target_pairs={{0,16},{16,0},{1,17},{17,1},{2,18},{18,2},{3,19},{19,3},{4,20},{20... | collective-permute-start | bytes 12582920 | tf_op jit(solution)/shard_map/ppermute | solution.py:424
  1155.0 231.7 %collective-permute-start.88 = (bf16[2048,1024]{1,0:T(8,128)(2,1)}, bf16[2048,1024]{1,0:T(8,128)(2,1)}, u32[]{:S(2)}, u32[]{:S(2)}) collective-permute-start(bf16[2048,1024]{1,0:T(8,128)(2,1)} %add_convert_fusion.7), channel_id=1, source_target_pairs={{0,16},{16,0},{1,17},{17,1},{2,18},{18,2},{3,19},{19,3},{4,20},{20... | collective-permute-start | bytes 12582920 | tf_op jit(solution)/shard_map/ppermute | solution.py:424
  1172.9 760.3 %all-reduce.4.cloned.1.call-start = ((), (), s32[]{:S(2)}) async-start(), calls=%async_computation.7 | async-start | bytes 1056768
  1294.5 98.8 %collective-permute-start.120 = (bf16[256,2048]{1,0:T(8,128)(2,1)}, bf16[256,2048]{1,0:T(8,128)(2,1)}, u32[]{:S(2)}, u32[]{:S(2)}) collective-permute-start(bf16[256,2048]{1,0:T(8,128)(2,1)} %get-tuple-element.123), channel_id=1, source_target_pairs={{3,2},{7,6},{11,10},{15,14},{19,18},{23,22},{27,26},{31,30}} | collective-permute-start | bytes 3145736 | tf_op jit(solution)/shard_map/ppermute | solution.py:472
  1442.7 111.9 %collective-permute-start.73 = (bf16[1024,2048]{1,0:T(8,128)(2,1)}, bf16[1024,2048]{1,0:T(8,128)(2,1)}, u32[]{:S(2)}, u32[]{:S(2)}) collective-permute-start(bf16[1024,2048]{1,0:T(8,128)(2,1)} %convolution_convert_fusion), channel_id=1, source_target_pairs={{0,16},{16,0},{1,17},{17,1},{2,18},{18,2},{3,19},{19,3},{4,20},{20... | collective-permute-start | bytes 12582920 | tf_op jit(solution)/shard_map/ppermute | solution.py:424
  1460.5 101.2 %collective-permute-start.62 = (bf16[1024,2048]{1,0:T(8,128)(2,1)}, bf16[1024,2048]{1,0:T(8,128)(2,1)}, u32[]{:S(2)}, u32[]{:S(2)}) collective-permute-start(bf16[1024,2048]{1,0:T(8,128)(2,1)} %convolution_convert_fusion.1), channel_id=1, source_target_pairs={{0,16},{16,0},{1,17},{17,1},{2,18},{18,2},{3,19},{19,3},{4,20},{20... | collective-permute-start | bytes 12582920 | tf_op jit(solution)/shard_map/ppermute | solution.py:424
  1492.8 121.8 %collective-permute-start.119 = (bf16[256,2048]{1,0:T(8,128)(2,1)}, bf16[256,2048]{1,0:T(8,128)(2,1)S(1)}, u32[]{:S(2)}, u32[]{:S(2)}) collective-permute-start(bf16[256,2048]{1,0:T(8,128)(2,1)} %get-tuple-element.120), channel_id=1, source_target_pairs={{0,1},{1,2},{2,3},{4,5},{5,6},{6,7},{8,9},{9,10},{10,11},{12,13},{... | collective-permute-start | bytes 3145736 | tf_op jit(solution)/shard_map/ppermute | solution.py:469
  1662.8 95.9 %collective-permute-start.115 = (bf16[256,2048]{1,0:T(8,128)(2,1)S(1)}, bf16[256,2048]{1,0:T(8,128)(2,1)S(1)}, u32[]{:S(2)}, u32[]{:S(2)}) collective-permute-start(bf16[256,2048]{1,0:T(8,128)(2,1)S(1)} %add_convert_fusion.16), channel_id=1, source_target_pairs={{0,16},{16,0},{1,17},{17,1},{2,18},{18,2},{3,19},{19,3},{4,20},{20... | collective-permute-start | bytes 3145736 | tf_op jit(solution)/shard_map/ppermute | solution.py:424
  (231 other events, 5944.5 us)
Sparse Core Ops, SparseCore 0:
  11.4 89.0 all-gather.4
  102.6 201.4 all-gather.6
  305.6 113.5 all-gather.8
  1804.9 128.2 all-reduce.3

commit v2 on v1

--- a/solution.py
+++ b/solution.py
@@ -321,107 +321,183 @@
     )(length, gate, projected, projected, projected, memory, normalizer, dot_read, lse, grad_mixed)
 
 
-def mlp_kernel(
-    tiles,
-    rows_ref,
-    grad_ref,
-    inner_a,
-    inner_b,
-    down_a,
-    down_b,
-    out_ref,
-    grad_two_ref,
-    hidden_ref,
-    grad_gate_ref,
-    grad_up_ref,
-    out_acc,
-    grad_acc,
+def unit_kernel(
+    rows_ref, grad_ref, inner_ref, down_ref, hidden_ref, grad_gate_ref, grad_up_ref
 ):
-    step = pl.program_id(0)
     width = rows_ref.shape[1]
-
-    @pl.when(step == 0)
-    def _():
-        out_acc[...] = jnp.zeros_like(out_acc)
-        grad_acc[...] = jnp.zeros_like(grad_acc)
-
-    def visit(inner_ref, down_ref):
-        gate_weight = inner_ref[:, :width]
-        up_weight = inner_ref[:, width:]
-        down = down_ref[...]
-        rows = rows_ref[...]
-        gates = nt(rows, gate_weight)
-        ups = nt(rows, up_weight)
-        sigmoid = 1.0 / (1.0 + jnp.exp(-gates))
-        silu = gates * sigmoid
-        hidden = (silu * ups).astype(BF16)
-        hidden_ref[...] = hidden
-        out_acc[...] += nn(hidden, down)
-        grad_hidden = nt(grad_ref[...], down)
-        grad_gates = (grad_hidden * ups * (sigmoid * (1.0 + gates * (1.0 - sigmoid)))).astype(BF16)
-        grad_ups = (grad_hidden * silu).astype(BF16)
-        grad_gate_ref[...] = grad_gates
-        grad_up_ref[...] = grad_ups
-        grad_acc[...] += nn(grad_gates, gate_weight) + nn(grad_ups, up_weight)
-
-    @pl.when(step < tiles)
-    def _():
-        visit(inner_a, down_a)
-
-    @pl.when(step >= tiles)
-    def _():
-        visit(inner_b, down_b)
-
-    @pl.when(step == 2 * tiles - 1)
-    def _():
-        out_ref[...] = out_acc[...].astype(BF16)
-        grad_two_ref[...] = grad_acc[...].astype(BF16)
-
-
-def mlp(rows, grads, inner_a, inner_b, down_a, down_b):
+    rows = rows_ref[...]
+    gates = nt(rows, inner_ref[:, :width])
+    ups = nt(rows, inner_ref[:, width:])
+    grad_hidden = nt(grad_ref[...], down_ref[...])
+    sigmoid = 1.0 / (1.0 + jnp.exp(-gates))
+    silu = gates * sigmoid
+    hidden_ref[...] = (silu * ups).astype(BF16)
+    grad_gate_ref[...] = (
+        grad_hidden * ups * (sigmoid * (1.0 + gates * (1.0 - sigmoid)))
+    ).astype(BF16)
+    grad_up_ref[...] = (grad_hidden * silu).astype(BF16)
+
+
+def unit_pass(rows, grads, inner, down):
     count, width = rows.shape
-    units = inner_a.shape[0]
+    units = inner.shape[0]
     tile = min(256, units)
-    tiles = units // tile
-    first = lambda t: (jnp.minimum(t, tiles - 1), 0)
-    second = lambda t: (jnp.maximum(t - tiles, 0), 0)
-    whole = lambda t: (0, 0)
-    once = pl.Buffered(1)
+    resident = pl.BlockSpec((count, width), lambda t: (0, 0), pipeline_mode=pl.Buffered(1))
     column = pl.BlockSpec((count, tile), lambda t: (0, t))
-    unit_shape = jax.ShapeDtypeStruct((count, 2 * units), BF16)
+    unit_shape = jax.ShapeDtypeStruct((count, units), BF16)
+    return pl.pallas_call(
+        unit_kernel,
+        grid=(units // tile,),
+        in_specs=[
+            resident,
+            resident,
+            pl.BlockSpec((tile, 2 * width), lambda t: (t, 0)),
+            pl.BlockSpec((tile, width), lambda t: (t, 0)),
+        ],
+        out_specs=[column] * 3,
+        out_shape=[unit_shape] * 3,
+        compiler_params=pltpu.CompilerParams(vmem_limit_bytes=56 << 20),
+        cost_estimate=pl.CostEstimate(
+            flops=2 * 3 * count * width * units,
+            bytes_accessed=units * (6 * width + 6 * count) + 4 * count * width,
+            transcendentals=count * units,
+        ),
+        name="unit_pass",
+    )(rows, grads, inner, down)
+
+
+def row_kernel(*refs):
+    hidden, gates, ups, gate_w, up_w, down_w = (refs[2 * i : 2 * i + 2] for i in range(6))
+    out_ref, grad_two_ref = refs[12:]
+    grad_two_ref[...] = (
+        nn(gates[0][...], gate_w[0][...])
+        + nn(gates[1][...], gate_w[1][...])
+        + nn(ups[0][...], up_w[0][...])
+        + nn(ups[1][...], up_w[1][...])
+    ).astype(BF16)
+    out_ref[...] = (
+        nn(hidden[0][...], down_w[0][...]) + nn(hidden[1][...], down_w[1][...])
+    ).astype(BF16)
+
+
+def row_pass(hidden, grad_gates, grad_ups, inner, down):
+    count, units = hidden[0].shape
+    width = down[0].shape[1]
+    tile = min(256, width)
+    tiles = width // tile
+    resident = pl.BlockSpec((count, units), lambda t: (0, 0), pipeline_mode=pl.Buffered(1))
+    low = pl.BlockSpec((units, tile), lambda t: (0, t))
+    high = pl.BlockSpec((units, tile), lambda t: (0, tiles + t))
+    column = pl.BlockSpec((count, tile), lambda t: (0, t))
     row_shape = jax.ShapeDtypeStruct((count, width), BF16)
     return pl.pallas_call(
-        functools.partial(mlp_kernel, tiles),
-        grid=(2 * tiles,),
-        in_specs=[
-            pl.BlockSpec((count, width), whole, pipeline_mode=once),
-            pl.BlockSpec((count, width), whole, pipeline_mode=once),
-            pl.BlockSpec((tile, 2 * width), first),
-            pl.BlockSpec((tile, 2 * width), second),
-            pl.BlockSpec((tile, width), first),
-            pl.BlockSpec((tile, width), second),
-        ],
-        out_specs=[
-            pl.BlockSpec((count, width), whole, pipeline_mode=once),
-            pl.BlockSpec((count, width), whole, pipeline_mode=once),
-            column,
-            column,
-            column,
-        ],
-        out_shape=[row_shape, row_shape, unit_shape, unit_shape, unit_shape],
-        scratch_shapes=[pltpu.VMEM((count, width), F32), pltpu.VMEM((count, width), F32)],
-        compiler_params=pltpu.CompilerParams(vmem_limit_bytes=60 << 20),
+        row_kernel,
+        grid=(tiles,),
+        in_specs=[resident] * 6 + [low, low, high, high, low, low],
+        out_specs=[column] * 2,
+        out_shape=[row_shape] * 2,
+        compiler_params=pltpu.CompilerParams(vmem_limit_bytes=56 << 20),
         cost_estimate=pl.CostEstimate(
-            flops=2 * 6 * count * width * 2 * units,
-            bytes_accessed=2 * units * (6 * width + 6 * count) + 8 * count * width,
-            transcendentals=count * 2 * units,
+            flops=2 * 3 * count * width * 2 * units,
+            bytes_accessed=12 * units * (width + count) + 4 * count * width,
+            transcendentals=0,
         ),
-        name="feed_forward",
-    )(rows, grads, inner_a, inner_b, down_a, down_b)
+        name="row_pass",
+    )(*hidden, *grad_gates, *grad_ups, *inner, *inner, *down)
+
+
+def weight_kernel(pairs, *refs):
+    out_ref = refs[-1]
+    total = tn(refs[0][...], refs[1][...])
+    for at in range(1, pairs):
+        total += tn(refs[2 * at][...], refs[2 * at + 1][...])
+    if len(refs) > 2 * pairs + 1:
+        total += refs[2 * pairs][...].astype(F32)
+    out_ref[...] = total.astype(BF16)
+
+
+def weight_pass(pairs, extra=None):
+    size, width = pairs[0][0].shape[1], pairs[0][1].shape[1]
+    tile = min(256, size)
+    in_specs, operands, flops, moved = [], [], 0, 2 * size * width
+    for left, right in pairs:
+        count = left.shape[0]
+        in_specs.append(pl.BlockSpec((count, tile), lambda t: (0, t)))
+        in_specs.append(
+            pl.BlockSpec((count, width), lambda t: (0, 0), pipeline_mode=pl.Buffered(1))
+        )
+        operands += [left, right]
+        flops += 2 * count * size * width
+        moved += 2 * count * (size + width)
+    if extra is not None:
+        in_specs.append(pl.BlockSpec((tile, width), lambda t: (t, 0)))
+        operands.append(extra)
+        moved += 2 * size * width
+    return pl.pallas_call(
+        functools.partial(weight_kernel, len(pairs)),
+        grid=(size // tile,),
+        in_specs=in_specs,
+        out_specs=pl.BlockSpec((tile, width), lambda t: (t, 0)),
+        out_shape=jax.ShapeDtypeStruct((size, width), BF16),
+        compiler_params=pltpu.CompilerParams(vmem_limit_bytes=56 << 20),
+        cost_estimate=pl.CostEstimate(flops=flops, bytes_accessed=moved, transcendentals=0),
+        name="weight_pass",
+    )(*operands)
+
+
+def back_kernel(half_ref, grad_ref, weight_ref, rows_ref, out_ref, gain_ref):
+    @pl.when(pl.program_id(0) == 0)
+    def _():
+        gain_ref[...] = jnp.zeros_like(gain_ref)
+
+    part = nn(grad_ref[...], weight_ref[...])
+    out_ref[...] = part.astype(BF16)
+    rows = rows_ref[...].astype(F32)
+    scale = lax.rsqrt(jnp.mean(rows * rows, axis=-1, keepdims=True) + EPSILON)
+    gain_ref[...] += jnp.sum(part * (rows * scale), axis=0, keepdims=True)
+
+
+def project_back(half, grads, weight, rows):
+    count, outs = grads.shape[0] // 2, grads.shape[1]
+    width = weight.shape[1]
+    block = min(256, count)
+    steps = count // block
+    return pl.pallas_call(
+        back_kernel,
+        grid_spec=pltpu.PrefetchScalarGridSpec(
+            num_scalar_prefetch=1,
+            grid=(steps,),
+            in_specs=[
+                pl.BlockSpec((block, outs), lambda i, at: (at[0] * steps + i, 0)),
+                pl.BlockSpec((outs, width), lambda i, at: (0, 0)),
+                pl.BlockSpec((block, width), lambda i, at: (at[0] * steps + i, 0)),
+            ],
+            out_specs=[
+                pl.BlockSpec((block, width), lambda i, at: (i, 0)),
+                pl.BlockSpec((1, width), lambda i, at: (0, 0)),
+            ],
+        ),
+        out_shape=[
+            jax.ShapeDtypeStruct((count, width), BF16),
+            jax.ShapeDtypeStruct((1, width), F32),
+        ],
+        compiler_params=pltpu.CompilerParams(vmem_limit_bytes=40 << 20),
+        cost_estimate=pl.CostEstimate(
+            flops=2 * count * width * outs,
+            bytes_accessed=4 * count * width + 2 * outs * (width + count),
+            transcendentals=count,
+        ),
+        name="project_back",
+    )(jnp.reshape(half, (1,)).astype(jnp.int32), grads, weight, rows)
 
 
 def swap(values):
     return lax.ppermute(values, "rep", [(0, 1), (1, 0)])
+
+
+def after(values, *earlier):
+    earlier = [e for e in earlier if e is not None]
+    return lax.optimization_barrier((values, *earlier))[0] if earlier else values
 
 
 def add_low(left_side, right_side):
@@ -451,7 +527,7 @@
     return table[(count - 1) * rows : (2 * count - 1) * rows]
 
 
-def line_scatter(values, axis):
+def line_scatter(values, axis, pins=()):
     count = lax.axis_size(axis)
     here = lax.axis_index(axis)
     rows = values.shape[0] // count
@@ -472,6 +548,8 @@
         falling = lax.ppermute(
             down.astype(BF16), axis, [(a, a - 1) for a in range(count) if a - reach >= 0]
         )
+        if hop <= len(pins):
+            rising, falling = after(rising, pins[hop - 1]), after(falling, pins[hop - 1])
     return block(here) + rising.astype(F32) + falling.astype(F32)
 
 
@@ -500,19 +578,198 @@
     return jnp.concatenate(parts, axis=0)
 
 
-def cube_scatter(values, axis):
+def cube_scatter(values, axis, pins=()):
     count = lax.axis_size(axis)
     half = values.shape[0] // 2
     parts = []
     for bits, start in zip(cube_bits(count), (0, half)):
         held = values[start : start + half]
-        for bit in bits:
+        for at, bit in enumerate(bits):
             pairs = [(a, a ^ bit) for a in range(count)]
             keep = held.shape[0] // 2
             got = lax.ppermute(held[keep:].astype(BF16), axis, pairs)
+            if at < len(pins):
+                got = after(got, pins[at])
             held = held[:keep].astype(F32) + got.astype(F32)
         parts.append(held)
     return jnp.concatenate(parts, axis=0)
+
+
+def remote(source, target, sent, landed, device):
+    return pltpu.make_async_remote_copy(
+        src_ref=source,
+        dst_ref=target,
+        send_sem=sent,
+        recv_sem=landed,
+        device_id=device,
+        device_id_type=pl.DeviceIdType.MESH,
+    )
+
+
+def greet(devices):
+    barrier = pltpu.get_barrier_semaphore()
+    for device in devices:
+        pl.semaphore_signal(barrier, inc=1, device_id=device, device_id_type=pl.DeviceIdType.MESH)
+    pl.semaphore_wait(barrier, len(devices))
+
+
+def heads_kernel(
+    sizes,
+    qkv_ref,
+    gain_ref,
+    head_ref,
+    gains_ref,
+    landed,
+    unit_sent,
+    unit_here,
+    block_sent,
+    block_here,
+    line_sent,
+    line_here,
+    cube_sent,
+    cube_here,
+    local,
+):
+    dp_count, seq_count, unit, per_shard, per_block, per_column = sizes
+    span_count = 2 * seq_count
+    block_rows = unit * per_block
+    core, column, place = lax.axis_index("rep"), lax.axis_index("dp"), lax.axis_index("seq")
+    span, shard = core * seq_count + place, column * seq_count + place
+    line = [(core, column, (place + k) % seq_count) for k in range(1, seq_count)]
+    cube = [(core, (column + k) % dp_count, place) for k in range(1, dp_count)]
+    greet(line + cube)
+
+    gains = []
+    for k, device in enumerate(line):
+        gains.append(
+            remote(gain_ref, gains_ref.at[shard], line_sent.at[k], line_here.at[k], device)
+        )
+    for copy in gains:
+        copy.start()
+    own_gain = pltpu.make_async_copy(gain_ref, gains_ref.at[shard], local.at[0])
+    own_gain.start()
+
+    def rows(ref, at, size):
+        return ref.at[pl.ds(pl.multiple_of(at * size, size), size)]
+
+    def unit_copy(i):
+        number = shard * per_shard + i
+        owner = (number // per_block) % span_count
+        source, target = rows(qkv_ref, i, unit), rows(landed, number % per_block, unit)
+        far = remote(
+            source,
+            target,
+            unit_sent.at[i],
+            unit_here.at[number % per_block],
+            (core, column, owner % seq_count),
+        )
+        near = pltpu.make_async_copy(source, target, local.at[1 + i])
+        mine = owner // seq_count == core
+        stays = owner % seq_count == place
+        return far, near, mine & jnp.logical_not(stays), mine & stays
+
+    for i in range(per_shard):
+        far, near, leaves, stays = unit_copy(i)
+        pl.when(leaves)(far.start)
+        pl.when(stays)(near.start)
+    for i in range(per_shard):
+        _, near, _, stays = unit_copy(i)
+        pl.when(stays)(near.wait)
+
+    def block_copies(part):
+        target = rows(head_ref, part, block_rows)
+        far = [
+            remote(landed, target, block_sent.at[k], block_here.at[part], device)
+            for k, device in enumerate(cube)
+        ]
+        return far, pltpu.make_async_copy(landed, target, local.at[0])
+
+    own_gain.wait()
+    for part in range(3):
+        number = part * span_count + span
+
+        @pl.when(number // per_column == column)
+        def _():
+            for j in range(per_block):
+                source = ((number * per_block + j) // per_shard) % seq_count
+
+                @pl.when(source != place)
+                def _():
+                    here = rows(landed, j, unit)
+                    remote(here, here, unit_sent.at[0], unit_here.at[j], line[0]).wait_recv()
+
+            far, near = block_copies(part)
+            for copy in far:
+                copy.start()
+            near.start()
+
+    for copy in gains:
+        copy.wait()
+    mine = gains_ref.at[pl.ds(column * seq_count, seq_count)]
+    gains = [
+        remote(mine, mine, cube_sent.at[k], cube_here.at[k], device)
+        for k, device in enumerate(cube)
+    ]
+    for copy in gains:
+        copy.start()
+    for part in range(3):
+        number = part * span_count + span
+        far, near = block_copies(part)
+
+        @pl.when(number // per_column == column)
+        def _():
+            near.wait()
+            for copy in far:
+                copy.wait_send()
+
+        @pl.when(number // per_column != column)
+        def _():
+            far[0].wait_recv()
+
+    for k, copy in enumerate(gains):
+        copy.wait_send()
+        origin = (column + dp_count - k - 1) % dp_count
+        theirs = gains_ref.at[pl.ds(origin * seq_count, seq_count)]
+        remote(theirs, theirs, cube_sent.at[k], cube_here.at[k], cube[k]).wait_recv()
+    for i in range(per_shard):
+        far, _, leaves, _ = unit_copy(i)
+        pl.when(leaves)(far.wait_send)
+
+
+def gather_heads(qkv_weight, gains, sizes):
+    dp_count, seq_count, unit, per_shard, per_block, _ = sizes
+    width = qkv_weight.shape[1]
+    block_rows = unit * per_block
+    anywhere = pl.BlockSpec(memory_space=pl.ANY)
+    dma = pltpu.SemaphoreType.DMA
+    return pl.pallas_call(
+        functools.partial(heads_kernel, sizes),
+        in_specs=[anywhere, anywhere],
+        out_specs=[anywhere, anywhere],
+        out_shape=[
+            jax.ShapeDtypeStruct((3 * block_rows, width), BF16),
+            jax.ShapeDtypeStruct((dp_count * seq_count, *gains.shape), F32),
+        ],
+        scratch_shapes=[
+            pltpu.VMEM((block_rows, width), BF16),
+            dma((per_shard,)),
+            dma((per_block,)),
+            dma((dp_count - 1,)),
+            dma((3,)),
+            dma((seq_count - 1,)),
+            dma((seq_count - 1,)),
+            dma((dp_count - 1,)),
+            dma((dp_count - 1,)),
+            dma((1 + per_shard,)),
+        ],
+        compiler_params=pltpu.CompilerParams(
+            collective_id=0, has_side_effects=True, vmem_limit_bytes=16 << 20
+        ),
+        cost_estimate=pl.CostEstimate(
+            flops=0, bytes_accessed=64 * block_rows * width, transcendentals=0
+        ),
+        name="gather_heads",
+    )(qkv_weight, gains)
 
 
 def heads_plan(shard_rows, block_rows, dp_count, seq_count, span_count):
@@ -566,7 +823,6 @@
     dp_count, seq_count = lax.axis_size("dp"), lax.axis_size("seq")
     span_count = 2 * seq_count
     total = span_rows * span_count
-    half_total = total // 2
     heads_here = head_count // span_count
     block_rows = heads_here * head_dim
     core, column, place = lax.axis_index("rep"), lax.axis_index("dp"), lax.axis_index("seq")
@@ -575,88 +831,68 @@
     inner_half = inner_weight.shape[0] // 2
 
     own_rows = [tokens[m, 0] for m in range(micros)]
-    near = [line_gather(rows, "seq") for rows in own_rows]
-    far = [swap(rows) for rows in near]
+
+    def gather_rows(rows):
+        return lax.all_gather(rows, ("rep", "seq"), axis=0, tiled=True)
+
+    all_rows = [gather_rows(own_rows[0])]
 
     unit, per_shard, per_block, per_column, rounds = heads_plan(
         qkv_weight.shape[0], block_rows, dp_count, seq_count, span_count
     )
-    landed = jnp.zeros(((per_block + 1) * unit, width), BF16)
     devices = 2 * dp_count * seq_count
-    for group in rounds:
-        send, slot, pairs = [0] * devices, [per_block] * devices, []
-        for c, col, source, target, from_unit, to_unit in group:
-            a = device_number(c, col, source, dp_count, seq_count)
-            b = device_number(c, col, target, dp_count, seq_count)
-            send[a], slot[b] = from_unit, to_unit
-            pairs.append((a, b))
-        piece = lax.dynamic_slice_in_dim(qkv_weight, pick(send, number) * unit, unit, 0)
-        piece = lax.ppermute(piece, ALL, pairs)
-        landed = lax.dynamic_update_slice_in_dim(landed, piece, pick(slot, number) * unit, 0)
-    forward_bits = cube_bits(dp_count)
-    blocks = cube_gather(landed[:block_rows], "dp")
+    shard_out, shard_gain = out_weight.shape[0], norm_gains.shape[1]
+    lanes = -(-shard_gain // 128) * 128
+    gain_tile = jnp.zeros((8, lanes), F32)
+    gain_tile = lax.dynamic_update_slice(gain_tile, norm_gains.astype(F32), (0, 0))
+    head_weight, gains_all = gather_heads(
+        qkv_weight, gain_tile, (dp_count, seq_count, unit, per_shard, per_block, per_column)
+    )
+    gains_all = jnp.swapaxes(gains_all[:, :2, :shard_gain], 0, 1).reshape(2, width)
+    gain_one, gain_two = gains_all[0:1], gains_all[1:2]
+    orders = [cube_order(bits) for bits in cube_bits(dp_count)]
+    spots = [[order.index(k) for k in range(dp_count)] for order in orders]
+
+    def column_block(gathered, half, owner):
+        sides = []
+        for side in range(2):
+            spot = pick(spots[side], owner ^ column) + side * dp_count
+            sides.append(lax.dynamic_slice_in_dim(gathered, spot * half, half, 0))
+        return sides
+
     half_block = block_rows // 2
-    orders = [cube_order(bits) for bits in forward_bits]
-    spots = [[order.index(k) for k in range(dp_count)] for order in orders]
-    head_weights = []
-    for part in range(3):
-        distance = ((part * span_count + span) // per_column) ^ column
-        for side in range(2):
-            spot = pick(spots[side], distance) + side * dp_count
-            head_weights.append(
-                lax.dynamic_slice_in_dim(blocks, spot * half_block, half_block, 0)
-            )
-    head_weight = jnp.concatenate(head_weights, axis=0)
-
-    gains_all = lax.all_gather(norm_gains, ("dp", "seq"), axis=1, tiled=True).astype(F32)
-    gain_one, gain_two = gains_all[0:1], gains_all[1:2]
     half_width = width // 2
-    out_near = lax.all_gather(
-        lax.dynamic_slice_in_dim(out_weight, core * half_width, half_width, 1),
-        ("dp", "seq"),
-        axis=0,
-        tiled=True,
-    )
-    inner_near = lax.all_gather(
-        lax.dynamic_slice_in_dim(inner_weight, core * inner_half, inner_half, 0),
-        "seq",
-        axis=0,
-        tiled=True,
-    )
-    down_near = lax.all_gather(
-        lax.dynamic_slice_in_dim(down_weight, core * inner_half, inner_half, 0),
-        "seq",
-        axis=0,
-        tiled=True,
-    )
-    out_far, inner_far, down_far = swap(out_near), swap(inner_near), swap(down_near)
+    out_line = line_gather(
+        lax.dynamic_slice_in_dim(out_weight, core * half_width, half_width, 1), "seq"
+    )
+    for rows in own_rows[1:]:
+        all_rows.append(gather_rows(after(rows, all_rows[-1], head_weight)))
+    column_out = seq_count * shard_out
+    out_blocks = cube_gather(out_line, "dp")
+    out_near = []
+    for owner in range(dp_count):
+        out_near += column_block(out_blocks, column_out // 2, owner)
+    out_near = jnp.concatenate(out_near, axis=0)
+    out_far = swap(out_near)
 
     positions = span * span_rows + jnp.arange(span_rows)
     gate_share = jax.nn.sigmoid(gate_logit)
     gate_here = lax.dynamic_slice_in_dim(gate_share, span * heads_here, heads_here, 0)
     near_at, far_at = core * half_width, (1 - core) * half_width
-
-    live_cots, grad_lows, grad_rows = [], [], []
-    for m in range(micros):
-        live_rows = (positions < lengths[m, 0]).astype(F32)
-        live = cotangent[m, 0].astype(F32) * live_rows[:, None]
-        live_cots.append(live)
-        grad_lows.append(live.astype(BF16))
-        grad_rows.append(cube_gather(grad_lows[m], "dp"))
+    low_first = core == 0
 
     saved = []
     outputs, new_memories, new_norms = [], [], []
     for m in range(micros):
-        hidden_near, projected_near = project(near[m], gain_one, head_weight)
-        hidden_far, projected_far = project(far[m], gain_one, head_weight)
-        low_first = core == 0
-        projected = jnp.concatenate(
-            [
-                jnp.where(low_first, projected_near, projected_far),
-                jnp.where(low_first, projected_far, projected_near),
-            ],
-            axis=0,
-        )
+        hidden_one, projected = project(all_rows[m], gain_one, head_weight)
+        live_rows = (positions < lengths[m, 0]).astype(F32)
+        live = cotangent[m, 0].astype(F32) * live_rows[:, None]
+        grad_rows = cube_gather(after(live.astype(BF16), projected), "dp")
+        if m == 0:
+            near_units, near_downs = (
+                lax.dynamic_slice_in_dim(w, core * inner_half, inner_half, 0)
+                for w in (inner_weight, down_weight)
+            )
         memory_here = lax.dynamic_slice_in_dim(memory[m, 0], span * heads_here, heads_here, 0)
         norm_here = lax.dynamic_slice_in_dim(
             normalizer[m, 0], span * heads_here, heads_here, 0
@@ -665,6 +901,13 @@
         mixed_heads, dot_read, lse, new_memory, new_norm = attend(
             length, gate_here, projected, memory_here, norm_here
         )
+        if m == 0:
+            inner_near = lax.all_gather(
+                after(near_units, all_rows[-1]),
+                "seq",
+                axis=0,
+                tiled=True,
+            )
         new_memories.append(new_memory)
         new_norms.append(new_norm.reshape(heads_here, head_dim))
         mixed = lax.all_to_all(
@@ -684,20 +927,86 @@
         normed_two = after_attn * scale_two
         hidden_two = (normed_two * gain_two).astype(BF16)
         rows_all = cube_gather(hidden_two, "dp")
-        mlp_part, grad_two_part, hidden, grad_gates, grad_ups = mlp(
-            rows_all, grad_rows[m], inner_near, inner_far, down_near, down_far
-        )
-        grad_two = cube_scatter(grad_two_part, "dp")
-        mlp_out = cube_scatter(mlp_part, "dp")
-        outputs.append((after_attn + mlp_out).astype(BF16))
+        saved.append(
+            dict(
+                hidden_one=hidden_one,
+                projected=projected,
+                live=live,
+                grads=grad_rows,
+                memory=memory_here,
+                norm=norm_here,
+                length=length,
+                dot_read=dot_read,
+                lse=lse,
+                mixed_heads=mixed_heads,
+                mixed_near=mixed_near,
+                mixed_far=mixed_far,
+                after_attn=after_attn,
+                scale_two=scale_two,
+                normed_two=normed_two,
+                rows=rows_all,
+            )
+        )
+
+    down_near = lax.all_gather(
+        after(near_downs, inner_near, *[s[n] for s in saved for n in ("rows", "grads")]),
+        "seq",
+        axis=0,
+        tiled=True,
+    )
+    inner_far, down_far = swap(inner_near), swap(down_near)
+
+    inner, down = (inner_near, inner_far), (down_near, down_far)
+    last = None
+    for s in saved:
+        halves = []
+        for half in range(2):
+            halves.append(unit_pass(after(s["rows"], last), s["grads"], inner[half], down[half]))
+            last = halves[-1][0]
+        s["hidden"], s["grad_gates"], s["grad_ups"] = zip(*halves)
+
+    def half_grads(left, right, half, earlier, extra=None):
+        pairs = [(s[left][half], s[right]) for s in saved]
+        pairs[0] = (after(pairs[0][0], earlier), pairs[0][1])
+        return weight_pass(pairs, extra)
+
+    def spread(values):
+        return lax.psum_scatter(values, "seq", scatter_dimension=0, tiled=True)
+
+    def rows_out(s, *earlier):
+        gates = (after(s["grad_gates"][0], *earlier), s["grad_gates"][1])
+        s["mlp_part"], s["grad_two_part"] = row_pass(
+            s["hidden"], gates, s["grad_ups"], inner, down
+        )
+        return s["grad_two_part"]
+
+    down_far_sum = half_grads("hidden", "grads", 1, last)
+    gate_far_sum = half_grads("grad_gates", "rows", 1, down_far_sum)
+    down_sum = half_grads("hidden", "grads", 0, gate_far_sum, swap(down_far_sum))
+    down_mine = spread(down_sum)
+    last = rows_out(saved[0], down_sum)
+    up_far_sum = half_grads("grad_ups", "rows", 1, last)
+    gate_sum = half_grads("grad_gates", "rows", 0, up_far_sum, swap(gate_far_sum))
+    gate_mine = spread(gate_sum)
+    last = gate_sum
+    for s in saved[1:]:
+        last = rows_out(s, last, down_mine)
+    up_sum = half_grads("grad_ups", "rows", 0, last, swap(up_far_sum))
+    up_mine = spread(up_sum)
+    last = up_sum
+
+    def rows_back(s, pins):
+        grad_two = cube_scatter(s["grad_two_part"], "dp", pins)
         grad_scaled = grad_two * gain_two
-        grad_after = live_cots[m] + scale_two * (
+        normed_two = s["normed_two"]
+        s["grad_after"] = s["live"] + s["scale_two"] * (
             grad_scaled
             - normed_two * jnp.mean(grad_scaled * normed_two, axis=-1, keepdims=True)
         )
-        grad_branch = grad_after.astype(BF16)
-        grad_mixed_near = nn(grad_branch, out_near).astype(BF16)
-        grad_mixed_far = nn(grad_branch, out_far).astype(BF16)
+        s["grad_branch"] = s["grad_after"].astype(BF16)
+        s["gains_two"] = jnp.sum(grad_two * normed_two, axis=0)
+        grad_mixed_near = nn(s["grad_branch"], out_near).astype(BF16)
+        grad_mixed_far = nn(s["grad_branch"], out_far).astype(BF16)
         grad_mixed = jnp.concatenate(
             [
                 jnp.where(low_first, grad_mixed_near, grad_mixed_far),
@@ -705,103 +1014,112 @@
             ],
             axis=1,
         )
-        grad_heads = lax.all_to_all(
+        return lax.all_to_all(
             jnp.swapaxes(grad_mixed.reshape(span_rows, span_count, block_rows), 0, 1),
             ("rep", "seq"),
             0,
             0,
             tiled=True,
         ).reshape(total, block_rows)
-        grad_projected, gate_sums = attend_back(
-            length, gate_here, projected, memory_here, norm_here, dot_read, lse, grad_heads
-        )
-        grad_near = lax.dynamic_slice_in_dim(grad_projected, core * half_total, half_total, 0)
-        grad_far = lax.dynamic_slice_in_dim(
-            grad_projected, (1 - core) * half_total, half_total, 0
-        )
-        grad_one_far = swap(nn(grad_far, head_weight).astype(BF16))
-        grad_one_near = (nn(grad_near, head_weight) + grad_one_far.astype(F32)).astype(BF16)
-        grad_one = line_scatter(grad_one_near, "seq")
+
+    def heads_back(s, m, grad_heads):
+        s["grad_projected"], gate_sums = attend_back(
+            s["length"],
+            gate_here,
+            s["projected"],
+            s["memory"],
+            s["norm"],
+            s["dot_read"],
+            s["lse"],
+            grad_heads,
+        )
+        s["gate"] = jnp.sum(gate_sums, axis=(1, 2))
+        part_far, gains_far = project_back(
+            1 - core, s["grad_projected"], head_weight, all_rows[m]
+        )
+        part_near, gains_near = project_back(
+            core, after(s["grad_projected"], part_far), head_weight, all_rows[m]
+        )
+        s["gains_one"] = (gains_far + gains_near)[0]
+        return part_near, add_low(part_near, swap(part_far))
+
+    def tokens_back(s, m, grad_one):
         rows_float = own_rows[m].astype(F32)
         scale_one = lax.rsqrt(jnp.mean(rows_float * rows_float, axis=-1, keepdims=True) + EPSILON)
         normed_one = rows_float * scale_one
-        grad_scaled_one = grad_one * gain_one
-        grad_tokens = (
-            grad_after
+        grad_scaled = grad_one * gain_one
+        return (
+            s["grad_after"]
             + scale_one
             * (
-                grad_scaled_one
-                - normed_one * jnp.mean(grad_scaled_one * normed_one, axis=-1, keepdims=True)
+                grad_scaled
+                - normed_one * jnp.mean(grad_scaled * normed_one, axis=-1, keepdims=True)
             )
         ).astype(BF16)
-        saved.append(
-            dict(
-                grad_tokens=grad_tokens,
-                gains_one=jnp.sum(grad_one * normed_one, axis=0),
-                gains_two=jnp.sum(grad_two * normed_two, axis=0),
-                gate=jnp.sum(gate_sums, axis=(1, 2)),
-                qkv=tn(grad_near, hidden_near) + tn(grad_far, hidden_far),
-                out_near=tn(grad_branch, mixed_near),
-                out_far=tn(grad_branch, mixed_far),
-                rows=rows_all,
-                grads=grad_rows[m],
-                hidden=hidden,
-                grad_gates=grad_gates,
-                grad_ups=grad_ups,
-            )
-        )
+
+    heads_grads = [rows_back(s, ()) for s in saved]
+    earlier = (last, gate_mine)
+    sums = []
+    for m, s in enumerate(saved):
+        last, part = heads_back(s, m, after(heads_grads[m], *earlier))
+        sums.append(part)
+        earlier = (last,)
+    grad_ones = line_scatter(
+        jnp.concatenate(
+            [p.reshape(seq_count, span_rows, width) for p in sums], axis=1
+        ).reshape(-1, width),
+        "seq",
+    )
+    grad_tokens = [
+        tokens_back(s, m, grad_ones[m * span_rows : (m + 1) * span_rows])
+        for m, s in enumerate(saved)
+    ]
+    out_far_sum = weight_pass(
+        [(after(s["grad_branch"], last, up_mine), s["mixed_far"]) for s in saved]
+    )
+    out_near_sum = weight_pass(
+        [(after(s["grad_branch"], out_far_sum), s["mixed_near"]) for s in saved]
+    )
+    qkv_low = weight_pass(
+        [(after(s["grad_projected"], out_near_sum), s["hidden_one"]) for s in saved]
+    ).reshape(3, block_rows, width)
+    for m, s in enumerate(saved):
+        mlp_out = cube_scatter(s["mlp_part"], "dp")
+        outputs.append((s["after_attn"] + mlp_out).astype(BF16))
 
     def joined(name):
         return functools.reduce(jnp.add, [s[name] for s in saved])
 
-    units = inner_near.shape[0]
-
-    def unit_grads(left, right):
-        def part(start):
-            return functools.reduce(
-                jnp.add, [tn(s[left][:, start : start + units], s[right]) for s in saved]
-            )
-
-        far_part = swap(part(units).astype(BF16))
-        near_part = (part(0) + far_part.astype(F32)).astype(BF16)
-        mine = line_scatter(near_part, "seq").astype(BF16)
+    def both_cores(mine, axis):
         other = swap(mine)
-        return jnp.concatenate(
-            [jnp.where(core == 0, mine, other), jnp.where(core == 0, other, mine)], axis=0
-        ).astype(F32)
-
-    grad_down = unit_grads("hidden", "grads")
-    grad_inner = jnp.concatenate(
-        [unit_grads("grad_gates", "rows"), unit_grads("grad_ups", "rows")], axis=1
-    )
-
-    out_other = swap(joined("out_far").astype(BF16))
-    out_mine = (joined("out_near") + out_other.astype(F32)).astype(BF16)
-    shard_out = out_weight.shape[0]
-    out_mine = out_mine.reshape(dp_count, seq_count * shard_out, half_width)
+        size = mine.shape[axis]
+        shape = list(mine.shape)
+        shape[axis] = 2 * size
+        whole = jnp.zeros(shape, F32)
+        whole = lax.dynamic_update_slice_in_dim(whole, mine.astype(F32), core * size, axis)
+        return lax.dynamic_update_slice_in_dim(
+            whole, other.astype(F32), (1 - core) * size, axis
+        )
+
+    grad_down = both_cores(down_mine, 0)
+    grad_inner = both_cores(jnp.concatenate([gate_mine, up_mine], axis=1), 0)
+
+    out_mine = add_low(out_near_sum, swap(out_far_sum)).reshape(
+        dp_count, column_out, half_width
+    )
     pieces = []
-    side_rows = seq_count * shard_out // 2
     for side in range(2):
         for k in orders[side]:
             owned = lax.dynamic_index_in_dim(out_mine, column ^ k, 0, keepdims=False)
-            pieces.append(owned[side * side_rows : (side + 1) * side_rows])
+            pieces.append(owned[side * column_out // 2 : (side + 1) * column_out // 2])
     out_column = cube_scatter(jnp.concatenate(pieces, axis=0), "dp").astype(BF16)
-    out_mine = line_scatter(out_column, "seq").astype(BF16)
-    out_other = swap(out_mine)
-    grad_out = jnp.concatenate(
-        [jnp.where(core == 0, out_mine, out_other), jnp.where(core == 0, out_other, out_mine)],
-        axis=1,
-    ).astype(F32)
-
-    qkv_low = joined("qkv").astype(BF16).reshape(3, block_rows, width)
+    grad_out = both_cores(line_scatter(out_column, "seq").astype(BF16), 1)
+
     qkv_low = jnp.concatenate([qkv_low, jnp.zeros((1, block_rows, width), BF16)], axis=0)
-    which = [
-        [3] * (span_count * dp_count) for _ in range(1)
-    ][0]
+    which = [3] * (span_count * dp_count)
     for part in range(3):
         for owner in range(span_count):
-            col = (part * span_count + owner) // per_column
-            which[owner * dp_count + col] = part
+            which[owner * dp_count + (part * span_count + owner) // per_column] = part
     pieces = []
     for side in range(2):
         for k in orders[side]:
@@ -828,18 +1146,19 @@
         jnp.zeros((head_count,), F32), gate_terms, span * heads_here, 0
     )
     small = jnp.concatenate([joined("gains_one"), joined("gains_two"), gate_row])
-    small = jnp.sum(lax.all_gather(small, ALL, axis=0), axis=0)
-    shard_gain = norm_gains.shape[1]
+    small = jnp.pad(small, (0, 8 * width - small.shape[0])).reshape(8, width)
+    small = lax.all_gather(after(small, up_mine), ALL, axis=0, tiled=True)
+    small = jnp.sum(small.reshape(devices, 8 * width)[:, : 3 * width], axis=0)
     gain_at = (column * seq_count + place) * shard_gain
     grad_gains = lax.dynamic_slice_in_dim(
         small[: 2 * width].reshape(2, width), gain_at, shard_gain, 1
     )
-    grad_gate = small[2 * width :]
+    grad_gate = small[2 * width : 2 * width + head_count]
     return (
         jnp.stack(outputs)[:, None],
         jnp.stack(new_memories)[:, None],
         jnp.stack(new_norms)[:, None],
-        jnp.stack([s["grad_tokens"] for s in saved])[:, None],
+        jnp.stack(grad_tokens)[:, None],
         grad_qkv,
         grad_out,
         grad_gains,

time: 1960 us -> 1480 us (0.76)
  waiting for transfers between devices: 835 us -> 480 us
  matrix products: 185 us -> 30.6 us
  Pallas kernels: 307 us -> 450 us
  starting transfers between devices: 266 us -> 209 us
  blocking collectives: 46.9 us -> 0 us
  local copies, waits for them, and re-layouts: 133 us -> 165 us
  other arithmetic: 135 us -> 106 us
    ppermute x6 -> x3, waiting for transfers between devices: 217 us -> 35.3 us  [line_gather(): lax.ppermute(rising, axis, [(a, a + 1) for a in range(count - 1) if a >=...]
    pallas_call x2 -> x20, Pallas kernels: 200 us -> 362 us  [the longest x9 125 us: weight_pass(): pl.pallas_call(functools.partial(weight_kernel, len(pairs)), grid=(size /...]
    dot_general x20 -> x0, matrix products: 137 us -> none  [tn(): lax.dot_general(left_side, right_side, (((0,), (0,)), ((), ())), preferre...]
    unnamed x5 -> x8, waiting for transfers between devices: 121 us -> 0.13 us
    all_gather x3 -> x5, waiting for transfers between devices: 0.01 us -> 112 us  [the longest x1 80.3 us: shards(): lax.all_gather(after(near_downs, inner_near, *[s[n] for s in saved for n...]
    ppermute x18 -> x6, waiting for transfers between devices: 116 us -> 41.3 us  [line_scatter(): lax.ppermute(down.astype(BF16), axis, [(a, a - 1) for a in range(count) i...]
    ppermute x18 -> x6, waiting for transfers between devices: 131 us -> 82.4 us  [line_scatter(): lax.ppermute(up.astype(BF16), axis, [(a, a + 1) for a in range(count) if...]
    all_gather x1 -> x0, blocking collectives: 46.9 us -> none  [shards(): lax.all_gather(norm_gains, ('dp', 'seq'), axis=1, tiled=True).astype(F32)]
  transfers between devices with their start and end apart: 132 -> 100, of which waited for: 54 -> 32; matrix products, arithmetic and copies ran while one was open for 19% -> 17% of each run, Pallas kernels for 6% -> 25%
where the time goes in v2:
time: 1480 us; the launch traced here: 1470 us
  waiting for transfers between devices  480 us (32%)
  Pallas kernels  450 us (30%)
  starting transfers between devices  209 us (14%)
  local copies, waits for them, and re-layouts  165 us (11%)
  other arithmetic  106 us (7%)
  matrix products  30.6 us (2%)
  between operations  30.6 us (2%)
    pallas_call x9, Pallas kernels, weight_pass(): pl.pallas_call(functools.partial(weight_kernel, len(pairs)), grid=(size /...  125 us
    ppermute x24, waiting for transfers between devices, cube_scatter(): got = lax.ppermute(held[keep:].astype(BF16), axis, pairs)  88.5 us
    unnamed x264, local copies, waits for them, and re-layouts  86.2 us
    ppermute x6, waiting for transfers between devices, line_scatter(): lax.ppermute(up.astype(BF16), axis, [(a, a + 1) for a in range(count) if...  82.4 us
    all_gather x1, waiting for transfers between devices, shards(): lax.all_gather(after(near_downs, inner_near, *[s[n] for s in saved for n...  80.3 us
    pallas_call x4, Pallas kernels, unit_pass(): pl.pallas_call(unit_kernel, grid=(units // tile,), in_specs=[resident, re...  78 us
    ppermute x30, waiting for transfers between devices, cube_gather(): lax.ppermute(v, axis, pairs)  76.3 us
    pallas_call x2, Pallas kernels, row_pass(): pl.pallas_call(row_kernel, grid=(tiles,), in_specs=[resident] * 6 + [low,...  70.2 us
  transfers between devices with their start and end apart: 100, of which 32 were waited for; matrix products, arithmetic and copies ran while one was open for 17% of the time, Pallas kernels for 25%

profile of v2, /device:TPU:17, one launch (start us, length us, event | category | flops | bytes accessed | tf_op | source)
XLA Modules:
  0.0 1471.3 jit_solution(8316573107016396372)
XLA Ops:
  12.0 59.7 %gather_heads.1 = (bf16[768,2048]{1,0:T(8,128)(2,1)S(1)}, f32[16,8,128]{2,1,0:T(8,128)S(1)}) custom-call(bf16[384,2048]{1,0:T(8,128)(2,1)S(1)} %copy-done.9, f32[8,128]{1,0:T(8,128)S(1)} %pad_convert_fusion.gain_ref), custom_call_target="tpu_custom_call" | custom-call | bytes 33554432 | tf_op jit(solution)/shard_map/gather_heads/pallas_call | solution.py:745
  73.4 31.6 %all-gather.15.cloned.1.call-done = bf16[1,1,2048,2048]{3,2,1,0:T(8,128)(2,1)} async-done(((bf16[1,1,256,2048]{3,2,1,0:T(8,128)(2,1)}), bf16[1,1,2048,2048]{3,2,1,0:T(8,128)(2,1)}) %all-gather.15.cloned.1.call-update) | async-done | bytes 8388624 | tf_op jit(solution)/shard_map/all_gather | solution.py:836
  133.0 17.0 %collective-permute-done.2 = bf16[128,1024]{1,0:T(8,128)(2,1)} collective-permute-done((bf16[128,1024]{1,0:T(8,128)(2,1)}, bf16[128,1024]{1,0:T(8,128)(2,1)}, u32[]{:S(2)}, u32[]{:S(2)}) %collective-permute-start.2) | collective-permute-done | bytes 262176 | tf_op jit(solution)/shard_map/ppermute | solution.py:519
  156.2 18.3 %collective-permute-done.4 = bf16[128,1024]{1,0:T(8,128)(2,1)S(1)} collective-permute-done((bf16[128,1024]{1,0:T(8,128)(2,1)}, bf16[128,1024]{1,0:T(8,128)(2,1)S(1)}, u32[]{:S(2)}, u32[]{:S(2)}) %collective-permute-start.4) | collective-permute-done | bytes 262176 | tf_op jit(solution)/shard_map/ppermute | solution.py:519
  256.2 12.5 attend.2
  296.5 11.7 project.3
  320.3 17.0 %attend.3 = (bf16[2048,256]{1,0:T(8,128)(2,1)S(1)}, f32[2048,256]{1,0:T(8,128)S(1)}, f32[2,1,2048]{2,1,0:T(1,128)S(1)}, f32[2,128,128]{2,1,0:T(8,128)S(1)}, f32[2,1,128]{2,1,0:T(1,128)S(1)}) custom-call(s32[1]{0:T(128)} %bitcast.17.length_ref, f32[2]{0:T(128)S(1)} %copy-done.19, bf16[2048,768]{1,0:T(8,128)(2,1)S(1)} %get-tuple-element.88.q_ref.k_ref.v_ref, ...), custom_call_target="tpu_custom_call" | custom-call | flops 4294967296 | bytes 6291456 | tf_op jit(solution)/shard_map/attend/pallas_call | solution.py:156
  372.9 28.7 %all-to-all-done.1 = bf16[8,256,256]{2,1,0:T(8,128)(2,1)} async-done(((bf16[8,256,256]{2,1,0:T(8,128)(2,1)}), bf16[8,256,256]{2,1,0:T(8,128)(2,1)}, u32[]{:S(2)}, u32[]{:S(2)}) %all-to-all-start.1) | async-done | bytes 1048608 | tf_op jit(solution)/shard_map/all_to_all | solution.py:913
  498.4 80.3 %all-gather.11.cloned.1.call-done.down_ref.refs_10_ = bf16[1024,2048]{1,0:T(8,128)(2,1)} async-done(((bf16[256,2048]{1,0:T(8,128)(2,1)}), bf16[1024,2048]{1,0:T(8,128)(2,1)}) %all-gather.11.cloned.1.call-update) | async-done | bytes 4194320 | tf_op jit(solution)/shard_map/all_gather | solution.py:951
  579.4 19.4 %unit_pass.4 = (bf16[1024,1024]{1,0:T(8,128)(2,1)}, bf16[1024,1024]{1,0:T(8,128)(2,1)}, bf16[1024,1024]{1,0:T(8,128)(2,1)}) custom-call(bf16[1024,2048]{1,0:T(8,128)(2,1)} %constant_dynamic-update-slice_fusion.8.rows_ref.refs_1_, bf16[1024,2048]{1,0:T(8,128)(2,1)} %constant_dynamic-update-slice_fusion.16.grad_ref.refs_1_, ...), custom_call_target="tpu_custom_call" | custom-call | flops 12884901888 | bytes 27262976 | tf_op jit(solution)/shard_map/unit_pass/pallas_call | solution.py:348
  600.8 19.6 %unit_pass.5 = (bf16[1024,1024]{1,0:T(8,128)(2,1)}, bf16[1024,1024]{1,0:T(8,128)(2,1)}, bf16[1024,1024]{1,0:T(8,128)(2,1)}) custom-call(bf16[1024,2048]{1,0:T(8,128)(2,1)} %constant_dynamic-update-slice_fusion.8.rows_ref.refs_1_, bf16[1024,2048]{1,0:T(8,128)(2,1)} %constant_dynamic-update-slice_fusion.16.grad_ref.refs_1_, ...), custom_call_target="tpu_custom_call" | custom-call | flops 12884901888 | bytes 27262976 | tf_op jit(solution)/shard_map/unit_pass/pallas_call | solution.py:348
  620.4 19.5 %unit_pass.6 = (bf16[1024,1024]{1,0:T(8,128)(2,1)}, bf16[1024,1024]{1,0:T(8,128)(2,1)}, bf16[1024,1024]{1,0:T(8,128)(2,1)}) custom-call(bf16[1024,2048]{1,0:T(8,128)(2,1)} %copy-done.84, bf16[1024,2048]{1,0:T(8,128)(2,1)} %constant_dynamic-update-slice_fusion.32.grad_ref.refs_3_, bf16[1024,4096]{1,0:T(8,128)(2,1)} %all-gather.9.cloned.1.call-done.inner_ref.refs_6_.refs_8_, ...), custom_call_target="tpu_custom_call" | custom-call | flops 12884901888 | bytes 27262976 | tf_op jit(solution)/shard_map/unit_pass/pallas_call | solution.py:348
  639.8 19.5 %unit_pass.7 = (bf16[1024,1024]{1,0:T(8,128)(2,1)}, bf16[1024,1024]{1,0:T(8,128)(2,1)}, bf16[1024,1024]{1,0:T(8,128)(2,1)}) custom-call(bf16[1024,2048]{1,0:T(8,128)(2,1)} %copy-done.84, bf16[1024,2048]{1,0:T(8,128)(2,1)} %constant_dynamic-update-slice_fusion.32.grad_ref.refs_3_, bf16[1024,4096]{1,0:T(8,128)(2,1)} %collective-permute-done.37.inner_ref.refs_7_.refs_9_, ...), custom_call_target="tpu_custom_call" | custom-call | flops 12884901888 | bytes 27262976 | tf_op jit(solution)/shard_map/unit_pass/pallas_call | solution.py:348
  659.3 14.5 weight_pass.9
  673.9 14.3 weight_pass.10
  690.2 14.8 %weight_pass.11 = bf16[1024,2048]{1,0:T(8,128)(2,1)} custom-call(bf16[1024,1024]{1,0:T(8,128)(2,1)} %get-tuple-element.104.refs_0_, bf16[1024,2048]{1,0:T(8,128)(2,1)} %constant_dynamic-update-slice_fusion.16.grad_ref.refs_1_, bf16[1024,1024]{1,0:T(8,128)(2,1)} %get-tuple-element.98.refs_2_.refs_0_, ...), custom_call_target="tpu_custom_call" | custom-call | flops 8589934592 | bytes 20971520 | tf_op jit(solution)/shard_map/weight_pass/pallas_call | solution.py:436
  705.6 35.0 %row_pass.2 = (bf16[1024,2048]{1,0:T(8,128)(2,1)}, bf16[1024,2048]{1,0:T(8,128)(2,1)}) custom-call(bf16[1024,1024]{1,0:T(8,128)(2,1)} %get-tuple-element.104.refs_0_, bf16[1024,1024]{1,0:T(8,128)(2,1)} %get-tuple-element.101.refs_0_.refs_1_, bf16[1024,1024]{1,0:T(8,128)(2,1)} %get-tuple-element.113.refs_2_.refs_0_, ...), custom_call_target="tpu_custom_call" | custom-call | flops 25769803776 | bytes 46137344 | tf_op jit(solution)/shard_map/row_pass/pallas_call | solution.py:393
  746.1 14.4 weight_pass.12
  763.3 14.9 %weight_pass.13 = bf16[1024,2048]{1,0:T(8,128)(2,1)} custom-call(bf16[1024,1024]{1,0:T(8,128)(2,1)} %get-tuple-element.113.refs_2_.refs_0_, bf16[1024,2048]{1,0:T(8,128)(2,1)} %constant_dynamic-update-slice_fusion.8.rows_ref.refs_1_, bf16[1024,1024]{1,0:T(8,128)(2,1)} %get-tuple-element.114.refs_2_, bf16[1024,2048]{1,0:T(8,128)(2,1)} %copy-done.84, ...), custom_call_target="tpu_custom_call" | custom-call | flops 8589934592 | bytes 20971520 | tf_op jit(solution)/shard_map/weight_pass/pallas_call | solution.py:436
  805.5 35.2 %row_pass.3 = (bf16[1024,2048]{1,0:T(8,128)(2,1)}, bf16[1024,2048]{1,0:T(8,128)(2,1)}) custom-call(bf16[1024,1024]{1,0:T(8,128)(2,1)} %get-tuple-element.98.refs_2_.refs_0_, bf16[1024,1024]{1,0:T(8,128)(2,1)} %get-tuple-element.100.refs_2_.refs_1_, bf16[1024,1024]{1,0:T(8,128)(2,1)} %get-tuple-element.114.refs_2_, ...), custom_call_target="tpu_custom_call" | custom-call | flops 25769803776 | bytes 46137344 | tf_op jit(solution)/shard_map/row_pass/pallas_call | solution.py:393
  848.3 17.1 %collective-permute-done.55 = bf16[256,2048]{1,0:T(8,128)(2,1)S(1)} collective-permute-done((bf16[256,2048]{1,0:T(8,128)(2,1)S(1)}, bf16[256,2048]{1,0:T(8,128)(2,1)S(1)}, u32[]{:S(2)}, u32[]{:S(2)}) %collective-permute-start.55) | collective-permute-done | bytes 1048608 | tf_op jit(solution)/shard_map/ppermute | solution.py:590
  868.8 19.1 %collective-permute-done.45 = bf16[256,2048]{1,0:T(8,128)(2,1)S(1)} collective-permute-done((bf16[256,2048]{1,0:T(8,128)(2,1)S(1)}, bf16[256,2048]{1,0:T(8,128)(2,1)S(1)}, u32[]{:S(2)}, u32[]{:S(2)}) %collective-permute-start.45) | collective-permute-done | bytes 1048608 | tf_op jit(solution)/shard_map/ppermute | solution.py:590
  942.2 15.6 %all-to-all-done.2 = bf16[8,256,256]{2,1,0:T(8,128)(2,1)} async-done(((bf16[8,256,256]{2,1,0:T(8,128)(2,1)}), bf16[8,256,256]{2,1,0:T(8,128)(2,1)}, u32[]{:S(2)}, u32[]{:S(2)}) %all-to-all-start.2) | async-done | bytes 1048608 | tf_op jit(solution)/shard_map/all_to_all | solution.py:1017
  964.1 14.8 %weight_pass.14 = bf16[1024,2048]{1,0:T(8,128)(2,1)} custom-call(bf16[1024,1024]{1,0:T(8,128)(2,1)} %get-tuple-element.124.refs_4_.refs_0_, bf16[1024,2048]{1,0:T(8,128)(2,1)} %constant_dynamic-update-slice_fusion.8.rows_ref.refs_1_, bf16[1024,1024]{1,0:T(8,128)(2,1)} %get-tuple-element.115.refs_4_.refs_2_, bf16[1024,2048]{1,0:T(8,128)(2,1)} %copy-done.84, ...), custom_call_target="tpu_custom_call" | custom-call | flops 8589934592 | bytes 20971520 | tf_op jit(solution)/shard_map/weight_pass/pallas_call | solution.py:436
  983.7 15.0 %attend_back.2 = (bf16[2048,768]{1,0:T(8,128)(2,1)S(1)}, f32[2,1,128]{2,1,0:T(1,128)S(1)}) custom-call(s32[1]{0:T(128)} %bitcast.1.length_ref, f32[2]{0:T(128)S(1)} %copy-done.20, bf16[2048,768]{1,0:T(8,128)(2,1)S(1)} %copy-done.23, bf16[2048,768]{1,0:T(8,128)(2,1)S(1)} %copy-done.23, bf16[2048,768]{1,0:T(8,128)(2,1)S(1)} %copy-done.23, ...), custom_call_target="tpu_custom_call" | custom-call | flops 10737418240 | bytes 10485760 | tf_op jit(solution)/shard_map/attend_back/pallas_call | solution.py:286
  1018.5 20.5 %attend_back.3 = (bf16[2048,768]{1,0:T(8,128)(2,1)S(1)}, f32[2,1,128]{2,1,0:T(1,128)S(1)}) custom-call(s32[1]{0:T(128)} %bitcast.17.length_ref, f32[2]{0:T(128)S(1)} %copy-done.21, bf16[2048,768]{1,0:T(8,128)(2,1)S(1)} %copy-done.25, bf16[2048,768]{1,0:T(8,128)(2,1)S(1)} %copy-done.25, bf16[2048,768]{1,0:T(8,128)(2,1)S(1)} %copy-done.25, ...), custom_call_target="tpu_custom_call" | custom-call | flops 10737418240 | bytes 10485760 | tf_op jit(solution)/shard_map/attend_back/pallas_call | solution.py:286
  1129.9 21.0 %weight_pass.17 = bf16[768,2048]{1,0:T(8,128)(2,1)} custom-call(bf16[2048,768]{1,0:T(8,128)(2,1)} %copy-done.4, bf16[2048,2048]{1,0:T(8,128)(2,1)} %copy-done.26, bf16[2048,768]{1,0:T(8,128)(2,1)} %copy-done.5, bf16[2048,2048]{1,0:T(8,128)(2,1)} %copy-done.27), custom_call_target="tpu_custom_call" | custom-call | flops 12884901888 | bytes 26214400 | tf_op jit(solution)/shard_map/weight_pass/pallas_call | solution.py:436
  1156.1 11.9 collective-permute-start.68
  1225.8 33.7 %collective-permute-done.61 = bf16[512,2048]{1,0:T(8,128)(2,1)S(1)} collective-permute-done((bf16[512,2048]{1,0:T(8,128)(2,1)S(1)}, bf16[512,2048]{1,0:T(8,128)(2,1)S(1)}, u32[]{:S(2)}, u32[]{:S(2)}) %collective-permute-start.61) | collective-permute-done | bytes 2097184 | tf_op jit(solution)/shard_map/ppermute | solution.py:545
  1290.0 39.5 %collective-permute-start.73 = (bf16[384,2048]{1,0:T(8,128)(2,1)S(1)}, bf16[384,2048]{1,0:T(8,128)(2,1)S(1)}, u32[]{:S(2)}, u32[]{:S(2)}) collective-permute-start(bf16[384,2048]{1,0:T(8,128)(2,1)S(1)} %slice.519), channel_id=1, source_target_pairs={{0,16},{16,0},{1,17},{17,1},{2,18},{18,2},{3,19},{19,3},{4,20},{20... | collective-permute-start | bytes 4718600 | tf_op jit(solution)/shard_map/ppermute | solution.py:495
  1342.5 48.6 %collective-permute-done.80 = bf16[128,1024]{1,0:T(8,128)(2,1)S(1)} collective-permute-done((bf16[128,1024]{1,0:T(8,128)(2,1)S(1)}, bf16[128,1024]{1,0:T(8,128)(2,1)S(1)}, u32[]{:S(2)}, u32[]{:S(2)}) %collective-permute-start.80) | collective-permute-done | bytes 262176 | tf_op jit(solution)/shard_map/ppermute | solution.py:545
  1404.5 41.0 %collective-permute-done.84 = bf16[128,1024]{1,0:T(8,128)(2,1)S(1)} collective-permute-done((bf16[128,1024]{1,0:T(8,128)(2,1)S(1)}, bf16[128,1024]{1,0:T(8,128)(2,1)S(1)}, u32[]{:S(2)}, u32[]{:S(2)}) %collective-permute-start.84) | collective-permute-done | bytes 262176 | tf_op jit(solution)/shard_map/ppermute | solution.py:548
  (628 shorter events, 645.0 us)
Async XLA Ops:
  7.2 97.8 %all-gather.15.cloned.1.call-start = ((), (), s32[]{:S(2)}) async-start(), calls=%async_computation.14 | async-start | bytes 9437184 | tf_op jit(solution)/shard_map/all_gather | solution.py:836
  10.5 280.3 %all-gather.7.cloned.1.call-start = ((), (), s32[]{:S(2)}) async-start(), calls=%async_computation.7 | async-start | bytes 9437184 | tf_op jit(solution)/shard_map/all_gather | solution.py:836
  247.1 156.2 %collective-permute-start.12 = (bf16[2048,1024]{1,0:T(8,128)(2,1)}, bf16[2048,1024]{1,0:T(8,128)(2,1)}, u32[]{:S(2)}, u32[]{:S(2)}) collective-permute-start(bf16[2048,1024]{1,0:T(8,128)(2,1)} %dynamic-slice_dynamic-update-slice_fusion), channel_id=1, source_target_pairs={{0,16},{16,0},{1,17},{17,1},{2,18},{18,2},{3,19},{19,3},{4,20},{20... | collective-permute-start | bytes 12582920 | tf_op jit(solution)/shard_map/ppermute | solution.py:495
  272.2 70.7 %all-to-all-start = ((bf16[8,256,256]{2,1,0:T(8,128)(2,1)}), bf16[8,256,256]{2,1,0:T(8,128)(2,1)}, u32[]{:S(2)}, u32[]{:S(2)}) async-start(bf16[8,256,256]{2,1,0:T(8,128)(2,1)} %bitcast.165), calls=%async_computation | async-start | bytes 2097152 | tf_op jit(solution)/shard_map/all_to_all | solution.py:913
  282.3 214.0 %all-gather.9.cloned.1.call-start = ((), (), s32[]{:S(2)}) async-start(), calls=%async_computation.8 | async-start | bytes 10485760 | tf_op jit(solution)/shard_map/all_gather | solution.py:905
  282.5 66.9 %collective-permute-start.24 = (bf16[128,2048]{1,0:T(8,128)(2,1)}, bf16[128,2048]{1,0:T(8,128)(2,1)}, u32[]{:S(2)}, u32[]{:S(2)}) collective-permute-start(bf16[128,2048]{1,0:T(8,128)(2,1)} %collective-permute-done.23), channel_id=1, source_target_pairs={{0,4},{4,0},{8,12},{12,8},{1,5},{5,1},{9,13},{13,9},{2,6},{6,2},{1... | collective-permute-start | bytes 1572872 | tf_op jit(solution)/shard_map/ppermute | solution.py:576
  342.9 58.7 %all-to-all-start.1 = ((bf16[8,256,256]{2,1,0:T(8,128)(2,1)}), bf16[8,256,256]{2,1,0:T(8,128)(2,1)}, u32[]{:S(2)}, u32[]{:S(2)}) async-start(bf16[8,256,256]{2,1,0:T(8,128)(2,1)} %bitcast.166), calls=%async_computation.1 | async-start | bytes 2097152 | tf_op jit(solution)/shard_map/all_to_all | solution.py:913
  349.4 229.3 %all-gather.11.cloned.1.call-start = ((), (), s32[]{:S(2)}) async-start(), calls=%async_computation.9 | async-start | bytes 5242880 | tf_op jit(solution)/shard_map/all_gather | solution.py:951
  357.9 67.8 %collective-permute-start.36 = (bf16[128,2048]{1,0:T(8,128)(2,1)}, bf16[128,2048]{1,0:T(8,128)(2,1)}, u32[]{:S(2)}, u32[]{:S(2)}) collective-permute-start(bf16[128,2048]{1,0:T(8,128)(2,1)} %collective-permute-done.35), channel_id=1, source_target_pairs={{0,4},{4,0},{8,12},{12,8},{1,5},{5,1},{9,13},{13,9},{2,6},{6,2},{1... | collective-permute-start | bytes 1572872 | tf_op jit(solution)/shard_map/ppermute | solution.py:576
  496.3 309.1 %reduce-scatter.4.cloned.1.call-start = ((), (), s32[]{:S(2)}) async-start(), calls=%async_computation.10 | async-start | bytes 5242880 | tf_op jit(solution)/shard_map/reduce_scatter | solution.py:974
  496.8 102.0 %collective-permute-start.37 = (bf16[1024,4096]{1,0:T(8,128)(2,1)}, bf16[1024,4096]{1,0:T(8,128)(2,1)}, u32[]{:S(2)}, u32[]{:S(2)}) collective-permute-start(bf16[1024,4096]{1,0:T(8,128)(2,1)} %all-gather.9.cloned.1.call-done.inner_ref.refs_6_.refs_8_), channel_id=1, source_target_pairs={{0,16},{16,0},{1,17},{17,1},{2,18},{18,2},{3,19},{19,3},{4,20},{20... | collective-permute-start | bytes 25165832 | tf_op jit(solution)/shard_map/ppermute | solution.py:495
  705.0 274.0 %reduce-scatter.6.cloned.1.call-start = ((), (), s32[]{:S(2)}) async-start(), calls=%async_computation.11 | async-start | bytes 5242880 | tf_op jit(solution)/shard_map/reduce_scatter | solution.py:974
  705.0 58.0 %collective-permute-start.44 = (bf16[1024,2048]{1,0:T(8,128)(2,1)}, bf16[1024,2048]{1,0:T(8,128)(2,1)}, u32[]{:S(2)}, u32[]{:S(2)}) collective-permute-start(bf16[1024,2048]{1,0:T(8,128)(2,1)} %weight_pass.10), channel_id=1, source_target_pairs={{0,16},{16,0},{1,17},{17,1},{2,18},{18,2},{3,19},{19,3},{4,20},{20... | collective-permute-start | bytes 12582920 | tf_op jit(solution)/shard_map/ppermute | solution.py:495
  762.1 202.0 %collective-permute-start.53 = (bf16[1024,2048]{1,0:T(8,128)(2,1)}, bf16[1024,2048]{1,0:T(8,128)(2,1)}, u32[]{:S(2)}, u32[]{:S(2)}) collective-permute-start(bf16[1024,2048]{1,0:T(8,128)(2,1)} %weight_pass.12), channel_id=1, source_target_pairs={{0,16},{16,0},{1,17},{17,1},{2,18},{18,2},{3,19},{19,3},{4,20},{20... | collective-permute-start | bytes 12582920 | tf_op jit(solution)/shard_map/ppermute | solution.py:495
  795.4 48.7 %collective-permute-start.50 = (bf16[128,2048]{1,0:T(8,128)(2,1)}, bf16[128,2048]{1,0:T(8,128)(2,1)}, u32[]{:S(2)}, u32[]{:S(2)}) collective-permute-start(bf16[128,2048]{1,0:T(8,128)(2,1)} %slice.619), channel_id=1, source_target_pairs={{0,8},{4,12},{8,0},{12,4},{1,9},{5,13},{9,1},{13,5},{2,10},{6,14},... | collective-permute-start | bytes 1572872 | tf_op jit(solution)/shard_map/ppermute | solution.py:590
  797.5 49.3 %collective-permute-start.52 = (bf16[128,2048]{1,0:T(8,128)(2,1)}, bf16[128,2048]{1,0:T(8,128)(2,1)}, u32[]{:S(2)}, u32[]{:S(2)}) collective-permute-start(bf16[128,2048]{1,0:T(8,128)(2,1)} %slice.618), channel_id=1, source_target_pairs={{0,4},{4,0},{8,12},{12,8},{1,5},{5,1},{9,13},{13,9},{2,6},{6,2},{1... | collective-permute-start | bytes 1572872 | tf_op jit(solution)/shard_map/ppermute | solution.py:590
  957.9 57.1 %all-to-all-start.3 = ((bf16[8,256,256]{2,1,0:T(8,128)(2,1)}), bf16[8,256,256]{2,1,0:T(8,128)(2,1)}, u32[]{:S(2)}, u32[]{:S(2)}) async-start(bf16[8,256,256]{2,1,0:T(8,128)(2,1)} %bitcast.190), calls=%async_computation.5 | async-start | bytes 2097152 | tf_op jit(solution)/shard_map/all_to_all | solution.py:1017
  964.1 149.3 %reduce-scatter.8.cloned.1.call-start = ((), (), s32[]{:S(2)}) async-start(), calls=%async_computation.12 | async-start | bytes 5242880 | tf_op jit(solution)/shard_map/reduce_scatter | solution.py:974
  978.9 471.6 %all-gather.13.cloned.1.call-start = ((), (), s32[]{:S(2)}) async-start(), calls=%async_computation.13 | async-start | bytes 2162688 | tf_op jit(solution)/shard_map/all_gather | solution.py:1150
  1006.7 78.5 %collective-permute-start.54 = (bf16[1024,2048]{1,0:T(8,128)(2,1)}, bf16[1024,2048]{1,0:T(8,128)(2,1)}, u32[]{:S(2)}, u32[]{:S(2)}) collective-permute-start(bf16[1024,2048]{1,0:T(8,128)(2,1)} %get-tuple-element.127), channel_id=1, source_target_pairs={{0,16},{16,0},{1,17},{17,1},{2,18},{18,2},{3,19},{19,3},{4,20},{20... | collective-permute-start | bytes 12582920 | tf_op jit(solution)/shard_map/ppermute | solution.py:495
  1111.4 90.9 %collective-permute-start.60 = (bf16[512,2048]{1,0:T(8,128)(2,1)}, bf16[512,2048]{1,0:T(8,128)(2,1)}, u32[]{:S(2)}, u32[]{:S(2)}) collective-permute-start(bf16[512,2048]{1,0:T(8,128)(2,1)} %get-tuple-element.200), channel_id=1, source_target_pairs={{0,1},{4,5},{8,9},{12,13},{16,17},{20,21},{24,25},{28,29}} | collective-permute-start | bytes 6291464 | tf_op jit(solution)/shard_map/ppermute | solution.py:545
  1121.6 94.1 %collective-permute-start.74 = (bf16[2048,1024]{1,0:T(8,128)(2,1)}, bf16[2048,1024]{1,0:T(8,128)(2,1)}, u32[]{:S(2)}, u32[]{:S(2)}) collective-permute-start(bf16[2048,1024]{1,0:T(8,128)(2,1)} %weight_pass.15), channel_id=1, source_target_pairs={{0,16},{16,0},{1,17},{17,1},{2,18},{18,2},{3,19},{19,3},{4,20},{20... | collective-permute-start | bytes 12582920 | tf_op jit(solution)/shard_map/ppermute | solution.py:495
  1176.1 48.3 %collective-permute-start.63 = (bf16[512,2048]{1,0:T(8,128)(2,1)}, bf16[512,2048]{1,0:T(8,128)(2,1)S(1)}, u32[]{:S(2)}, u32[]{:S(2)}) collective-permute-start(bf16[512,2048]{1,0:T(8,128)(2,1)} %get-tuple-element.201), channel_id=1, source_target_pairs={{3,2},{7,6},{11,10},{15,14},{19,18},{23,22},{27,26},{31,30}} | collective-permute-start | bytes 6291464 | tf_op jit(solution)/shard_map/ppermute | solution.py:548
  1191.6 206.8 %collective-permute-start.86 = (bf16[256,4096]{1,0:T(8,128)(2,1)}, bf16[256,4096]{1,0:T(8,128)(2,1)}, u32[]{:S(2)}, u32[]{:S(2)}) collective-permute-start(bf16[256,4096]{1,0:T(8,128)(2,1)} %constant_dynamic-update-slice_fusion.40), channel_id=1, source_target_pairs={{0,16},{16,0},{1,17},{17,1},{2,18},{18,2},{3,19},{19,3},{4,20},{20... | collective-permute-start | bytes 6291464 | tf_op jit(solution)/shard_map/ppermute | solution.py:495
  1221.7 48.7 %collective-permute-start.75 = (bf16[512,1024]{1,0:T(8,128)(2,1)S(1)}, bf16[512,1024]{1,0:T(8,128)(2,1)S(1)}, u32[]{:S(2)}, u32[]{:S(2)}) collective-permute-start(bf16[512,1024]{1,0:T(8,128)(2,1)S(1)} %pad_maximum_fusion.7), channel_id=1, source_target_pairs={{0,4},{4,0},{8,12},{12,8},{1,5},{5,1},{9,13},{13,9},{2,6},{6,2},{1... | collective-permute-start | bytes 3145736 | tf_op jit(solution)/shard_map/ppermute | solution.py:590
  1224.5 57.1 %collective-permute-start.70 = (bf16[128,2048]{1,0:T(8,128)(2,1)}, bf16[128,2048]{1,0:T(8,128)(2,1)}, u32[]{:S(2)}, u32[]{:S(2)}) collective-permute-start(bf16[128,2048]{1,0:T(8,128)(2,1)} %get-tuple-element.256), channel_id=1, source_target_pairs={{0,0},{1,1},{3,2},{16,18},{17,19},{22,20},{23,21},{4,5},{5,6},{6,7... | collective-permute-start | bytes 1572872 | tf_op jit(solution)/shard_map/ppermute | solution.py:1139
  1263.8 70.1 %collective-permute-start.64 = (bf16[512,2048]{1,0:T(8,128)(2,1)}, bf16[512,2048]{1,0:T(8,128)(2,1)}, u32[]{:S(2)}, u32[]{:S(2)}) collective-permute-start(bf16[512,2048]{1,0:T(8,128)(2,1)} %get-tuple-element.199), channel_id=1, source_target_pairs={{2,1},{3,2},{6,5},{7,6},{10,9},{11,10},{14,13},{15,14},{18,17},{19... | collective-permute-start | bytes 6291464 | tf_op jit(solution)/shard_map/ppermute | solution.py:548
  1290.0 158.3 %collective-permute-start.73 = (bf16[384,2048]{1,0:T(8,128)(2,1)S(1)}, bf16[384,2048]{1,0:T(8,128)(2,1)S(1)}, u32[]{:S(2)}, u32[]{:S(2)}) collective-permute-start(bf16[384,2048]{1,0:T(8,128)(2,1)S(1)} %slice.519), channel_id=1, source_target_pairs={{0,16},{16,0},{1,17},{17,1},{2,18},{18,2},{3,19},{19,3},{4,20},{20... | collective-permute-start | bytes 4718600 | tf_op jit(solution)/shard_map/ppermute | solution.py:495
  1329.6 125.0 %collective-permute-start.62 = (bf16[512,2048]{1,0:T(8,128)(2,1)}, bf16[512,2048]{1,0:T(8,128)(2,1)}, u32[]{:S(2)}, u32[]{:S(2)}) collective-permute-start(bf16[512,2048]{1,0:T(8,128)(2,1)} %get-tuple-element.198), channel_id=1, source_target_pairs={{0,1},{1,2},{2,3},{4,5},{5,6},{6,7},{8,9},{9,10},{10,11},{12,13},{... | collective-permute-start | bytes 6291464 | tf_op jit(solution)/shard_map/ppermute | solution.py:545
  1332.6 58.5 %collective-permute-start.80 = (bf16[128,1024]{1,0:T(8,128)(2,1)S(1)}, bf16[128,1024]{1,0:T(8,128)(2,1)S(1)}, u32[]{:S(2)}, u32[]{:S(2)}) collective-permute-start(bf16[128,1024]{1,0:T(8,128)(2,1)S(1)} %get-tuple-element.251), channel_id=1, source_target_pairs={{0,1},{1,2},{4,5},{5,6},{8,9},{9,10},{12,13},{13,14},{16,17},{17,1... | collective-permute-start | bytes 786440 | tf_op jit(solution)/shard_map/ppermute | solution.py:545
  1333.9 60.4 %collective-permute-start.83 = (bf16[128,1024]{1,0:T(8,128)(2,1)S(1)}, bf16[128,1024]{1,0:T(8,128)(2,1)S(1)}, u32[]{:S(2)}, u32[]{:S(2)}) collective-permute-start(bf16[128,1024]{1,0:T(8,128)(2,1)S(1)} %get-tuple-element.252), channel_id=1, source_target_pairs={{2,1},{3,2},{6,5},{7,6},{10,9},{11,10},{14,13},{15,14},{18,17},{19... | collective-permute-start | bytes 786440 | tf_op jit(solution)/shard_map/ppermute | solution.py:548
  1391.2 63.5 %collective-permute-start.65 = (bf16[512,2048]{1,0:T(8,128)(2,1)}, bf16[512,2048]{1,0:T(8,128)(2,1)}, u32[]{:S(2)}, u32[]{:S(2)}) collective-permute-start(bf16[512,2048]{1,0:T(8,128)(2,1)} %add_convert_fusion.3), channel_id=1, source_target_pairs={{1,0},{2,1},{3,2},{5,4},{6,5},{7,6},{9,8},{10,9},{11,10},{13,12},{... | collective-permute-start | bytes 6291464 | tf_op jit(solution)/shard_map/ppermute | solution.py:548
  (181 other events, 3077.9 us)
Sparse Core Ops, SparseCore 0:
  10.6 94.3 all-gather.14
  107.2 92.2 all-gather.6
  291.0 173.1 all-gather.8
  496.5 82.1 all-gather.10
  705.1 77.1 reduce-scatter.3
  784.5 77.2 reduce-scatter.5
  979.1 78.0 reduce-scatter.7
  1281.7 69.1 all-gather.12

commit v3 on v2

--- a/solution.py
+++ b/solution.py
@@ -366,7 +366,7 @@
     )(rows, grads, inner, down)
 
 
-def row_kernel(*refs):
+def row_kernel(starts_ref, *refs):
     hidden, gates, ups, gate_w, up_w, down_w = (refs[2 * i : 2 * i + 2] for i in range(6))
     out_ref, grad_two_ref = refs[12:]
     grad_two_ref[...] = (
@@ -375,12 +375,17 @@
         + nn(ups[0][...], up_w[0][...])
         + nn(ups[1][...], up_w[1][...])
     ).astype(BF16)
-    out_ref[...] = (
+    out = (
         nn(hidden[0][...], down_w[0][...]) + nn(hidden[1][...], down_w[1][...])
     ).astype(BF16)
-
-
-def row_pass(hidden, grad_gates, grad_ups, inner, down):
+    pieces = starts_ref.shape[0]
+    size = out.shape[0] // pieces
+    for i in range(pieces):
+        start = pl.multiple_of(starts_ref[i], size)
+        out_ref[pl.ds(start, size), :] = out[i * size : (i + 1) * size]
+
+
+def row_pass(starts, hidden, grad_gates, grad_ups, inner, down):
     count, units = hidden[0].shape
     width = down[0].shape[1]
     tile = min(256, width)
@@ -393,7 +398,9 @@
     return pl.pallas_call(
         row_kernel,
         grid=(tiles,),
-        in_specs=[resident] * 6 + [low, low, high, high, low, low],
+        in_specs=[pl.BlockSpec(memory_space=pltpu.SMEM)]
+        + [resident] * 6
+        + [low, low, high, high, low, low],
         out_specs=[column] * 2,
         out_shape=[row_shape] * 2,
         compiler_params=pltpu.CompilerParams(vmem_limit_bytes=56 << 20),
@@ -403,7 +410,7 @@
             transcendentals=0,
         ),
         name="row_pass",
-    )(*hidden, *grad_gates, *grad_ups, *inner, *inner, *down)
+    )(starts, *hidden, *grad_gates, *grad_ups, *inner, *inner, *down)
 
 
 def weight_kernel(pairs, *refs):
@@ -445,19 +452,22 @@
     )(*operands)
 
 
-def back_kernel(half_ref, grad_ref, weight_ref, rows_ref, out_ref, gain_ref):
+def back_kernel(half_ref, grad_ref, weight_ref, rows_ref, *refs):
+    out_ref, gain_ref = refs[-2:]
+
     @pl.when(pl.program_id(0) == 0)
     def _():
         gain_ref[...] = jnp.zeros_like(gain_ref)
 
     part = nn(grad_ref[...], weight_ref[...])
-    out_ref[...] = part.astype(BF16)
+    total = part + refs[0][...].astype(F32) if len(refs) > 2 else part
+    out_ref[...] = total.astype(BF16)
     rows = rows_ref[...].astype(F32)
     scale = lax.rsqrt(jnp.mean(rows * rows, axis=-1, keepdims=True) + EPSILON)
     gain_ref[...] += jnp.sum(part * (rows * scale), axis=0, keepdims=True)
 
 
-def project_back(half, grads, weight, rows):
+def project_back(half, grads, weight, rows, extra=None):
     count, outs = grads.shape[0] // 2, grads.shape[1]
     width = weight.shape[1]
     block = min(256, count)
@@ -471,7 +481,8 @@
                 pl.BlockSpec((block, outs), lambda i, at: (at[0] * steps + i, 0)),
                 pl.BlockSpec((outs, width), lambda i, at: (0, 0)),
                 pl.BlockSpec((block, width), lambda i, at: (at[0] * steps + i, 0)),
-            ],
+            ]
+            + [pl.BlockSpec((block, width), lambda i, at: (i, 0))] * (extra is not None),
             out_specs=[
                 pl.BlockSpec((block, width), lambda i, at: (i, 0)),
                 pl.BlockSpec((1, width), lambda i, at: (0, 0)),
@@ -488,7 +499,13 @@
             transcendentals=count,
         ),
         name="project_back",
-    )(jnp.reshape(half, (1,)).astype(jnp.int32), grads, weight, rows)
+    )(
+        jnp.reshape(half, (1,)).astype(jnp.int32),
+        grads,
+        weight,
+        rows,
+        *([] if extra is None else [extra]),
+    )
 
 
 def swap(values):
@@ -772,32 +789,439 @@
     )(qkv_weight, gains)
 
 
-def heads_plan(shard_rows, block_rows, dp_count, seq_count, span_count):
-    unit = math.gcd(shard_rows, block_rows)
-    per_shard, per_block = shard_rows // unit, block_rows // unit
-    per_column = 3 * span_count // dp_count
-    edges = []
-    for u in range(dp_count * seq_count * per_shard):
-        shard, block = u // per_shard, u // per_block
-        column, source = divmod(shard, seq_count)
-        core, target = divmod(block % span_count, seq_count)
-        edges.append((core, column, source, target, u % per_shard, u % per_block))
-    rounds = []
-    for edge in edges:
-        core, column, source, target = edge[:4]
-        for group in rounds:
-            if all(
-                (core, column) != e[:2] or (source != e[2] and target != e[3]) for e in group
-            ):
-                group.append(edge)
-                break
-        else:
-            rounds.append([edge])
-    return unit, per_shard, per_block, per_column, rounds
-
-
-def device_number(core, column, place, dp_count, seq_count):
-    return (core * dp_count + column) * seq_count + place
+def flipped(value, bits):
+    bit = 1
+    while bit <= bits:
+        if bits & bit:
+            value = value + bit - 2 * bit * ((value // bit) % 2)
+        bit *= 2
+    return value
+
+
+def cot_copies(cot_ref, cot_all, cube, sent, here, local, first):
+    count = len(cube) + 1
+    half = cot_ref.shape[0] // 2
+    stays, leaves = [], []
+    for side, bits in enumerate(cube_bits(count)):
+        order = cube_order(bits)
+        source = cot_ref.at[pl.ds(side * half, half)]
+        for k in range(count):
+            target = cot_all.at[pl.ds((side * count + order.index(k)) * half, half)]
+            if k == 0:
+                stays.append(pltpu.make_async_copy(source, target, local.at[first + side]))
+            else:
+                at = side * (count - 1) + k - 1
+                leaves.append(remote(source, target, sent.at[at], here.at[at], cube[k - 1]))
+    return stays, leaves
+
+
+def cot_kernel(count, cot_ref, cot_all, sent, here, local):
+    core, column, place = lax.axis_index("rep"), lax.axis_index("dp"), lax.axis_index("seq")
+    cube = [(core, flipped(column, k), place) for k in range(1, count)]
+    greet(cube)
+    stays, leaves = cot_copies(cot_ref, cot_all, cube, sent, here, local, 0)
+    for copy in stays + leaves:
+        copy.start()
+    for copy in stays + leaves:
+        copy.wait()
+
+
+def gather_cot(cot, count):
+    rows, width = cot.shape
+    anywhere = pl.BlockSpec(memory_space=pl.ANY)
+    dma = pltpu.SemaphoreType.DMA
+    return pl.pallas_call(
+        functools.partial(cot_kernel, count),
+        in_specs=[anywhere],
+        out_specs=anywhere,
+        out_shape=jax.ShapeDtypeStruct((count * rows, width), BF16),
+        scratch_shapes=[dma((2 * (count - 1),)), dma((2 * (count - 1),)), dma((2,))],
+        compiler_params=pltpu.CompilerParams(collective_id=3, has_side_effects=True),
+        cost_estimate=pl.CostEstimate(
+            flops=0, bytes_accessed=8 * rows * width, transcendentals=0
+        ),
+        name="gather_cot",
+    )(cot)
+
+
+def rest_kernel(sizes, *refs):
+    dp_count, seq_count = sizes
+    out_ref, cot_ref, out_all, cot_all = refs[:4]
+    line_sent, line_here, cube_sent, cube_here, cot_sent, cot_here, local = refs[4:]
+    core, column, place = lax.axis_index("rep"), lax.axis_index("dp"), lax.axis_index("seq")
+    line = [(core, column, (place + k) % seq_count) for k in range(1, seq_count)]
+    cube = [(core, flipped(column, k), place) for k in range(1, dp_count)]
+    greet(line + cube)
+    shard_rows = out_ref.shape[0]
+    column_rows = seq_count * shard_rows
+    def out_rows(start, size):
+        return out_all.at[pl.ds(pl.multiple_of(start, shard_rows), size)]
+
+    mine = out_rows((column * seq_count + place) * shard_rows, shard_rows)
+    lines = [
+        remote(out_ref, mine, line_sent.at[k], line_here.at[k], device)
+        for k, device in enumerate(line)
+    ]
+    own_out = pltpu.make_async_copy(out_ref, mine, local.at[0])
+
+    own_cots, cots = cot_copies(cot_ref, cot_all, cube, cot_sent, cot_here, local, 1)
+    for copy in lines + [own_out] + own_cots + cots:
+        copy.start()
+    own_out.wait()
+    for copy in lines:
+        copy.wait()
+    mine = out_rows(column * column_rows, column_rows)
+    cubes = [
+        remote(mine, mine, cube_sent.at[k], cube_here.at[k], device)
+        for k, device in enumerate(cube)
+    ]
+    for copy in cubes:
+        copy.start()
+    for copy in own_cots + cots:
+        copy.wait()
+    for k, copy in enumerate(cubes):
+        copy.wait_send()
+        theirs = out_rows(cube[k][1] * column_rows, column_rows)
+        remote(theirs, theirs, cube_sent.at[k], cube_here.at[k], cube[k]).wait_recv()
+
+
+def gather_rest(out_half, cot, sizes):
+    dp_count, seq_count = sizes
+    rows, width = cot.shape
+    anywhere = pl.BlockSpec(memory_space=pl.ANY)
+    dma = pltpu.SemaphoreType.DMA
+    return pl.pallas_call(
+        functools.partial(rest_kernel, sizes),
+        in_specs=[anywhere] * 2,
+        out_specs=[anywhere] * 2,
+        out_shape=[
+            jax.ShapeDtypeStruct(
+                (dp_count * seq_count * out_half.shape[0], out_half.shape[1]), BF16
+            ),
+            jax.ShapeDtypeStruct((dp_count * rows, width), BF16),
+        ],
+        scratch_shapes=[
+            dma((seq_count - 1,)),
+            dma((seq_count - 1,)),
+            dma((dp_count - 1,)),
+            dma((dp_count - 1,)),
+            dma((2 * (dp_count - 1),)),
+            dma((2 * (dp_count - 1),)),
+            dma((3,)),
+        ],
+        compiler_params=pltpu.CompilerParams(collective_id=2, has_side_effects=True),
+        cost_estimate=pl.CostEstimate(
+            flops=0, bytes_accessed=8 * rows * width, transcendentals=0
+        ),
+        name="gather_rest",
+    )(out_half, cot)
+
+
+def add_rows(out_ref, refs, size):
+    def some(i, _):
+        rows = pl.ds(pl.multiple_of(i * size, size), size)
+        total = refs[0][rows, :].astype(F32)
+        for ref in refs[1:]:
+            total += ref[rows, :].astype(F32)
+        out_ref[rows, :] = total.astype(out_ref.dtype)
+        return 0
+
+    lax.fori_loop(0, out_ref.shape[0] // size, some, 0)
+
+
+def spread_kernel(
+    sizes,
+    micros,
+    *refs,
+):
+    spread_body(sizes, refs[:micros], *refs[micros:])
+
+
+def spread_body(
+    sizes,
+    line_refs,
+    qkv_ref,
+    out_ref,
+    grad_ref,
+    qkv_done,
+    out_done,
+    rising,
+    falling,
+    qkv_in,
+    qkv_sum,
+    out_in,
+    out_part,
+    out_line,
+    rise_sent,
+    rise_here,
+    fall_sent,
+    fall_here,
+    qkv_sent,
+    qkv_here,
+    out_sent,
+    out_here,
+    unit_sent,
+    unit_here,
+    line_sent,
+    line_here,
+    swap_sent,
+    swap_here,
+    local,
+):
+    dp_count, seq_count, unit, per_shard, per_block, per_column = sizes
+    span_count = 2 * seq_count
+    micros = len(line_refs)
+    core, column, place = lax.axis_index("rep"), lax.axis_index("dp"), lax.axis_index("seq")
+    span = core * seq_count + place
+    cube = [(core, (column + k) % dp_count, place) for k in range(1, dp_count)]
+    line = [(core, column, (place + k) % seq_count) for k in range(1, seq_count)]
+    across = [(1 - core, column, (place + k) % seq_count) for k in range(seq_count)]
+    greet(cube + line + across)
+
+    def part_at(part, col):
+        return (part * span_count + span) // per_column == col
+
+    def out_copy(k):
+        target = cube[k]
+        return remote(
+            out_ref.at[target[1]], out_in.at[k], out_sent.at[k], out_here.at[k], target
+        )
+
+    def qkv_copy(k, part):
+        return remote(
+            qkv_ref.at[part], qkv_in.at[k], qkv_sent.at[k], qkv_here.at[k], cube[k]
+        )
+
+    def hop(number, m, up):
+        reach = seq_count - number
+        buffer, sent, here = (
+            (rising, rise_sent, rise_here) if up else (falling, fall_sent, fall_here)
+        )
+        behind = place if up else seq_count - 1 - place
+        owner = place + reach if up else place - reach
+        owner = jnp.clip(owner, 0, seq_count - 1)
+        next_place = jnp.clip(place + 1 if up else place - 1, 0, seq_count - 1)
+        device = (core, column, next_place)
+        at = (number - 1) * micros + m
+        target = buffer.at[at]
+
+        def send(source):
+            remote(source, target, sent.at[at], here.at[at], device).start()
+
+        own = line_refs[m].at[owner]
+        if number == 1:
+            pl.when(behind == 0)(lambda: send(own))
+            return
+
+        @pl.when(behind == 0)
+        def _():
+            send(own)
+
+        @pl.when((behind >= 1) & (behind <= number - 1))
+        def _():
+            before = buffer.at[at - micros]
+            remote(before, before, sent.at[0], here.at[at - micros], across[0]).wait_recv()
+            add_rows(before, [before, own], 64)
+            send(before)
+
+    def hop_sent(number, m, up):
+        sent = rise_sent if up else fall_sent
+        buffer = rising if up else falling
+        behind = place if up else seq_count - 1 - place
+        at = (number - 1) * micros + m
+        piece = buffer.at[at]
+
+        @pl.when(behind <= number - 1)
+        def _():
+            remote(piece, piece, sent.at[at], sent.at[at], across[0]).wait_send()
+
+    def hops(number):
+        for m in range(micros):
+            hop(number, m, True)
+            hop(number, m, False)
+
+    hops(1)
+    for k in range(dp_count - 1):
+        out_copy(k).start()
+        for part in range(3):
+
+            @pl.when(part_at(part, cube[k][1]))
+            def _():
+                qkv_copy(k, part).start()
+
+    hops(2)
+
+    for k in range(dp_count - 1):
+        out_copy(k).wait_recv()
+    for s in range(seq_count):
+        add_rows(
+            out_part.at[s],
+            [out_ref.at[column, s]] + [out_in.at[k, s] for k in range(dp_count - 1)],
+            32,
+        )
+
+    def line_copy(k):
+        return remote(
+            out_part.at[line[k][2]], out_line.at[k], line_sent.at[k], line_here.at[k], line[k]
+        )
+
+    for k in range(seq_count - 1):
+        line_copy(k).start()
+
+    def unit_copies(part, j):
+        number = (part * span_count + span) * per_block + j
+        owner = (number // per_shard) % seq_count
+        source = qkv_sum.at[pl.ds(j * unit, unit)]
+        target = qkv_done.at[pl.ds(pl.multiple_of((number % per_shard) * unit, unit), unit)]
+        here = unit_here.at[number % per_shard]
+        other = remote(
+            source, target, unit_sent.at[2 * j], here, (1 - core, column, owner)
+        )
+        same = remote(source, target, unit_sent.at[2 * j + 1], here, (core, column, owner))
+        stays = pltpu.make_async_copy(source, target, local.at[j])
+        return owner, other, same, stays
+
+    for part in range(3):
+
+        @pl.when(part_at(part, column))
+        def _():
+            for k in range(dp_count - 1):
+                qkv_copy(k, part).wait_recv()
+            add_rows(
+                qkv_sum, [qkv_ref.at[part]] + [qkv_in.at[k] for k in range(dp_count - 1)], 32
+            )
+            for j in range(per_block):
+                owner, other, same, stays = unit_copies(part, j)
+                other.start()
+                pl.when(owner != place)(same.start)
+                pl.when(owner == place)(stays.start)
+
+    for number in range(3, seq_count):
+        hops(number)
+
+    for k in range(seq_count - 1):
+        line_copy(k).wait_recv()
+    add_rows(
+        out_done.at[core],
+        [out_part.at[place]] + [out_line.at[k] for k in range(seq_count - 1)],
+        32,
+    )
+    mine = out_done.at[core]
+    swapped = remote(mine, mine, swap_sent, swap_here, across[0])
+    swapped.start()
+
+    last = (seq_count - 2) * micros
+    for m in range(micros):
+        own = line_refs[m].at[place]
+        up, down = rising.at[last + m], falling.at[last + m]
+
+        @pl.when(place > 0)
+        def _():
+            remote(up, up, rise_sent.at[0], rise_here.at[last + m], across[0]).wait_recv()
+
+        @pl.when(place < seq_count - 1)
+        def _():
+            remote(down, down, fall_sent.at[0], fall_here.at[last + m], across[0]).wait_recv()
+
+        @pl.when(place == 0)
+        def _():
+            add_rows(grad_ref.at[m], [own, down], 64)
+
+        @pl.when(place == seq_count - 1)
+        def _():
+            add_rows(grad_ref.at[m], [own, up], 64)
+
+        @pl.when((place > 0) & (place < seq_count - 1))
+        def _():
+            add_rows(grad_ref.at[m], [own, up, down], 64)
+
+    for number in range(1, seq_count):
+        for m in range(micros):
+            hop_sent(number, m, True)
+            hop_sent(number, m, False)
+    for k in range(dp_count - 1):
+        out_copy(k).wait_send()
+        for part in range(3):
+
+            @pl.when(part_at(part, cube[k][1]))
+            def _():
+                qkv_copy(k, part).wait_send()
+
+    for k in range(seq_count - 1):
+        line_copy(k).wait_send()
+    for part in range(3):
+
+        @pl.when(part_at(part, column))
+        def _():
+            for j in range(per_block):
+                owner, other, same, stays = unit_copies(part, j)
+                other.wait_send()
+                pl.when(owner != place)(same.wait_send)
+                pl.when(owner == place)(stays.wait)
+
+    for i in range(per_shard):
+        number = (column * seq_count + place) * per_shard + i
+        piece = qkv_done.at[pl.ds(i * unit, unit)]
+
+        @pl.when((number // per_block) % span_count != span)
+        def _():
+            remote(piece, piece, unit_sent.at[0], unit_here.at[i], across[0]).wait_recv()
+
+    swapped.wait_send()
+    theirs = out_done.at[1 - core]
+    remote(theirs, theirs, swap_sent, swap_here, across[0]).wait_recv()
+
+
+def spread_sums(lines, qkv, out, sizes):
+    dp_count, seq_count, unit, per_shard, per_block, _ = sizes
+    micros = len(lines)
+    _, rows, width = lines[0].shape
+    shard_out, half_width = out.shape[2:]
+    block_rows = unit * per_block
+    hops = (seq_count - 1) * micros
+    vmem = pl.BlockSpec(memory_space=pltpu.VMEM)
+    dma = pltpu.SemaphoreType.DMA
+    return pl.pallas_call(
+        functools.partial(spread_kernel, sizes, micros),
+        in_specs=[vmem] * (micros + 2),
+        out_specs=[vmem] * 3,
+        out_shape=[
+            jax.ShapeDtypeStruct((micros, rows, width), F32),
+            jax.ShapeDtypeStruct((per_shard * unit, width), BF16),
+            jax.ShapeDtypeStruct((2, shard_out, half_width), BF16),
+        ],
+        scratch_shapes=[
+            pltpu.VMEM((hops, rows, width), BF16),
+            pltpu.VMEM((hops, rows, width), BF16),
+            pltpu.VMEM((dp_count - 1, block_rows, width), BF16),
+            pltpu.VMEM((block_rows, width), BF16),
+            pltpu.VMEM((dp_count - 1, seq_count, shard_out, half_width), BF16),
+            pltpu.VMEM((seq_count, shard_out, half_width), BF16),
+            pltpu.VMEM((seq_count - 1, shard_out, half_width), BF16),
+            dma((hops,)),
+            dma((hops,)),
+            dma((hops,)),
+            dma((hops,)),
+            dma((dp_count - 1,)),
+            dma((dp_count - 1,)),
+            dma((dp_count - 1,)),
+            dma((dp_count - 1,)),
+            dma((2 * per_block,)),
+            dma((per_shard,)),
+            dma((seq_count - 1,)),
+            dma((seq_count - 1,)),
+            dma,
+            dma,
+            dma((per_block,)),
+        ],
+        compiler_params=pltpu.CompilerParams(
+            collective_id=1, has_side_effects=True, vmem_limit_bytes=56 << 20
+        ),
+        cost_estimate=pl.CostEstimate(
+            flops=0, bytes_accessed=256 * rows * width, transcendentals=0
+        ),
+        name="spread_sums",
+    )(*lines, qkv, out)
 
 
 def pick(table, number):
@@ -827,7 +1251,6 @@
     block_rows = heads_here * head_dim
     core, column, place = lax.axis_index("rep"), lax.axis_index("dp"), lax.axis_index("seq")
     span = core * seq_count + place
-    number = device_number(core, column, place, dp_count, seq_count)
     inner_half = inner_weight.shape[0] // 2
 
     own_rows = [tokens[m, 0] for m in range(micros)]
@@ -837,9 +1260,9 @@
 
     all_rows = [gather_rows(own_rows[0])]
 
-    unit, per_shard, per_block, per_column, rounds = heads_plan(
-        qkv_weight.shape[0], block_rows, dp_count, seq_count, span_count
-    )
+    unit = math.gcd(qkv_weight.shape[0], block_rows)
+    per_shard, per_block = qkv_weight.shape[0] // unit, block_rows // unit
+    per_column = 3 * span_count // dp_count
     devices = 2 * dp_count * seq_count
     shard_out, shard_gain = out_weight.shape[0], norm_gains.shape[1]
     lanes = -(-shard_gain // 128) * 128
@@ -850,32 +1273,24 @@
     )
     gains_all = jnp.swapaxes(gains_all[:, :2, :shard_gain], 0, 1).reshape(2, width)
     gain_one, gain_two = gains_all[0:1], gains_all[1:2]
-    orders = [cube_order(bits) for bits in cube_bits(dp_count)]
-    spots = [[order.index(k) for k in range(dp_count)] for order in orders]
-
-    def column_block(gathered, half, owner):
-        sides = []
-        for side in range(2):
-            spot = pick(spots[side], owner ^ column) + side * dp_count
-            sides.append(lax.dynamic_slice_in_dim(gathered, spot * half, half, 0))
-        return sides
-
-    half_block = block_rows // 2
     half_width = width // 2
-    out_line = line_gather(
-        lax.dynamic_slice_in_dim(out_weight, core * half_width, half_width, 1), "seq"
-    )
+    positions = span * span_rows + jnp.arange(span_rows)
+    lives = []
+    for m in range(micros):
+        live_rows = (positions < lengths[m, 0]).astype(F32)
+        lives.append(cotangent[m, 0].astype(F32) * live_rows[:, None])
     for rows in own_rows[1:]:
         all_rows.append(gather_rows(after(rows, all_rows[-1], head_weight)))
-    column_out = seq_count * shard_out
-    out_blocks = cube_gather(out_line, "dp")
-    out_near = []
-    for owner in range(dp_count):
-        out_near += column_block(out_blocks, column_out // 2, owner)
-    out_near = jnp.concatenate(out_near, axis=0)
+    out_half = lax.dynamic_slice_in_dim(out_weight, core * half_width, half_width, 1)
+    cots = [live.astype(BF16) for live in lives]
+    out_near, cot_all = gather_rest(
+        after(out_half, head_weight, all_rows[0]), cots[0], (dp_count, seq_count)
+    )
+    grads_all = [cot_all]
+    for cot in cots[1:]:
+        grads_all.append(gather_cot(after(cot, grads_all[-1], all_rows[-1]), dp_count))
     out_far = swap(out_near)
 
-    positions = span * span_rows + jnp.arange(span_rows)
     gate_share = jax.nn.sigmoid(gate_logit)
     gate_here = lax.dynamic_slice_in_dim(gate_share, span * heads_here, heads_here, 0)
     near_at, far_at = core * half_width, (1 - core) * half_width
@@ -884,10 +1299,11 @@
     saved = []
     outputs, new_memories, new_norms = [], [], []
     for m in range(micros):
-        hidden_one, projected = project(all_rows[m], gain_one, head_weight)
-        live_rows = (positions < lengths[m, 0]).astype(F32)
-        live = cotangent[m, 0].astype(F32) * live_rows[:, None]
-        grad_rows = cube_gather(after(live.astype(BF16), projected), "dp")
+        hidden_one, projected = project(
+            after(all_rows[m], all_rows[-1], grads_all[-1]),
+            gain_one,
+            head_weight,
+        )
         if m == 0:
             near_units, near_downs = (
                 lax.dynamic_slice_in_dim(w, core * inner_half, inner_half, 0)
@@ -903,7 +1319,7 @@
         )
         if m == 0:
             inner_near = lax.all_gather(
-                after(near_units, all_rows[-1]),
+                after(near_units, all_rows[-1], out_near),
                 "seq",
                 axis=0,
                 tiled=True,
@@ -921,18 +1337,22 @@
         mixed_near = lax.dynamic_slice_in_dim(mixed, near_at, half_width, 1)
         mixed_far = lax.dynamic_slice_in_dim(mixed, far_at, half_width, 1)
         after_attn = (
-            own_rows[m].astype(F32) + nt(mixed_near, out_near) + nt(mixed_far, out_far)
+            own_rows[m].astype(F32)
+            + nt(mixed_near, out_near)
+            + nt(mixed_far, out_far)
         )
         scale_two = lax.rsqrt(jnp.mean(after_attn * after_attn, axis=-1, keepdims=True) + EPSILON)
         normed_two = after_attn * scale_two
         hidden_two = (normed_two * gain_two).astype(BF16)
+        if m + 1 == micros:
+            hidden_two = after(hidden_two, inner_near)
         rows_all = cube_gather(hidden_two, "dp")
         saved.append(
             dict(
                 hidden_one=hidden_one,
                 projected=projected,
-                live=live,
-                grads=grad_rows,
+                live=lives[m],
+                grads=grads_all[m],
                 memory=memory_here,
                 norm=norm_here,
                 length=length,
@@ -949,7 +1369,7 @@
         )
 
     down_near = lax.all_gather(
-        after(near_downs, inner_near, *[s[n] for s in saved for n in ("rows", "grads")]),
+        near_downs,
         "seq",
         axis=0,
         tiled=True,
@@ -973,10 +1393,18 @@
     def spread(values):
         return lax.psum_scatter(values, "seq", scatter_dimension=0, tiled=True)
 
+    starts = jnp.stack(
+        [
+            (column ^ k) * span_rows + side * (span_rows // 2)
+            for side, bits in enumerate(cube_bits(dp_count))
+            for k in cube_order(bits)
+        ]
+    ).astype(jnp.int32)
+
     def rows_out(s, *earlier):
         gates = (after(s["grad_gates"][0], *earlier), s["grad_gates"][1])
         s["mlp_part"], s["grad_two_part"] = row_pass(
-            s["hidden"], gates, s["grad_ups"], inner, down
+            starts, s["hidden"], gates, s["grad_ups"], inner, down
         )
         return s["grad_two_part"]
 
@@ -988,13 +1416,6 @@
     up_far_sum = half_grads("grad_ups", "rows", 1, last)
     gate_sum = half_grads("grad_gates", "rows", 0, up_far_sum, swap(gate_far_sum))
     gate_mine = spread(gate_sum)
-    last = gate_sum
-    for s in saved[1:]:
-        last = rows_out(s, last, down_mine)
-    up_sum = half_grads("grad_ups", "rows", 0, last, swap(up_far_sum))
-    up_mine = spread(up_sum)
-    last = up_sum
-
     def rows_back(s, pins):
         grad_two = cube_scatter(s["grad_two_part"], "dp", pins)
         grad_scaled = grad_two * gain_two
@@ -1038,10 +1459,10 @@
             1 - core, s["grad_projected"], head_weight, all_rows[m]
         )
         part_near, gains_near = project_back(
-            core, after(s["grad_projected"], part_far), head_weight, all_rows[m]
+            core, s["grad_projected"], head_weight, all_rows[m], swap(part_far)
         )
         s["gains_one"] = (gains_far + gains_near)[0]
-        return part_near, add_low(part_near, swap(part_far))
+        return part_near
 
     def tokens_back(s, m, grad_one):
         rows_float = own_rows[m].astype(F32)
@@ -1057,35 +1478,46 @@
             )
         ).astype(BF16)
 
-    heads_grads = [rows_back(s, ()) for s in saved]
-    earlier = (last, gate_mine)
-    sums = []
+    heads_grads = [rows_back(saved[0], ())]
+    last = gate_sum
+    for m, s in enumerate(saved[1:]):
+        last = rows_out(s, last, down_mine)
+        heads_grads.append(rows_back(s, ()))
+
+    def spread_out(s, *earlier):
+        return lax.psum_scatter(
+            after(s["mlp_part"], *earlier), "dp", scatter_dimension=0, tiled=True
+        )
+
+    mlp_outs, sums = [spread_out(saved[0], saved[-1]["grad_branch"])], []
+    last = after(last, gate_mine)
     for m, s in enumerate(saved):
-        last, part = heads_back(s, m, after(heads_grads[m], *earlier))
-        sums.append(part)
-        earlier = (last,)
-    grad_ones = line_scatter(
-        jnp.concatenate(
-            [p.reshape(seq_count, span_rows, width) for p in sums], axis=1
-        ).reshape(-1, width),
-        "seq",
-    )
-    grad_tokens = [
-        tokens_back(s, m, grad_ones[m * span_rows : (m + 1) * span_rows])
-        for m, s in enumerate(saved)
-    ]
-    out_far_sum = weight_pass(
-        [(after(s["grad_branch"], last, up_mine), s["mixed_far"]) for s in saved]
-    )
-    out_near_sum = weight_pass(
-        [(after(s["grad_branch"], out_far_sum), s["mixed_near"]) for s in saved]
-    )
-    qkv_low = weight_pass(
-        [(after(s["grad_projected"], out_near_sum), s["hidden_one"]) for s in saved]
-    ).reshape(3, block_rows, width)
-    for m, s in enumerate(saved):
-        mlp_out = cube_scatter(s["mlp_part"], "dp")
-        outputs.append((s["after_attn"] + mlp_out).astype(BF16))
+        sums.append(heads_back(s, m, after(heads_grads[m], last)))
+        if m == 0:
+            up_sum = half_grads("grad_ups", "rows", 0, s["grad_projected"], swap(up_far_sum))
+            up_mine = spread(up_sum)
+            last = after(up_sum, mlp_outs[0])
+        else:
+            mlp_outs.append(spread_out(s, up_sum))
+    out_far_sum = weight_pass([(s["grad_branch"], s["mixed_far"]) for s in saved])
+    out_sum = weight_pass(
+        [(s["grad_branch"], s["mixed_near"]) for s in saved], swap(out_far_sum)
+    )
+    qkv_low = weight_pass([(s["grad_projected"], s["hidden_one"]) for s in saved]).reshape(
+        3, block_rows, width
+    )
+
+    grad_ones, qkv_done, out_done = spread_sums(
+        [after(p, up_mine, *mlp_outs).reshape(seq_count, span_rows, width) for p in sums],
+        qkv_low,
+        out_sum.reshape(dp_count, seq_count, shard_out, half_width),
+        (dp_count, seq_count, unit, per_shard, per_block, per_column),
+    )
+    grad_tokens = [tokens_back(s, m, grad_ones[m]) for m, s in enumerate(saved)]
+    grad_qkv = qkv_done.astype(F32)
+    grad_out = jnp.swapaxes(out_done, 0, 1).reshape(shard_out, width).astype(F32)
+    for s, mlp_out in zip(saved, mlp_outs):
+        outputs.append((s["after_attn"] + mlp_out.astype(F32)).astype(BF16))
 
     def joined(name):
         return functools.reduce(jnp.add, [s[name] for s in saved])
@@ -1103,43 +1535,6 @@
 
     grad_down = both_cores(down_mine, 0)
     grad_inner = both_cores(jnp.concatenate([gate_mine, up_mine], axis=1), 0)
-
-    out_mine = add_low(out_near_sum, swap(out_far_sum)).reshape(
-        dp_count, column_out, half_width
-    )
-    pieces = []
-    for side in range(2):
-        for k in orders[side]:
-            owned = lax.dynamic_index_in_dim(out_mine, column ^ k, 0, keepdims=False)
-            pieces.append(owned[side * column_out // 2 : (side + 1) * column_out // 2])
-    out_column = cube_scatter(jnp.concatenate(pieces, axis=0), "dp").astype(BF16)
-    grad_out = both_cores(line_scatter(out_column, "seq").astype(BF16), 1)
-
-    qkv_low = jnp.concatenate([qkv_low, jnp.zeros((1, block_rows, width), BF16)], axis=0)
-    which = [3] * (span_count * dp_count)
-    for part in range(3):
-        for owner in range(span_count):
-            which[owner * dp_count + (part * span_count + owner) // per_column] = part
-    pieces = []
-    for side in range(2):
-        for k in orders[side]:
-            part = pick(which, span * dp_count + (column ^ k))
-            block = lax.dynamic_index_in_dim(qkv_low, part, 0, keepdims=False)
-            pieces.append(block[side * half_block : (side + 1) * half_block])
-    qkv_block = cube_scatter(jnp.concatenate(pieces, axis=0), "dp").astype(BF16)
-    returned = jnp.zeros(((per_shard + 1) * unit, width), BF16)
-    for group in rounds:
-        send, slot, pairs = [0] * devices, [per_shard] * devices, []
-        for c, col, source, target, from_unit, to_unit in group:
-            a = device_number(c, col, target, dp_count, seq_count)
-            b = device_number(c, col, source, dp_count, seq_count)
-            send[a], slot[b] = to_unit, from_unit
-            pairs.append((a, b))
-        piece = lax.dynamic_slice_in_dim(qkv_block, pick(send, number) * unit, unit, 0)
-        piece = lax.ppermute(piece, ALL, pairs)
-        returned = lax.dynamic_update_slice_in_dim(returned, piece, pick(slot, number) * unit, 0)
-    returned = returned[: per_shard * unit]
-    grad_qkv = returned.astype(F32) + swap(returned).astype(F32)
 
     gate_terms = joined("gate") * gate_here * (1.0 - gate_here)
     gate_row = lax.dynamic_update_slice_in_dim(

time: 1480 us -> 1370 us (0.926)
  Pallas kernels: 450 us -> 839 us
  waiting for transfers between devices: 480 us -> 266 us
  starting transfers between devices: 209 us -> 43.7 us
  local copies, waits for them, and re-layouts: 165 us -> 94.2 us
  other arithmetic: 106 us -> 48.5 us
  blocking collectives: 0 us -> 28.7 us
  between operations: 30.6 us -> 15.6 us
    pallas_call x2 -> x5, Pallas kernels: 70.2 us -> 435 us  [the longest x1 213 us: spread_sums(): pl.pallas_call(functools.partial(spread_kernel, sizes, micros), in_specs=...]
    ppermute x21 -> x0, waiting for transfers between devices: 159 us -> none  [the longest x6 82.4 us: line_scatter(): lax.ppermute(up.astype(BF16), axis, [(a, a + 1) for a in range(count) if...]
    ppermute x24 -> x8, waiting for transfers between devices: 88.5 us -> 38.6 us  [cube_scatter(): got = lax.ppermute(held[keep:].astype(BF16), axis, pairs)]
    ppermute x21 -> x0, starting transfers between devices: 45.9 us -> none  [the longest x6 16.2 us: line_scatter(): lax.ppermute(down.astype(BF16), axis, [(a, a - 1) for a in range(count) i...]
    ppermute x13 -> x11, starting transfers between devices: 52.4 us -> 8.58 us  [swap(): return lax.ppermute(values, 'rep', [(0, 1), (1, 0)])]
    all_gather x2, waiting for transfers between devices: 80.3 us -> 45.1 us  [the longest x1 45 us: shards(): down_near = lax.all_gather(near_downs, 'seq', axis=0, tiled=True)]
    ppermute x24 -> x8, starting transfers between devices: 40 us -> 6.38 us  [cube_scatter(): got = lax.ppermute(held[keep:].astype(BF16), axis, pairs)]
    unnamed x264 -> x186, local copies, waits for them, and re-layouts: 86.2 us -> 53.9 us
  transfers between devices with their start and end apart: 100 -> 44, of which waited for: 32 -> 17; matrix products, arithmetic and copies ran while one was open for 17% -> 9% of each run, Pallas kernels for 25% -> 55%
where the time goes in v3:
time: 1370 us; the launch traced here: 1360 us
  Pallas kernels  839 us (61%)
  waiting for transfers between devices  266 us (19%)
  local copies, waits for them, and re-layouts  94.2 us (7%)
  other arithmetic  48.5 us (4%)
  starting transfers between devices  43.7 us (3%)
  blocking collectives  28.7 us (2%)
  matrix products  24.7 us (2%)
  between operations  15.6 us (1%)
    pallas_call x1, Pallas kernels, spread_sums(): pl.pallas_call(functools.partial(spread_kernel, sizes, micros), in_specs=...  213 us
    pallas_call x9, Pallas kernels, weight_pass(): pl.pallas_call(functools.partial(weight_kernel, len(pairs)), grid=(size /...  127 us
    pallas_call x1, Pallas kernels, gather_rest(): pl.pallas_call(functools.partial(rest_kernel, sizes), in_specs=[anywhere]...  104 us
    pallas_call x4, Pallas kernels, unit_pass(): pl.pallas_call(unit_kernel, grid=(units // tile,), in_specs=[resident, re...  78.5 us
    pallas_call x2, Pallas kernels, row_pass(): pl.pallas_call(row_kernel, grid=(tiles,), in_specs=[pl.BlockSpec(memory_s...  70.7 us
    pallas_call x1, Pallas kernels, gather_heads(): pl.pallas_call(functools.partial(heads_kernel, sizes), in_specs=[anywhere...  59.7 us
    unnamed x186, local copies, waits for them, and re-layouts  53.9 us
    ppermute x12, waiting for transfers between devices, cube_gather(): lax.ppermute(v, axis, pairs)  51.1 us
  transfers between devices with their start and end apart: 44, of which 17 were waited for; matrix products, arithmetic and copies ran while one was open for 9% of the time, Pallas kernels for 55%

profile of v3, /device:TPU:17, one launch (start us, length us, event | category | flops | bytes accessed | tf_op | source)
XLA Modules:
  0.0 1359.7 jit_solution(1732024992388145478)
XLA Ops:
  12.1 59.7 %gather_heads.1 = (bf16[768,2048]{1,0:T(8,128)(2,1)S(1)}, f32[16,8,128]{2,1,0:T(8,128)S(1)}) custom-call(bf16[384,2048]{1,0:T(8,128)(2,1)S(1)} %copy-done.13, f32[8,128]{1,0:T(8,128)S(1)} %pad_convert_fusion.gain_ref), custom_call_target="tpu_custom_call" | custom-call | bytes 33554432 | tf_op jit(solution)/shard_map/gather_heads/pallas_call | solution.py:762
  73.4 31.6 %all-gather.15.cloned.1.call-done = bf16[1,1,2048,2048]{3,2,1,0:T(8,128)(2,1)} async-done(((bf16[1,1,256,2048]{3,2,1,0:T(8,128)(2,1)}), bf16[1,1,2048,2048]{3,2,1,0:T(8,128)(2,1)}) %all-gather.15.cloned.1.call-update) | async-done | bytes 8388624 | tf_op jit(solution)/shard_map/all_gather | solution.py:1259
  114.1 104.1 %gather_rest.1 = (bf16[2048,1024]{1,0:T(8,128)(2,1)}, bf16[1024,2048]{1,0:T(8,128)(2,1)}) custom-call(bf16[128,1024]{1,0:T(8,128)(2,1)} %constant_dynamic-slice_fusion.9.refs_0_, bf16[256,2048]{1,0:T(8,128)(2,1)} %get-tuple-element.220.refs_1_), custom_call_target="tpu_custom_call" | custom-call | bytes 4194304 | tf_op jit(solution)/shard_map/gather_rest/pallas_call | solution.py:893
  221.3 47.4 %gather_cot.1.grad_ref.refs_3_ = bf16[1024,2048]{1,0:T(8,128)(2,1)} custom-call(bf16[256,2048]{1,0:T(8,128)(2,1)} %get-tuple-element.86.cot_ref), custom_call_target="tpu_custom_call" | custom-call | bytes 4194304 | tf_op jit(solution)/shard_map/gather_cot/pallas_call | solution.py:833
  270.6 11.3 project.2
  285.3 21.6 %attend.2 = (bf16[2048,256]{1,0:T(8,128)(2,1)}, f32[2048,256]{1,0:T(8,128)S(1)}, f32[2,1,2048]{2,1,0:T(1,128)S(1)}, f32[2,128,128]{2,1,0:T(8,128)S(1)}, f32[2,1,128]{2,1,0:T(1,128)S(1)}) custom-call(s32[1]{0:T(128)} %bitcast.1.length_ref, f32[2]{0:T(128)S(1)} %dynamic_slice.43.gate_ref, bf16[2048,768]{1,0:T(8,128)(2,1)S(1)} %get-tuple-element.89.q_ref.k_ref.v_ref, ...), custom_call_target="tpu_custom_call" | custom-call | flops 4294967296 | bytes 6291456 | tf_op jit(solution)/shard_map/attend/pallas_call | solution.py:156
  319.3 11.3 project.3
  333.8 17.4 %attend.3 = (bf16[2048,256]{1,0:T(8,128)(2,1)}, f32[2048,256]{1,0:T(8,128)S(1)}, f32[2,1,2048]{2,1,0:T(1,128)S(1)}, f32[2,128,128]{2,1,0:T(8,128)S(1)}, f32[2,1,128]{2,1,0:T(1,128)S(1)}) custom-call(s32[1]{0:T(128)} %bitcast.23.length_ref, f32[2]{0:T(128)S(1)} %dynamic_slice.43.gate_ref, bf16[2048,768]{1,0:T(8,128)(2,1)S(1)} %get-tuple-element.99.q_ref.k_ref.v_ref, ...), custom_call_target="tpu_custom_call" | custom-call | flops 4294967296 | bytes 6291456 | tf_op jit(solution)/shard_map/attend/pallas_call | solution.py:156
  354.9 13.3 all-to-all-done
  375.6 35.7 %all-to-all-done.1 = bf16[8,256,256]{2,1,0:T(8,128)(2,1)S(1)} async-done(((bf16[8,256,256]{2,1,0:T(8,128)(2,1)}), bf16[8,256,256]{2,1,0:T(8,128)(2,1)S(1)}, u32[]{:S(2)}, u32[]{:S(2)}) %all-to-all-start.1) | async-done | bytes 1048608 | tf_op jit(solution)/shard_map/all_to_all | solution.py:1329
  436.4 12.2 collective-permute-done.2
  448.6 45.0 %all-gather.11.cloned.1.call-done.down_ref.refs_10_ = bf16[1024,2048]{1,0:T(8,128)(2,1)} async-done(((bf16[256,2048]{1,0:T(8,128)(2,1)}), bf16[1024,2048]{1,0:T(8,128)(2,1)}) %all-gather.11.cloned.1.call-update) | async-done | bytes 4194320 | tf_op jit(solution)/shard_map/all_gather | solution.py:1371
  531.5 19.9 %unit_pass.4 = (bf16[1024,1024]{1,0:T(8,128)(2,1)}, bf16[1024,1024]{1,0:T(8,128)(2,1)}, bf16[1024,1024]{1,0:T(8,128)(2,1)}) custom-call(bf16[1024,2048]{1,0:T(8,128)(2,1)} %constant_dynamic-update-slice_fusion.rows_ref.refs_1_, bf16[1024,2048]{1,0:T(8,128)(2,1)} %get-tuple-element.85.grad_ref.refs_1_, ...), custom_call_target="tpu_custom_call" | custom-call | flops 12884901888 | bytes 27262976 | tf_op jit(solution)/shard_map/unit_pass/pallas_call | solution.py:348
  575.9 19.7 %unit_pass.5 = (bf16[1024,1024]{1,0:T(8,128)(2,1)}, bf16[1024,1024]{1,0:T(8,128)(2,1)}, bf16[1024,1024]{1,0:T(8,128)(2,1)}) custom-call(bf16[1024,2048]{1,0:T(8,128)(2,1)} %constant_dynamic-update-slice_fusion.rows_ref.refs_1_, bf16[1024,2048]{1,0:T(8,128)(2,1)} %get-tuple-element.85.grad_ref.refs_1_, ...), custom_call_target="tpu_custom_call" | custom-call | flops 12884901888 | bytes 27262976 | tf_op jit(solution)/shard_map/unit_pass/pallas_call | solution.py:348
  595.6 19.4 %unit_pass.6 = (bf16[1024,1024]{1,0:T(8,128)(2,1)}, bf16[1024,1024]{1,0:T(8,128)(2,1)}, bf16[1024,1024]{1,0:T(8,128)(2,1)}) custom-call(bf16[1024,2048]{1,0:T(8,128)(2,1)} %constant_dynamic-update-slice_fusion.8.rows_ref.refs_3_, bf16[1024,2048]{1,0:T(8,128)(2,1)} %gather_cot.1.grad_ref.refs_3_, ...), custom_call_target="tpu_custom_call" | custom-call | flops 12884901888 | bytes 27262976 | tf_op jit(solution)/shard_map/unit_pass/pallas_call | solution.py:348
  615.1 19.5 %unit_pass.7 = (bf16[1024,1024]{1,0:T(8,128)(2,1)}, bf16[1024,1024]{1,0:T(8,128)(2,1)}, bf16[1024,1024]{1,0:T(8,128)(2,1)}) custom-call(bf16[1024,2048]{1,0:T(8,128)(2,1)} %constant_dynamic-update-slice_fusion.8.rows_ref.refs_3_, bf16[1024,2048]{1,0:T(8,128)(2,1)} %gather_cot.1.grad_ref.refs_3_, ...), custom_call_target="tpu_custom_call" | custom-call | flops 12884901888 | bytes 27262976 | tf_op jit(solution)/shard_map/unit_pass/pallas_call | solution.py:348
  634.6 14.5 %weight_pass.9 = bf16[1024,2048]{1,0:T(8,128)(2,1)} custom-call(bf16[1024,1024]{1,0:T(8,128)(2,1)} %get-tuple-element.106.refs_0_.refs_1_, bf16[1024,2048]{1,0:T(8,128)(2,1)} %get-tuple-element.85.grad_ref.refs_1_, bf16[1024,1024]{1,0:T(8,128)(2,1)} %get-tuple-element.105.refs_2_.refs_1_, bf16[1024,2048]{1,0:T(8,128)(2,1)} %gather_cot.1.grad_ref.refs_3_), custom_call_target="tpu_custom_call" | custom-call | flops 8589934592 | bytes 16777216 | tf_op jit(solution)/shard_map/weight_pass/pallas_call | solution.py:443
  651.1 14.3 %weight_pass.10 = bf16[1024,2048]{1,0:T(8,128)(2,1)} custom-call(bf16[1024,1024]{1,0:T(8,128)(2,1)} %get-tuple-element.107.refs_0_.refs_3_, bf16[1024,2048]{1,0:T(8,128)(2,1)} %constant_dynamic-update-slice_fusion.rows_ref.refs_1_, bf16[1024,1024]{1,0:T(8,128)(2,1)} %get-tuple-element.108.refs_2_.refs_3_, ...), custom_call_target="tpu_custom_call" | custom-call | flops 8589934592 | bytes 16777216 | tf_op jit(solution)/shard_map/weight_pass/pallas_call | solution.py:443
  667.4 14.8 %weight_pass.11 = bf16[1024,2048]{1,0:T(8,128)(2,1)} custom-call(bf16[1024,1024]{1,0:T(8,128)(2,1)} %get-tuple-element.109.refs_0_, bf16[1024,2048]{1,0:T(8,128)(2,1)} %get-tuple-element.85.grad_ref.refs_1_, bf16[1024,1024]{1,0:T(8,128)(2,1)} %get-tuple-element.103.refs_2_.refs_0_, bf16[1024,2048]{1,0:T(8,128)(2,1)} %gather_cot.1.grad_ref.refs_3_, ...), custom_call_target="tpu_custom_call" | custom-call | flops 8589934592 | bytes 20971520 | tf_op jit(solution)/shard_map/weight_pass/pallas_call | solution.py:443
  683.0 35.7 %row_pass.2 = (bf16[1024,2048]{1,0:T(8,128)(2,1)}, bf16[1024,2048]{1,0:T(8,128)(2,1)}) custom-call(s32[8]{0:T(128)} %stack.65.starts_ref, bf16[1024,1024]{1,0:T(8,128)(2,1)} %get-tuple-element.109.refs_0_, bf16[1024,1024]{1,0:T(8,128)(2,1)} %get-tuple-element.106.refs_0_.refs_1_, bf16[1024,1024]{1,0:T(8,128)(2,1)} %get-tuple-element.118.refs_2_.refs_0_, ...), custom_call_target="tpu_custom_call" | custom-call | flops 25769803776 | bytes 46137344 | tf_op jit(solution)/shard_map/row_pass/pallas_call | solution.py:398
  718.7 14.4 %weight_pass.12 = bf16[1024,2048]{1,0:T(8,128)(2,1)} custom-call(bf16[1024,1024]{1,0:T(8,128)(2,1)} %get-tuple-element.116.refs_5_.refs_0_, bf16[1024,2048]{1,0:T(8,128)(2,1)} %constant_dynamic-update-slice_fusion.rows_ref.refs_1_, bf16[1024,1024]{1,0:T(8,128)(2,1)} %get-tuple-element.117.refs_2_.refs_5_, ...), custom_call_target="tpu_custom_call" | custom-call | flops 8589934592 | bytes 16777216 | tf_op jit(solution)/shard_map/weight_pass/pallas_call | solution.py:443
  733.1 14.8 %weight_pass.13 = bf16[1024,2048]{1,0:T(8,128)(2,1)} custom-call(bf16[1024,1024]{1,0:T(8,128)(2,1)} %get-tuple-element.118.refs_2_.refs_0_, bf16[1024,2048]{1,0:T(8,128)(2,1)} %constant_dynamic-update-slice_fusion.rows_ref.refs_1_, bf16[1024,1024]{1,0:T(8,128)(2,1)} %get-tuple-element.119.refs_2_, ...), custom_call_target="tpu_custom_call" | custom-call | flops 8589934592 | bytes 20971520 | tf_op jit(solution)/shard_map/weight_pass/pallas_call | solution.py:443
  758.3 35.1 %row_pass.3 = (bf16[1024,2048]{1,0:T(8,128)(2,1)}, bf16[1024,2048]{1,0:T(8,128)(2,1)}) custom-call(s32[8]{0:T(128)} %stack.65.starts_ref, bf16[1024,1024]{1,0:T(8,128)(2,1)} %get-tuple-element.103.refs_2_.refs_0_, bf16[1024,1024]{1,0:T(8,128)(2,1)} %get-tuple-element.105.refs_2_.refs_1_, bf16[1024,1024]{1,0:T(8,128)(2,1)} %get-tuple-element.119.refs_2_, ...), custom_call_target="tpu_custom_call" | custom-call | flops 25769803776 | bytes 46137344 | tf_op jit(solution)/shard_map/row_pass/pallas_call | solution.py:398
  801.3 18.1 %collective-permute-done.17 = bf16[256,2048]{1,0:T(8,128)(2,1)S(1)} collective-permute-done((bf16[256,2048]{1,0:T(8,128)(2,1)S(1)}, bf16[256,2048]{1,0:T(8,128)(2,1)S(1)}, u32[]{:S(2)}, u32[]{:S(2)}) %collective-permute-start.17) | collective-permute-done | bytes 1048608 | tf_op jit(solution)/shard_map/ppermute | solution.py:607
  832.3 10.4 collective-permute-done.18
  856.8 28.7 %all_to_all.20 = bf16[8,256,256]{2,1,0:T(8,128)(2,1)S(1)} all-to-all(bf16[8,256,256]{2,1,0:T(8,128)(2,1)S(1)} %bitcast.164), channel_id=1, replica_groups=mesh['rep'=2,'dp'=4,'seq'=4] {'rep','seq'}, dimensions={0} | all-to-all | bytes 2097152 | tf_op jit(solution)/shard_map/all_to_all | solution.py:1438
  885.5 25.1 %attend_back.2 = (bf16[2048,768]{1,0:T(8,128)(2,1)S(1)}, f32[2,1,128]{2,1,0:T(1,128)S(1)}) custom-call(s32[1]{0:T(128)} %bitcast.1.length_ref, f32[2]{0:T(128)S(1)} %dynamic_slice.43.gate_ref, bf16[2048,768]{1,0:T(8,128)(2,1)S(1)} %copy-done.29, bf16[2048,768]{1,0:T(8,128)(2,1)S(1)} %copy-done.29, bf16[2048,768]{1,0:T(8,128)(2,1)S(1)} %copy-done.29, ...), custom_call_target="tpu_custom_call" | custom-call | flops 10737418240 | bytes 10485760 | tf_op jit(solution)/shard_map/attend_back/pallas_call | solution.py:286
  912.3 14.8 %weight_pass.14 = bf16[1024,2048]{1,0:T(8,128)(2,1)} custom-call(bf16[1024,1024]{1,0:T(8,128)(2,1)} %get-tuple-element.127.refs_4_.refs_0_, bf16[1024,2048]{1,0:T(8,128)(2,1)} %constant_dynamic-update-slice_fusion.rows_ref.refs_1_, bf16[1024,1024]{1,0:T(8,128)(2,1)} %get-tuple-element.120.refs_4_.refs_2_, ...), custom_call_target="tpu_custom_call" | custom-call | flops 8589934592 | bytes 20971520 | tf_op jit(solution)/shard_map/weight_pass/pallas_call | solution.py:443
  949.3 42.2 %all-to-all-done.3 = bf16[8,256,256]{2,1,0:T(8,128)(2,1)S(1)} async-done(((bf16[8,256,256]{2,1,0:T(8,128)(2,1)}), bf16[8,256,256]{2,1,0:T(8,128)(2,1)S(1)}, u32[]{:S(2)}, u32[]{:S(2)}) %all-to-all-start.3) | async-done | bytes 1048608 | tf_op jit(solution)/shard_map/all_to_all | solution.py:1438
  998.5 20.3 %attend_back.3 = (bf16[2048,768]{1,0:T(8,128)(2,1)S(1)}, f32[2,1,128]{2,1,0:T(1,128)S(1)}) custom-call(s32[1]{0:T(128)} %bitcast.23.length_ref, f32[2]{0:T(128)S(1)} %copy-done.25, bf16[2048,768]{1,0:T(8,128)(2,1)S(1)} %copy-done.27, bf16[2048,768]{1,0:T(8,128)(2,1)S(1)} %copy-done.27, bf16[2048,768]{1,0:T(8,128)(2,1)S(1)} %copy-done.27, ...), custom_call_target="tpu_custom_call" | custom-call | flops 10737418240 | bytes 10485760 | tf_op jit(solution)/shard_map/attend_back/pallas_call | solution.py:286
  1048.2 21.4 %weight_pass.15 = bf16[768,2048]{1,0:T(8,128)(2,1)} custom-call(bf16[2048,768]{1,0:T(8,128)(2,1)} %copy-done.6, bf16[2048,2048]{1,0:T(8,128)(2,1)} %copy-done.30, bf16[2048,768]{1,0:T(8,128)(2,1)} %copy-done.9, bf16[2048,2048]{1,0:T(8,128)(2,1)} %copy-done.31), custom_call_target="tpu_custom_call" | custom-call | flops 12884901888 | bytes 26214400 | tf_op jit(solution)/shard_map/weight_pass/pallas_call | solution.py:443
  1103.0 212.9 %spread_sums.1 = (f32[2,256,2048]{2,1,0:T(8,128)}, bf16[384,2048]{1,0:T(8,128)(2,1)}, bf16[2,128,1024]{2,1,0:T(8,128)(2,1)}) custom-call(bf16[4,256,2048]{2,1,0:T(8,128)(2,1)} %bitcast.146, bf16[4,256,2048]{2,1,0:T(8,128)(2,1)} %bitcast.145, bf16[3,256,2048]{2,1,0:T(8,128)(2,1)} %bitcast.168, bf16[4,4,128,1024]{3,2,1,0:T(8,128)(2,1)} %bitcast.160), custom_call_target="tpu_custom_call" | custom-call | bytes 134217728 | tf_op jit(solution)/shard_map/spread_sums/pallas_call | solution.py:1184
  (374 shorter events, 317.5 us)
Async XLA Ops:
  7.2 97.9 %all-gather.15.cloned.1.call-start = ((), (), s32[]{:S(2)}) async-start(), calls=%async_computation.18 | async-start | bytes 9437184 | tf_op jit(solution)/shard_map/all_gather | solution.py:1259
  10.5 207.7 %all-gather.7.cloned.1.call-start = ((), (), s32[]{:S(2)}) async-start(), calls=%async_computation.9 | async-start | bytes 9437184 | tf_op jit(solution)/shard_map/all_gather | solution.py:1259
  105.1 315.4 %all-gather.9.cloned.1.call-start = ((), (), s32[]{:S(2)}) async-start(), calls=%async_computation.10 | async-start | bytes 10485760 | tf_op jit(solution)/shard_map/all_gather | solution.py:1321
  308.2 59.9 %all-to-all-start = ((bf16[8,256,256]{2,1,0:T(8,128)(2,1)}), bf16[8,256,256]{2,1,0:T(8,128)(2,1)}, u32[]{:S(2)}, u32[]{:S(2)}) async-start(bf16[8,256,256]{2,1,0:T(8,128)(2,1)} %bitcast.12), calls=%async_computation | async-start | bytes 2097152 | tf_op jit(solution)/shard_map/all_to_all | solution.py:1329
  315.9 177.7 %all-gather.11.cloned.1.call-start = ((), (), s32[]{:S(2)}) async-start(), calls=%async_computation.11 | async-start | bytes 5242880 | tf_op jit(solution)/shard_map/all_gather | solution.py:1371
  315.9 100.9 %collective-permute-start = (bf16[2048,1024]{1,0:T(8,128)(2,1)}, bf16[2048,1024]{1,0:T(8,128)(2,1)}, u32[]{:S(2)}, u32[]{:S(2)}) collective-permute-start(bf16[2048,1024]{1,0:T(8,128)(2,1)} %get-tuple-element.91), channel_id=1, source_target_pairs={{0,16},{16,0},{1,17},{17,1},{2,18},{18,2},{3,19},{19,3},{4,20},{20... | collective-permute-start | bytes 12582920 | tf_op jit(solution)/shard_map/ppermute | solution.py:512
  368.1 43.2 %all-to-all-start.1 = ((bf16[8,256,256]{2,1,0:T(8,128)(2,1)}), bf16[8,256,256]{2,1,0:T(8,128)(2,1)S(1)}, u32[]{:S(2)}, u32[]{:S(2)}) async-start(bf16[8,256,256]{2,1,0:T(8,128)(2,1)} %bitcast.26), calls=%async_computation.1 | async-start | bytes 2097152 | tf_op jit(solution)/shard_map/all_to_all | solution.py:1329
  374.0 384.2 %reduce-scatter.6.cloned.1.call-start = ((), (), s32[]{:S(2)}) async-start(), calls=%async_computation.12 | async-start | bytes 5242880 | tf_op jit(solution)/shard_map/reduce_scatter | solution.py:1394
  420.5 155.4 %collective-permute-start.7 = (bf16[1024,4096]{1,0:T(8,128)(2,1)}, bf16[1024,4096]{1,0:T(8,128)(2,1)}, u32[]{:S(2)}, u32[]{:S(2)}) collective-permute-start(bf16[1024,4096]{1,0:T(8,128)(2,1)} %all-gather.9.cloned.1.call-done.inner_ref.refs_6_.refs_8_), channel_id=1, source_target_pairs={{0,16},{16,0},{1,17},{17,1},{2,18},{18,2},{3,19},{19,3},{4,20},{20... | collective-permute-start | bytes 25165832 | tf_op jit(solution)/shard_map/ppermute | solution.py:512
  434.9 59.4 %collective-permute-start.1 = (bf16[128,2048]{1,0:T(8,128)(2,1)S(1)}, bf16[128,2048]{1,0:T(8,128)(2,1)}, u32[]{:S(2)}, u32[]{:S(2)}) collective-permute-start(bf16[128,2048]{1,0:T(8,128)(2,1)S(1)} %get-tuple-element.230), channel_id=1, source_target_pairs={{0,8},{4,12},{8,0},{12,4},{1,9},{5,13},{9,1},{13,5},{2,10},{6,14},... | collective-permute-start | bytes 1572872 | tf_op jit(solution)/shard_map/ppermute | solution.py:593
  434.9 60.6 %collective-permute-start.5 = (bf16[128,2048]{1,0:T(8,128)(2,1)S(1)}, bf16[128,2048]{1,0:T(8,128)(2,1)}, u32[]{:S(2)}, u32[]{:S(2)}) collective-permute-start(bf16[128,2048]{1,0:T(8,128)(2,1)S(1)} %get-tuple-element.228), channel_id=1, source_target_pairs={{0,8},{4,12},{8,0},{12,4},{1,9},{5,13},{9,1},{13,5},{2,10},{6,14},... | collective-permute-start | bytes 1572872 | tf_op jit(solution)/shard_map/ppermute | solution.py:593
  448.6 50.0 %collective-permute-start.3 = (bf16[128,2048]{1,0:T(8,128)(2,1)S(1)}, bf16[128,2048]{1,0:T(8,128)(2,1)}, u32[]{:S(2)}, u32[]{:S(2)}) collective-permute-start(bf16[128,2048]{1,0:T(8,128)(2,1)S(1)} %collective-permute-done.2), channel_id=1, source_target_pairs={{0,8},{4,12},{8,0},{12,4},{1,9},{5,13},{9,1},{13,5},{2,10},{6,14},... | collective-permute-start | bytes 1572872 | tf_op jit(solution)/shard_map/ppermute | solution.py:593
  493.6 82.3 %collective-permute-start.8 = (bf16[1024,2048]{1,0:T(8,128)(2,1)}, bf16[1024,2048]{1,0:T(8,128)(2,1)}, u32[]{:S(2)}, u32[]{:S(2)}) collective-permute-start(bf16[1024,2048]{1,0:T(8,128)(2,1)} %all-gather.11.cloned.1.call-done.down_ref.refs_10_), channel_id=1, source_target_pairs={{0,16},{16,0},{1,17},{17,1},{2,18},{18,2},{3,19},{19,3},{4,20},{20... | collective-permute-start | bytes 12582920 | tf_op jit(solution)/shard_map/ppermute | solution.py:512
  502.3 28.0 %collective-permute-start.10 = (bf16[128,2048]{1,0:T(8,128)(2,1)S(1)}, bf16[128,2048]{1,0:T(8,128)(2,1)S(1)}, u32[]{:S(2)}, u32[]{:S(2)}) collective-permute-start(bf16[128,2048]{1,0:T(8,128)(2,1)S(1)} %get-tuple-element.235), channel_id=1, source_target_pairs={{0,4},{4,0},{8,12},{12,8},{1,5},{5,1},{9,13},{13,9},{2,6},{6,2},{1... | collective-permute-start | bytes 1572872 | tf_op jit(solution)/shard_map/ppermute | solution.py:593
  520.0 31.5 %collective-permute-start.9 = (bf16[128,2048]{1,0:T(8,128)(2,1)S(1)}, bf16[128,2048]{1,0:T(8,128)(2,1)S(1)}, u32[]{:S(2)}, u32[]{:S(2)}) collective-permute-start(bf16[128,2048]{1,0:T(8,128)(2,1)S(1)} %get-tuple-element.235), channel_id=1, source_target_pairs={{0,8},{4,12},{8,0},{12,4},{1,9},{5,13},{9,1},{13,5},{2,10},{6,14},... | collective-permute-start | bytes 1572872 | tf_op jit(solution)/shard_map/ppermute | solution.py:593
  521.2 31.5 %collective-permute-start.13 = (bf16[128,2048]{1,0:T(8,128)(2,1)S(1)}, bf16[128,2048]{1,0:T(8,128)(2,1)S(1)}, u32[]{:S(2)}, u32[]{:S(2)}) collective-permute-start(bf16[128,2048]{1,0:T(8,128)(2,1)S(1)} %get-tuple-element.233), channel_id=1, source_target_pairs={{0,8},{4,12},{8,0},{12,4},{1,9},{5,13},{9,1},{13,5},{2,10},{6,14},... | collective-permute-start | bytes 1572872 | tf_op jit(solution)/shard_map/ppermute | solution.py:593
  682.2 355.1 %reduce-scatter.14.cloned.1.call-start = ((), (), s32[]{:S(2)}) async-start(), calls=%async_computation.17 | async-start | bytes 5242880 | tf_op jit(solution)/shard_map/reduce_scatter | solution.py:1394
  682.3 50.8 %collective-permute-start.16 = (bf16[1024,2048]{1,0:T(8,128)(2,1)}, bf16[1024,2048]{1,0:T(8,128)(2,1)}, u32[]{:S(2)}, u32[]{:S(2)}) collective-permute-start(bf16[1024,2048]{1,0:T(8,128)(2,1)} %weight_pass.10), channel_id=1, source_target_pairs={{0,16},{16,0},{1,17},{17,1},{2,18},{18,2},{3,19},{19,3},{4,20},{20... | collective-permute-start | bytes 12582920 | tf_op jit(solution)/shard_map/ppermute | solution.py:512
  747.9 349.2 %reduce-scatter.8.cloned.1.call-start = ((), (), s32[]{:S(2)}) async-start(), calls=%async_computation.13 | async-start | bytes 5242880 | tf_op jit(solution)/shard_map/reduce_scatter | solution.py:1488
  749.7 47.9 %collective-permute-start.21 = (bf16[256,2048]{1,0:T(8,128)(2,1)S(1)}, bf16[256,2048]{1,0:T(8,128)(2,1)}, u32[]{:S(2)}, u32[]{:S(2)}) collective-permute-start(bf16[256,2048]{1,0:T(8,128)(2,1)S(1)} %get-tuple-element.214), channel_id=1, source_target_pairs={{0,4},{4,0},{8,12},{12,8},{1,5},{5,1},{9,13},{13,9},{2,6},{6,2},{1... | collective-permute-start | bytes 3145736 | tf_op jit(solution)/shard_map/ppermute | solution.py:607
  750.9 46.7 %collective-permute-start.23 = (bf16[256,2048]{1,0:T(8,128)(2,1)S(1)}, bf16[256,2048]{1,0:T(8,128)(2,1)}, u32[]{:S(2)}, u32[]{:S(2)}) collective-permute-start(bf16[256,2048]{1,0:T(8,128)(2,1)S(1)} %get-tuple-element.215), channel_id=1, source_target_pairs={{0,8},{4,12},{8,0},{12,4},{1,9},{5,13},{9,1},{13,5},{2,10},{6,14},... | collective-permute-start | bytes 3145736 | tf_op jit(solution)/shard_map/ppermute | solution.py:607
  800.2 31.4 %collective-permute-start.22 = (bf16[128,2048]{1,0:T(8,128)(2,1)S(1)}, bf16[128,2048]{1,0:T(8,128)(2,1)S(1)}, u32[]{:S(2)}, u32[]{:S(2)}) collective-permute-start(bf16[128,2048]{1,0:T(8,128)(2,1)S(1)} %slice.252), channel_id=1, source_target_pairs={{0,8},{4,12},{8,0},{12,4},{1,9},{5,13},{9,1},{13,5},{2,10},{6,14},... | collective-permute-start | bytes 1572872 | tf_op jit(solution)/shard_map/ppermute | solution.py:607
  800.6 31.5 %collective-permute-start.24 = (bf16[128,2048]{1,0:T(8,128)(2,1)S(1)}, bf16[128,2048]{1,0:T(8,128)(2,1)S(1)}, u32[]{:S(2)}, u32[]{:S(2)}) collective-permute-start(bf16[128,2048]{1,0:T(8,128)(2,1)S(1)} %slice.251), channel_id=1, source_target_pairs={{0,4},{4,0},{8,12},{12,8},{1,5},{5,1},{9,13},{13,9},{2,6},{6,2},{1... | collective-permute-start | bytes 1572872 | tf_op jit(solution)/shard_map/ppermute | solution.py:607
  848.3 252.0 %reduce-scatter.12.cloned.1.call-start = ((), (), s32[]{:S(2)}) async-start(), calls=%async_computation.15 | async-start | bytes 5242880 | tf_op jit(solution)/shard_map/reduce_scatter | solution.py:1394
  848.4 64.0 %collective-permute-start.25 = (bf16[1024,2048]{1,0:T(8,128)(2,1)}, bf16[1024,2048]{1,0:T(8,128)(2,1)}, u32[]{:S(2)}, u32[]{:S(2)}) collective-permute-start(bf16[1024,2048]{1,0:T(8,128)(2,1)} %weight_pass.12), channel_id=1, source_target_pairs={{0,16},{16,0},{1,17},{17,1},{2,18},{18,2},{3,19},{19,3},{4,20},{20... | collective-permute-start | bytes 12582920 | tf_op jit(solution)/shard_map/ppermute | solution.py:512
  933.2 58.3 %all-to-all-start.3 = ((bf16[8,256,256]{2,1,0:T(8,128)(2,1)}), bf16[8,256,256]{2,1,0:T(8,128)(2,1)S(1)}, u32[]{:S(2)}, u32[]{:S(2)}) async-start(bf16[8,256,256]{2,1,0:T(8,128)(2,1)} %bitcast.142), calls=%async_computation.7 | async-start | bytes 2097152 | tf_op jit(solution)/shard_map/all_to_all | solution.py:1438
  939.5 163.5 %reduce-scatter.10.cloned.1.call-start = ((), (), s32[]{:S(2)}) async-start(), calls=%async_computation.14 | async-start | bytes 5242880 | tf_op jit(solution)/shard_map/reduce_scatter | solution.py:1488
  940.3 407.3 %all-gather.13.cloned.1.call-start = ((), (), s32[]{:S(2)}) async-start(), calls=%async_computation.16 | async-start | bytes 2162688 | tf_op jit(solution)/shard_map/all_gather | solution.py:1545
  949.0 120.6 %collective-permute-start.28 = (bf16[2048,1024]{1,0:T(8,128)(2,1)}, bf16[2048,1024]{1,0:T(8,128)(2,1)}, u32[]{:S(2)}, u32[]{:S(2)}) collective-permute-start(bf16[2048,1024]{1,0:T(8,128)(2,1)} %weight_pass.16), channel_id=1, source_target_pairs={{0,16},{16,0},{1,17},{17,1},{2,18},{18,2},{3,19},{19,3},{4,20},{20... | collective-permute-start | bytes 12582920 | tf_op jit(solution)/shard_map/ppermute | solution.py:512
  1027.2 51.6 %collective-permute-start.27 = (bf16[1024,2048]{1,0:T(8,128)(2,1)}, bf16[1024,2048]{1,0:T(8,128)(2,1)}, u32[]{:S(2)}, u32[]{:S(2)}) collective-permute-start(bf16[1024,2048]{1,0:T(8,128)(2,1)} %get-tuple-element.139), channel_id=1, source_target_pairs={{0,16},{16,0},{1,17},{17,1},{2,18},{18,2},{3,19},{19,3},{4,20},{20... | collective-permute-start | bytes 12582920 | tf_op jit(solution)/shard_map/ppermute | solution.py:512
  1035.0 51.0 %collective-permute-start.26 = (bf16[1024,2048]{1,0:T(8,128)(2,1)}, bf16[1024,2048]{1,0:T(8,128)(2,1)}, u32[]{:S(2)}, u32[]{:S(2)}) collective-permute-start(bf16[1024,2048]{1,0:T(8,128)(2,1)} %get-tuple-element.133), channel_id=1, source_target_pairs={{0,16},{16,0},{1,17},{17,1},{2,18},{18,2},{3,19},{19,3},{4,20},{20... | collective-permute-start | bytes 12582920 | tf_op jit(solution)/shard_map/ppermute | solution.py:512
  1102.6 240.7 %collective-permute-start.29 = (bf16[256,4096]{1,0:T(8,128)(2,1)}, bf16[256,4096]{1,0:T(8,128)(2,1)}, u32[]{:S(2)}, u32[]{:S(2)}) collective-permute-start(bf16[256,4096]{1,0:T(8,128)(2,1)} %constant_dynamic-update-slice_fusion.16), channel_id=1, source_target_pairs={{0,16},{16,0},{1,17},{17,1},{2,18},{18,2},{3,19},{19,3},{4,20},{20... | collective-permute-start | bytes 6291464 | tf_op jit(solution)/shard_map/ppermute | solution.py:512
  (98 other events, 3201.4 us)
Sparse Core Ops, SparseCore 0:
  10.6 94.3 all-gather.14
  107.2 102.4 all-gather.6
  218.4 192.7 all-gather.8
  413.2 80.3 all-gather.10
  682.3 75.8 reduce-scatter.5
  760.5 77.2 reduce-scatter.13
  848.4 54.4 reduce-scatter.7
  927.3 96.2 reduce-scatter.11
  1026.6 52.6 reduce-scatter.9
  1103.1 104.0 all-gather.12

commit v4 on v3

--- a/solution.py
+++ b/solution.py
@@ -364,53 +364,6 @@
         ),
         name="unit_pass",
     )(rows, grads, inner, down)
-
-
-def row_kernel(starts_ref, *refs):
-    hidden, gates, ups, gate_w, up_w, down_w = (refs[2 * i : 2 * i + 2] for i in range(6))
-    out_ref, grad_two_ref = refs[12:]
-    grad_two_ref[...] = (
-        nn(gates[0][...], gate_w[0][...])
-        + nn(gates[1][...], gate_w[1][...])
-        + nn(ups[0][...], up_w[0][...])
-        + nn(ups[1][...], up_w[1][...])
-    ).astype(BF16)
-    out = (
-        nn(hidden[0][...], down_w[0][...]) + nn(hidden[1][...], down_w[1][...])
-    ).astype(BF16)
-    pieces = starts_ref.shape[0]
-    size = out.shape[0] // pieces
-    for i in range(pieces):
-        start = pl.multiple_of(starts_ref[i], size)
-        out_ref[pl.ds(start, size), :] = out[i * size : (i + 1) * size]
-
-
-def row_pass(starts, hidden, grad_gates, grad_ups, inner, down):
-    count, units = hidden[0].shape
-    width = down[0].shape[1]
-    tile = min(256, width)
-    tiles = width // tile
-    resident = pl.BlockSpec((count, units), lambda t: (0, 0), pipeline_mode=pl.Buffered(1))
-    low = pl.BlockSpec((units, tile), lambda t: (0, t))
-    high = pl.BlockSpec((units, tile), lambda t: (0, tiles + t))
-    column = pl.BlockSpec((count, tile), lambda t: (0, t))
-    row_shape = jax.ShapeDtypeStruct((count, width), BF16)
-    return pl.pallas_call(
-        row_kernel,
-        grid=(tiles,),
-        in_specs=[pl.BlockSpec(memory_space=pltpu.SMEM)]
-        + [resident] * 6
-        + [low, low, high, high, low, low],
-        out_specs=[column] * 2,
-        out_shape=[row_shape] * 2,
-        compiler_params=pltpu.CompilerParams(vmem_limit_bytes=56 << 20),
-        cost_estimate=pl.CostEstimate(
-            flops=2 * 3 * count * width * 2 * units,
-            bytes_accessed=12 * units * (width + count) + 4 * count * width,
-            transcendentals=0,
-        ),
-        name="row_pass",
-    )(starts, *hidden, *grad_gates, *grad_ups, *inner, *inner, *down)
 
 
 def weight_kernel(pairs, *refs):
@@ -915,6 +868,115 @@
         ),
         name="gather_rest",
     )(out_half, cot)
+
+
+def row_kernel(count, *refs):
+    hidden, gates, ups, gate_w, up_w, down_w = (refs[2 * i : 2 * i + 2] for i in range(6))
+    out_ref, grad_ref, parts, landed, sent, here = refs[12:]
+    step, steps = pl.program_id(0), pl.num_programs(0)
+    core, column, place = lax.axis_index("rep"), lax.axis_index("dp"), lax.axis_index("seq")
+    cube = [(core, flipped(column, k), place) for k in range(1, count)]
+
+    @pl.when(step == 0)
+    def _():
+        greet(cube)
+
+    size = out_ref.shape[0] // (2 * count)
+    spots = [
+        (side, at, order_k)
+        for side, bits in enumerate(cube_bits(count))
+        for at, order_k in enumerate(cube_order(bits))
+    ]
+
+    def piece(side, at):
+        return pl.ds((side * count + at) * size, size)
+
+    def leaving(t, side, at, k):
+        number = side * (count - 1) + k - 1
+        flat = t * (2 * (count - 1)) + number
+        return remote(
+            parts.at[t, piece(side, at)],
+            landed.at[t, number],
+            sent.at[flat],
+            here.at[flat],
+            cube[k - 1],
+        )
+
+    parts[step] = (
+        nn(gates[0][...], gate_w[0][...])
+        + nn(gates[1][...], gate_w[1][...])
+        + nn(ups[0][...], up_w[0][...])
+        + nn(ups[1][...], up_w[1][...])
+    ).astype(BF16)
+    for side, at, k in spots:
+        if k:
+            leaving(step, side, at, k).start()
+    out = (
+        nn(hidden[0][...], down_w[0][...]) + nn(hidden[1][...], down_w[1][...])
+    ).astype(BF16)
+    for side, at, k in spots:
+        owner = flipped(column, k) if k else column
+        start = pl.multiple_of((2 * owner + side) * size, size)
+        out_ref[pl.ds(start, size), :] = out[(side * count + at) * size :][:size]
+
+    @pl.when(step == steps - 1)
+    def _():
+        width = parts.shape[2]
+
+        def finish(t, _):
+            for side, at, k in spots:
+                if k:
+                    leaving(t, side, at, k).wait()
+            columns = pl.ds(pl.multiple_of(t * width, width), width)
+            for side in range(2):
+                total = parts[t, piece(side, 0), :].astype(F32)
+                for k in range(1, count):
+                    total += landed[t, side * (count - 1) + k - 1].astype(F32)
+                grad_ref[side * size : (side + 1) * size, columns] = total
+            return 0
+
+        lax.fori_loop(0, steps, finish, 0)
+
+
+def row_pass(hidden, grad_gates, grad_ups, inner, down, dp_count):
+    count, units = hidden[0].shape
+    width = down[0].shape[1]
+    tile = min(256, width)
+    tiles = width // tile
+    pieces = 2 * (dp_count - 1)
+    size = count // (2 * dp_count)
+    resident = pl.BlockSpec((count, units), lambda t: (0, 0), pipeline_mode=pl.Buffered(1))
+    low = pl.BlockSpec((units, tile), lambda t: (0, t))
+    high = pl.BlockSpec((units, tile), lambda t: (0, tiles + t))
+    dma = pltpu.SemaphoreType.DMA
+    return pl.pallas_call(
+        functools.partial(row_kernel, dp_count),
+        grid=(tiles,),
+        in_specs=[resident] * 6 + [low, low, high, high, low, low],
+        out_specs=[
+            pl.BlockSpec((count, tile), lambda t: (0, t)),
+            pl.BlockSpec((2 * size, width), lambda t: (0, 0)),
+        ],
+        out_shape=[
+            jax.ShapeDtypeStruct((count, width), BF16),
+            jax.ShapeDtypeStruct((2 * size, width), F32),
+        ],
+        scratch_shapes=[
+            pltpu.VMEM((tiles, count, tile), BF16),
+            pltpu.VMEM((tiles, pieces, size, tile), BF16),
+            dma((tiles * pieces,)),
+            dma((tiles * pieces,)),
+        ],
+        compiler_params=pltpu.CompilerParams(
+            collective_id=4, has_side_effects=True, vmem_limit_bytes=56 << 20
+        ),
+        cost_estimate=pl.CostEstimate(
+            flops=2 * 3 * count * width * 2 * units,
+            bytes_accessed=12 * units * (width + count) + 4 * count * width,
+            transcendentals=0,
+        ),
+        name="row_pass",
+    )(*hidden, *grad_gates, *grad_ups, *inner, *inner, *down)
 
 
 def add_rows(out_ref, refs, size):
@@ -1368,11 +1430,8 @@
             )
         )
 
-    down_near = lax.all_gather(
-        near_downs,
-        "seq",
-        axis=0,
-        tiled=True,
+    down_near = after(
+        lax.all_gather(near_downs, "seq", axis=0, tiled=True), *[s["rows"] for s in saved]
     )
     inner_far, down_far = swap(inner_near), swap(down_near)
 
@@ -1385,39 +1444,31 @@
             last = halves[-1][0]
         s["hidden"], s["grad_gates"], s["grad_ups"] = zip(*halves)
 
-    def half_grads(left, right, half, earlier, extra=None):
+    def half_grads(left, right, half, extra, *earlier):
         pairs = [(s[left][half], s[right]) for s in saved]
-        pairs[0] = (after(pairs[0][0], earlier), pairs[0][1])
+        pairs[0] = (after(pairs[0][0], *earlier), pairs[0][1])
         return weight_pass(pairs, extra)
 
     def spread(values):
         return lax.psum_scatter(values, "seq", scatter_dimension=0, tiled=True)
 
-    starts = jnp.stack(
-        [
-            (column ^ k) * span_rows + side * (span_rows // 2)
-            for side, bits in enumerate(cube_bits(dp_count))
-            for k in cube_order(bits)
-        ]
-    ).astype(jnp.int32)
-
     def rows_out(s, *earlier):
         gates = (after(s["grad_gates"][0], *earlier), s["grad_gates"][1])
-        s["mlp_part"], s["grad_two_part"] = row_pass(
-            starts, s["hidden"], gates, s["grad_ups"], inner, down
-        )
-        return s["grad_two_part"]
-
-    down_far_sum = half_grads("hidden", "grads", 1, last)
-    gate_far_sum = half_grads("grad_gates", "rows", 1, down_far_sum)
-    down_sum = half_grads("hidden", "grads", 0, gate_far_sum, swap(down_far_sum))
+        s["mlp_part"], s["grad_two"] = row_pass(
+            s["hidden"], gates, s["grad_ups"], inner, down, dp_count
+        )
+        return s["grad_two"]
+
+    down_far_sum = half_grads("hidden", "grads", 1, None, last)
+    gate_far_sum = half_grads("grad_gates", "rows", 1, None, down_far_sum)
+    down_sum = half_grads("hidden", "grads", 0, swap(down_far_sum), gate_far_sum)
     down_mine = spread(down_sum)
     last = rows_out(saved[0], down_sum)
-    up_far_sum = half_grads("grad_ups", "rows", 1, last)
-    gate_sum = half_grads("grad_gates", "rows", 0, up_far_sum, swap(gate_far_sum))
+    up_far_sum = half_grads("grad_ups", "rows", 1, None, last)
+    gate_sum = half_grads("grad_gates", "rows", 0, swap(gate_far_sum), up_far_sum)
     gate_mine = spread(gate_sum)
-    def rows_back(s, pins):
-        grad_two = cube_scatter(s["grad_two_part"], "dp", pins)
+    def rows_back(s):
+        grad_two = s["grad_two"]
         grad_scaled = grad_two * gain_two
         normed_two = s["normed_two"]
         s["grad_after"] = s["live"] + s["scale_two"] * (
@@ -1435,13 +1486,12 @@
             ],
             axis=1,
         )
-        return lax.all_to_all(
-            jnp.swapaxes(grad_mixed.reshape(span_rows, span_count, block_rows), 0, 1),
-            ("rep", "seq"),
-            0,
-            0,
-            tiled=True,
-        ).reshape(total, block_rows)
+        s["grad_mixed"] = jnp.swapaxes(
+            grad_mixed.reshape(span_rows, span_count, block_rows), 0, 1
+        )
+        return lax.all_to_all(s["grad_mixed"], ("rep", "seq"), 0, 0, tiled=True).reshape(
+            total, block_rows
+        )
 
     def heads_back(s, m, grad_heads):
         s["grad_projected"], gate_sums = attend_back(
@@ -1478,11 +1528,11 @@
             )
         ).astype(BF16)
 
-    heads_grads = [rows_back(saved[0], ())]
+    heads_grads = [rows_back(saved[0])]
     last = gate_sum
     for m, s in enumerate(saved[1:]):
         last = rows_out(s, last, down_mine)
-        heads_grads.append(rows_back(s, ()))
+        heads_grads.append(rows_back(s))
 
     def spread_out(s, *earlier):
         return lax.psum_scatter(
@@ -1490,13 +1540,15 @@
         )
 
     mlp_outs, sums = [spread_out(saved[0], saved[-1]["grad_branch"])], []
-    last = after(last, gate_mine)
+    earlier = (saved[-1]["grad_mixed"], gate_mine)
     for m, s in enumerate(saved):
-        sums.append(heads_back(s, m, after(heads_grads[m], last)))
+        sums.append(heads_back(s, m, after(heads_grads[m], *earlier)))
         if m == 0:
-            up_sum = half_grads("grad_ups", "rows", 0, s["grad_projected"], swap(up_far_sum))
+            up_sum = half_grads(
+                "grad_ups", "rows", 0, swap(up_far_sum), s["grad_projected"], heads_grads[-1]
+            )
             up_mine = spread(up_sum)
-            last = after(up_sum, mlp_outs[0])
+            earlier = (up_sum, mlp_outs[0])
         else:
             mlp_outs.append(spread_out(s, up_sum))
     out_far_sum = weight_pass([(s["grad_branch"], s["mixed_far"]) for s in saved])
@@ -1508,7 +1560,7 @@
     )
 
     grad_ones, qkv_done, out_done = spread_sums(
-        [after(p, up_mine, *mlp_outs).reshape(seq_count, span_rows, width) for p in sums],
+        [after(p, up_mine, mlp_outs[0]).reshape(seq_count, span_rows, width) for p in sums],
         qkv_low,
         out_sum.reshape(dp_count, seq_count, shard_out, half_width),
         (dp_count, seq_count, unit, per_shard, per_block, per_column),

time: 1370 us -> 1300 us (0.949)
  waiting for transfers between devices: 266 us -> 187 us
  Pallas kernels: 839 us -> 869 us
  blocking collectives: 28.7 us -> 0 us
    pallas_call x2, Pallas kernels: 70.7 us -> 122 us  [row_pass(): pl.pallas_call(functools.partial(row_kernel, dp_count), grid=(tiles,), in...]
    all_gather x1, waiting for transfers between devices: 45 us -> 0.01 us  [shards(): lax.all_gather(near_downs, 'seq', axis=0, tiled=True)]
    ppermute x8 -> x0, waiting for transfers between devices: 38.6 us -> none  [cube_scatter(): got = lax.ppermute(held[keep:].astype(BF16), axis, pairs)]
    reduce_scatter x2, waiting for transfers between devices: 0.02 us -> 34.3 us  [spread_out(): lax.psum_scatter(after(s['mlp_part'], *earlier), 'dp', scatter_dimension=...]
    all_to_all x1 -> x0, blocking collectives: 28.7 us -> none  [rows_back(): lax.all_to_all(jnp.swapaxes(grad_mixed.reshape(span_rows, span_count, blo...]
    all_to_all x1 -> x2, waiting for transfers between devices: 42.2 us -> 18 us  [rows_back(): lax.all_to_all(s['grad_mixed'], ('rep', 'seq'), 0, 0, tiled=True)]
    unnamed x186 -> x172, local copies, waits for them, and re-layouts: 53.9 us -> 63.1 us
  transfers between devices with their start and end apart: 44 -> 37, of which waited for: 17 -> 11; matrix products, arithmetic and copies ran while one was open for 9% -> 9% of each run, Pallas kernels for 55% -> 60%
where the time goes in v4:
time: 1300 us; the launch traced here: 1290 us
  Pallas kernels  869 us (67%)
  waiting for transfers between devices  187 us (14%)
  local copies, waits for them, and re-layouts  99.4 us (8%)
  starting transfers between devices  52.6 us (4%)
  other arithmetic  46.4 us (4%)
  matrix products  20.6 us (2%)
  between operations  15.7 us (1%)
    pallas_call x1, Pallas kernels, spread_sums(): pl.pallas_call(functools.partial(spread_kernel, sizes, micros), in_specs=...  212 us
    pallas_call x9, Pallas kernels, weight_pass(): pl.pallas_call(functools.partial(weight_kernel, len(pairs)), grid=(size /...  127 us
    pallas_call x2, Pallas kernels, row_pass(): pl.pallas_call(functools.partial(row_kernel, dp_count), grid=(tiles,), in...  122 us
    pallas_call x1, Pallas kernels, gather_rest(): pl.pallas_call(functools.partial(rest_kernel, sizes), in_specs=[anywhere]...  104 us
    pallas_call x4, Pallas kernels, unit_pass(): pl.pallas_call(unit_kernel, grid=(units // tile,), in_specs=[resident, re...  78.3 us
    unnamed x172, local copies, waits for them, and re-layouts  63.1 us
    pallas_call x1, Pallas kernels, gather_heads(): pl.pallas_call(functools.partial(heads_kernel, sizes), in_specs=[anywhere...  59.7 us
    all_to_all x2, waiting for transfers between devices, shards(): lax.all_to_all(mixed_heads.reshape(span_count, span_rows, block_rows), ('...  54 us
  transfers between devices with their start and end apart: 37, of which 11 were waited for; matrix products, arithmetic and copies ran while one was open for 9% of the time, Pallas kernels for 60%

profile of v4, /device:TPU:17, one launch (start us, length us, event | category | flops | bytes accessed | tf_op | source)
XLA Modules:
  0.0 1291.2 jit_solution(4127597246256393999)
XLA Ops:
  12.1 59.7 %gather_heads.1 = (bf16[768,2048]{1,0:T(8,128)(2,1)S(1)}, f32[16,8,128]{2,1,0:T(8,128)S(1)}) custom-call(bf16[384,2048]{1,0:T(8,128)(2,1)S(1)} %copy-done.13, f32[8,128]{1,0:T(8,128)S(1)} %pad_convert_fusion.gain_ref), custom_call_target="tpu_custom_call" | custom-call | bytes 33554432 | tf_op jit(solution)/shard_map/gather_heads/pallas_call | solution.py:715
  73.4 31.6 %all-gather.15.cloned.1.call-done = bf16[1,1,2048,2048]{3,2,1,0:T(8,128)(2,1)} async-done(((bf16[1,1,256,2048]{3,2,1,0:T(8,128)(2,1)}), bf16[1,1,2048,2048]{3,2,1,0:T(8,128)(2,1)}) %all-gather.15.cloned.1.call-update) | async-done | bytes 8388624 | tf_op jit(solution)/shard_map/all_gather | solution.py:1321
  114.3 104.1 %gather_rest.1 = (bf16[2048,1024]{1,0:T(8,128)(2,1)}, bf16[1024,2048]{1,0:T(8,128)(2,1)}) custom-call(bf16[128,1024]{1,0:T(8,128)(2,1)} %constant_dynamic-slice_fusion.9.refs_0_, bf16[256,2048]{1,0:T(8,128)(2,1)} %get-tuple-element.218.refs_1_), custom_call_target="tpu_custom_call" | custom-call | bytes 4194304 | tf_op jit(solution)/shard_map/gather_rest/pallas_call | solution.py:846
  221.1 47.4 %gather_cot.1.grad_ref.refs_3_ = bf16[1024,2048]{1,0:T(8,128)(2,1)} custom-call(bf16[256,2048]{1,0:T(8,128)(2,1)} %get-tuple-element.89.cot_ref), custom_call_target="tpu_custom_call" | custom-call | bytes 4194304 | tf_op jit(solution)/shard_map/gather_cot/pallas_call | solution.py:786
  270.4 11.3 project.2
  285.1 17.5 %attend.2 = (bf16[2048,256]{1,0:T(8,128)(2,1)}, f32[2048,256]{1,0:T(8,128)S(1)}, f32[2,1,2048]{2,1,0:T(1,128)S(1)}, f32[2,128,128]{2,1,0:T(8,128)S(1)}, f32[2,1,128]{2,1,0:T(1,128)S(1)}) custom-call(s32[1]{0:T(128)} %bitcast.1.length_ref, f32[2]{0:T(128)S(1)} %dynamic_slice.43.gate_ref, bf16[2048,768]{1,0:T(8,128)(2,1)S(1)} %get-tuple-element.92.q_ref.k_ref.v_ref, ...), custom_call_target="tpu_custom_call" | custom-call | flops 4294967296 | bytes 6291456 | tf_op jit(solution)/shard_map/attend/pallas_call | solution.py:156
  304.0 9.0 all-to-all-start
  315.2 11.3 project.3
  329.9 13.1 %attend.3 = (bf16[2048,256]{1,0:T(8,128)(2,1)}, f32[2048,256]{1,0:T(8,128)S(1)}, f32[2,1,2048]{2,1,0:T(1,128)S(1)}, f32[2,128,128]{2,1,0:T(8,128)S(1)}, f32[2,1,128]{2,1,0:T(1,128)S(1)}) custom-call(s32[1]{0:T(128)} %bitcast.15.length_ref, f32[2]{0:T(128)S(1)} %dynamic_slice.43.gate_ref, bf16[2048,768]{1,0:T(8,128)(2,1)S(1)} %get-tuple-element.97.q_ref.k_ref.v_ref, ...), custom_call_target="tpu_custom_call" | custom-call | flops 4294967296 | bytes 6291456 | tf_op jit(solution)/shard_map/attend/pallas_call | solution.py:156
  346.0 15.7 %all-to-all-done = bf16[8,256,256]{2,1,0:T(8,128)(2,1)} async-done(((bf16[8,256,256]{2,1,0:T(8,128)(2,1)}), bf16[8,256,256]{2,1,0:T(8,128)(2,1)}, u32[]{:S(2)}, u32[]{:S(2)}) %all-to-all-start) | async-done | bytes 1048608 | tf_op jit(solution)/shard_map/all_to_all | solution.py:1391
  372.2 38.3 %all-to-all-done.1 = bf16[8,256,256]{2,1,0:T(8,128)(2,1)} async-done(((bf16[8,256,256]{2,1,0:T(8,128)(2,1)}), bf16[8,256,256]{2,1,0:T(8,128)(2,1)}, u32[]{:S(2)}, u32[]{:S(2)}) %all-to-all-start.1) | async-done | bytes 1048608 | tf_op jit(solution)/shard_map/all_to_all | solution.py:1391
  432.8 10.8 collective-permute-done.2
  511.7 19.7 %unit_pass.4 = (bf16[1024,1024]{1,0:T(8,128)(2,1)}, bf16[1024,1024]{1,0:T(8,128)(2,1)}, bf16[1024,1024]{1,0:T(8,128)(2,1)}) custom-call(bf16[1024,2048]{1,0:T(8,128)(2,1)} %constant_dynamic-update-slice_fusion.rows_ref.refs_1_, bf16[1024,2048]{1,0:T(8,128)(2,1)} %get-tuple-element.88.grad_ref.refs_1_, ...), custom_call_target="tpu_custom_call" | custom-call | flops 12884901888 | bytes 27262976 | tf_op jit(solution)/shard_map/unit_pass/pallas_call | solution.py:348
  533.5 19.5 %unit_pass.5 = (bf16[1024,1024]{1,0:T(8,128)(2,1)}, bf16[1024,1024]{1,0:T(8,128)(2,1)}, bf16[1024,1024]{1,0:T(8,128)(2,1)}) custom-call(bf16[1024,2048]{1,0:T(8,128)(2,1)} %constant_dynamic-update-slice_fusion.rows_ref.refs_1_, bf16[1024,2048]{1,0:T(8,128)(2,1)} %get-tuple-element.88.grad_ref.refs_1_, ...), custom_call_target="tpu_custom_call" | custom-call | flops 12884901888 | bytes 27262976 | tf_op jit(solution)/shard_map/unit_pass/pallas_call | solution.py:348
  552.9 19.5 %unit_pass.6 = (bf16[1024,1024]{1,0:T(8,128)(2,1)}, bf16[1024,1024]{1,0:T(8,128)(2,1)}, bf16[1024,1024]{1,0:T(8,128)(2,1)}) custom-call(bf16[1024,2048]{1,0:T(8,128)(2,1)} %constant_dynamic-update-slice_fusion.8.rows_ref.refs_3_, bf16[1024,2048]{1,0:T(8,128)(2,1)} %gather_cot.1.grad_ref.refs_3_, ...), custom_call_target="tpu_custom_call" | custom-call | flops 12884901888 | bytes 27262976 | tf_op jit(solution)/shard_map/unit_pass/pallas_call | solution.py:348
  572.4 19.6 %unit_pass.7 = (bf16[1024,1024]{1,0:T(8,128)(2,1)}, bf16[1024,1024]{1,0:T(8,128)(2,1)}, bf16[1024,1024]{1,0:T(8,128)(2,1)}) custom-call(bf16[1024,2048]{1,0:T(8,128)(2,1)} %constant_dynamic-update-slice_fusion.8.rows_ref.refs_3_, bf16[1024,2048]{1,0:T(8,128)(2,1)} %gather_cot.1.grad_ref.refs_3_, ...), custom_call_target="tpu_custom_call" | custom-call | flops 12884901888 | bytes 27262976 | tf_op jit(solution)/shard_map/unit_pass/pallas_call | solution.py:348
  592.0 14.8 %weight_pass.9 = bf16[1024,2048]{1,0:T(8,128)(2,1)} custom-call(bf16[1024,1024]{1,0:T(8,128)(2,1)} %get-tuple-element.110.refs_0_.refs_1_, bf16[1024,2048]{1,0:T(8,128)(2,1)} %get-tuple-element.88.grad_ref.refs_1_, bf16[1024,1024]{1,0:T(8,128)(2,1)} %get-tuple-element.109.refs_2_.refs_1_, bf16[1024,2048]{1,0:T(8,128)(2,1)} %gather_cot.1.grad_ref.refs_3_), custom_call_target="tpu_custom_call" | custom-call | flops 8589934592 | bytes 16777216 | tf_op jit(solution)/shard_map/weight_pass/pallas_call | solution.py:396
  606.8 14.3 %weight_pass.10 = bf16[1024,2048]{1,0:T(8,128)(2,1)} custom-call(bf16[1024,1024]{1,0:T(8,128)(2,1)} %get-tuple-element.111.refs_0_.refs_3_, bf16[1024,2048]{1,0:T(8,128)(2,1)} %constant_dynamic-update-slice_fusion.rows_ref.refs_1_, bf16[1024,1024]{1,0:T(8,128)(2,1)} %get-tuple-element.112.refs_2_.refs_3_, ...), custom_call_target="tpu_custom_call" | custom-call | flops 8589934592 | bytes 16777216 | tf_op jit(solution)/shard_map/weight_pass/pallas_call | solution.py:396
  623.1 14.7 %weight_pass.11 = bf16[1024,2048]{1,0:T(8,128)(2,1)} custom-call(bf16[1024,1024]{1,0:T(8,128)(2,1)} %get-tuple-element.113.refs_0_, bf16[1024,2048]{1,0:T(8,128)(2,1)} %get-tuple-element.88.grad_ref.refs_1_, bf16[1024,1024]{1,0:T(8,128)(2,1)} %get-tuple-element.107.refs_2_.refs_0_, bf16[1024,2048]{1,0:T(8,128)(2,1)} %gather_cot.1.grad_ref.refs_3_, ...), custom_call_target="tpu_custom_call" | custom-call | flops 8589934592 | bytes 20971520 | tf_op jit(solution)/shard_map/weight_pass/pallas_call | solution.py:396
  638.4 61.4 %row_pass.2 = (bf16[1024,2048]{1,0:T(8,128)(2,1)}, f32[256,2048]{1,0:T(8,128)}) custom-call(bf16[1024,1024]{1,0:T(8,128)(2,1)} %get-tuple-element.113.refs_0_, bf16[1024,1024]{1,0:T(8,128)(2,1)} %get-tuple-element.110.refs_0_.refs_1_, bf16[1024,1024]{1,0:T(8,128)(2,1)} %get-tuple-element.122.refs_2_.refs_0_, ...), custom_call_target="tpu_custom_call" | custom-call | flops 25769803776 | bytes 46137344 | tf_op jit(solution)/shard_map/row_pass/pallas_call | solution.py:952
  699.9 14.4 %weight_pass.12 = bf16[1024,2048]{1,0:T(8,128)(2,1)} custom-call(bf16[1024,1024]{1,0:T(8,128)(2,1)} %get-tuple-element.120.refs_5_.refs_0_, bf16[1024,2048]{1,0:T(8,128)(2,1)} %constant_dynamic-update-slice_fusion.rows_ref.refs_1_, bf16[1024,1024]{1,0:T(8,128)(2,1)} %get-tuple-element.121.refs_2_.refs_5_, ...), custom_call_target="tpu_custom_call" | custom-call | flops 8589934592 | bytes 16777216 | tf_op jit(solution)/shard_map/weight_pass/pallas_call | solution.py:396
  716.2 14.8 %weight_pass.13 = bf16[1024,2048]{1,0:T(8,128)(2,1)} custom-call(bf16[1024,1024]{1,0:T(8,128)(2,1)} %get-tuple-element.122.refs_2_.refs_0_, bf16[1024,2048]{1,0:T(8,128)(2,1)} %constant_dynamic-update-slice_fusion.rows_ref.refs_1_, bf16[1024,1024]{1,0:T(8,128)(2,1)} %get-tuple-element.123.refs_2_, ...), custom_call_target="tpu_custom_call" | custom-call | flops 8589934592 | bytes 20971520 | tf_op jit(solution)/shard_map/weight_pass/pallas_call | solution.py:396
  731.1 60.7 %row_pass.3 = (bf16[1024,2048]{1,0:T(8,128)(2,1)}, f32[256,2048]{1,0:T(8,128)}) custom-call(bf16[1024,1024]{1,0:T(8,128)(2,1)} %get-tuple-element.107.refs_2_.refs_0_, bf16[1024,1024]{1,0:T(8,128)(2,1)} %get-tuple-element.109.refs_2_.refs_1_, bf16[1024,1024]{1,0:T(8,128)(2,1)} %get-tuple-element.123.refs_2_, ...), custom_call_target="tpu_custom_call" | custom-call | flops 25769803776 | bytes 46137344 | tf_op jit(solution)/shard_map/row_pass/pallas_call | solution.py:952
  806.3 9.8 all-to-all-start.2
  822.2 18.0 %all-to-all-done.2 = bf16[8,256,256]{2,1,0:T(8,128)(2,1)S(1)} async-done(((bf16[8,256,256]{2,1,0:T(8,128)(2,1)}), bf16[8,256,256]{2,1,0:T(8,128)(2,1)S(1)}, u32[]{:S(2)}, u32[]{:S(2)}) %all-to-all-start.2) | async-done | bytes 1048608 | tf_op jit(solution)/shard_map/all_to_all | solution.py:1492
  849.3 20.5 %attend_back.2 = (bf16[2048,768]{1,0:T(8,128)(2,1)S(1)}, f32[2,1,128]{2,1,0:T(1,128)S(1)}) custom-call(s32[1]{0:T(128)} %bitcast.1.length_ref, f32[2]{0:T(128)S(1)} %copy-done.23, bf16[2048,768]{1,0:T(8,128)(2,1)S(1)} %copy-done.27, bf16[2048,768]{1,0:T(8,128)(2,1)S(1)} %copy-done.27, bf16[2048,768]{1,0:T(8,128)(2,1)S(1)} %copy-done.27, ...), custom_call_target="tpu_custom_call" | custom-call | flops 10737418240 | bytes 10485760 | tf_op jit(solution)/shard_map/attend_back/pallas_call | solution.py:286
  871.5 15.2 %weight_pass.14 = bf16[1024,2048]{1,0:T(8,128)(2,1)} custom-call(bf16[1024,1024]{1,0:T(8,128)(2,1)} %get-tuple-element.132.refs_4_.refs_0_, bf16[1024,2048]{1,0:T(8,128)(2,1)} %constant_dynamic-update-slice_fusion.rows_ref.refs_1_, bf16[1024,1024]{1,0:T(8,128)(2,1)} %get-tuple-element.124.refs_4_.refs_2_, ...), custom_call_target="tpu_custom_call" | custom-call | flops 8589934592 | bytes 20971520 | tf_op jit(solution)/shard_map/weight_pass/pallas_call | solution.py:396
  917.9 14.6 %attend_back.3 = (bf16[2048,768]{1,0:T(8,128)(2,1)S(1)}, f32[2,1,128]{2,1,0:T(1,128)S(1)}) custom-call(s32[1]{0:T(128)} %bitcast.15.length_ref, f32[2]{0:T(128)S(1)} %copy-done.23, bf16[2048,768]{1,0:T(8,128)(2,1)S(1)} %copy-done.25, bf16[2048,768]{1,0:T(8,128)(2,1)S(1)} %copy-done.25, bf16[2048,768]{1,0:T(8,128)(2,1)S(1)} %copy-done.25, ...), custom_call_target="tpu_custom_call" | custom-call | flops 10737418240 | bytes 10485760 | tf_op jit(solution)/shard_map/attend_back/pallas_call | solution.py:286
  945.0 9.1 weight_pass.17
  966.6 21.4 %weight_pass.15 = bf16[768,2048]{1,0:T(8,128)(2,1)} custom-call(bf16[2048,768]{1,0:T(8,128)(2,1)} %copy-done.6, bf16[2048,2048]{1,0:T(8,128)(2,1)} %copy-done.28, bf16[2048,768]{1,0:T(8,128)(2,1)} %copy-done.9, bf16[2048,2048]{1,0:T(8,128)(2,1)} %copy-done.29), custom_call_target="tpu_custom_call" | custom-call | flops 12884901888 | bytes 26214400 | tf_op jit(solution)/shard_map/weight_pass/pallas_call | solution.py:396
  990.8 34.3 %reduce-scatter.12.cloned.1.call-done = bf16[256,2048]{1,0:T(8,128)(2,1)} async-done(((bf16[1024,2048]{1,0:T(8,128)(2,1)}), bf16[256,2048]{1,0:T(8,128)(2,1)}) %reduce-scatter.12.cloned.1.call-update) | async-done | bytes 1048592 | tf_op jit(solution)/shard_map/reduce_scatter | solution.py:1538
  1050.7 212.3 %spread_sums.1 = (f32[2,256,2048]{2,1,0:T(8,128)}, bf16[384,2048]{1,0:T(8,128)(2,1)}, bf16[2,128,1024]{2,1,0:T(8,128)(2,1)}) custom-call(bf16[4,256,2048]{2,1,0:T(8,128)(2,1)} %bitcast.137, bf16[4,256,2048]{2,1,0:T(8,128)(2,1)} %bitcast.138, bf16[3,256,2048]{2,1,0:T(8,128)(2,1)} %bitcast.159, bf16[4,4,128,1024]{3,2,1,0:T(8,128)(2,1)} %bitcast.152), custom_call_target="tpu_custom_call" | custom-call | bytes 134217728 | tf_op jit(solution)/shard_map/spread_sums/pallas_call | solution.py:1246
  (332 shorter events, 277.2 us)
Async XLA Ops:
  7.2 97.9 %all-gather.15.cloned.1.call-start = ((), (), s32[]{:S(2)}) async-start(), calls=%async_computation.18 | async-start | bytes 9437184 | tf_op jit(solution)/shard_map/all_gather | solution.py:1321
  10.5 208.0 %all-gather.7.cloned.1.call-start = ((), (), s32[]{:S(2)}) async-start(), calls=%async_computation.9 | async-start | bytes 9437184 | tf_op jit(solution)/shard_map/all_gather | solution.py:1321
  105.1 341.2 %all-gather.9.cloned.1.call-start = ((), (), s32[]{:S(2)}) async-start(), calls=%async_computation.10 | async-start | bytes 10485760 | tf_op jit(solution)/shard_map/all_gather | solution.py:1383
  304.0 57.7 %all-to-all-start = ((bf16[8,256,256]{2,1,0:T(8,128)(2,1)}), bf16[8,256,256]{2,1,0:T(8,128)(2,1)}, u32[]{:S(2)}, u32[]{:S(2)}) async-start(bf16[8,256,256]{2,1,0:T(8,128)(2,1)} %bitcast.12), calls=%async_computation | async-start | bytes 2097152 | tf_op jit(solution)/shard_map/all_to_all | solution.py:1391
  313.0 104.3 %collective-permute-start = (bf16[2048,1024]{1,0:T(8,128)(2,1)}, bf16[2048,1024]{1,0:T(8,128)(2,1)}, u32[]{:S(2)}, u32[]{:S(2)}) collective-permute-start(bf16[2048,1024]{1,0:T(8,128)(2,1)} %get-tuple-element.94), channel_id=1, source_target_pairs={{0,16},{16,0},{1,17},{17,1},{2,18},{18,2},{3,19},{19,3},{4,20},{20... | collective-permute-start | bytes 12582920 | tf_op jit(solution)/shard_map/ppermute | solution.py:465
  361.7 48.8 %all-to-all-start.1 = ((bf16[8,256,256]{2,1,0:T(8,128)(2,1)}), bf16[8,256,256]{2,1,0:T(8,128)(2,1)}, u32[]{:S(2)}, u32[]{:S(2)}) async-start(bf16[8,256,256]{2,1,0:T(8,128)(2,1)} %bitcast.18), calls=%async_computation.1 | async-start | bytes 2097152 | tf_op jit(solution)/shard_map/all_to_all | solution.py:1391
  369.5 139.7 %all-gather.11.cloned.1.call-start = ((), (), s32[]{:S(2)}) async-start(), calls=%async_computation.11 | async-start | bytes 5242880 | tf_op jit(solution)/shard_map/all_gather | solution.py:1434
  370.6 360.4 %reduce-scatter.6.cloned.1.call-start = ((), (), s32[]{:S(2)}) async-start(), calls=%async_computation.12 | async-start | bytes 5242880 | tf_op jit(solution)/shard_map/reduce_scatter | solution.py:1453
  432.5 22.9 %collective-permute-start.1 = (bf16[128,2048]{1,0:T(8,128)(2,1)}, bf16[128,2048]{1,0:T(8,128)(2,1)}, u32[]{:S(2)}, u32[]{:S(2)}) collective-permute-start(bf16[128,2048]{1,0:T(8,128)(2,1)} %get-tuple-element.228), channel_id=1, source_target_pairs={{0,8},{4,12},{8,0},{12,4},{1,9},{5,13},{9,1},{13,5},{2,10},{6,14},... | collective-permute-start | bytes 1572872 | tf_op jit(solution)/shard_map/ppermute | solution.py:546
  443.6 23.1 %collective-permute-start.3 = (bf16[128,2048]{1,0:T(8,128)(2,1)}, bf16[128,2048]{1,0:T(8,128)(2,1)}, u32[]{:S(2)}, u32[]{:S(2)}) collective-permute-start(bf16[128,2048]{1,0:T(8,128)(2,1)} %collective-permute-done.2), channel_id=1, source_target_pairs={{0,8},{4,12},{8,0},{12,4},{1,9},{5,13},{9,1},{13,5},{2,10},{6,14},... | collective-permute-start | bytes 1572872 | tf_op jit(solution)/shard_map/ppermute | solution.py:546
  444.8 27.1 %collective-permute-start.4 = (bf16[128,2048]{1,0:T(8,128)(2,1)S(1)}, bf16[128,2048]{1,0:T(8,128)(2,1)}, u32[]{:S(2)}, u32[]{:S(2)}) collective-permute-start(bf16[128,2048]{1,0:T(8,128)(2,1)S(1)} %get-tuple-element.226), channel_id=1, source_target_pairs={{0,4},{4,0},{8,12},{12,8},{1,5},{5,1},{9,13},{13,9},{2,6},{6,2},{1... | collective-permute-start | bytes 1572872 | tf_op jit(solution)/shard_map/ppermute | solution.py:546
  445.9 36.8 %collective-permute-start.6 = (bf16[128,2048]{1,0:T(8,128)(2,1)}, bf16[128,2048]{1,0:T(8,128)(2,1)}, u32[]{:S(2)}, u32[]{:S(2)}) collective-permute-start(bf16[128,2048]{1,0:T(8,128)(2,1)} %collective-permute-done.5), channel_id=1, source_target_pairs={{0,4},{4,0},{8,12},{12,8},{1,5},{5,1},{9,13},{13,9},{2,6},{6,2},{1... | collective-permute-start | bytes 1572872 | tf_op jit(solution)/shard_map/ppermute | solution.py:546
  446.3 85.2 %collective-permute-start.13 = (bf16[1024,4096]{1,0:T(8,128)(2,1)}, bf16[1024,4096]{1,0:T(8,128)(2,1)}, u32[]{:S(2)}, u32[]{:S(2)}) collective-permute-start(bf16[1024,4096]{1,0:T(8,128)(2,1)} %all-gather.9.cloned.1.call-done.inner_ref.refs_6_.refs_8_), channel_id=1, source_target_pairs={{0,16},{16,0},{1,17},{17,1},{2,18},{18,2},{3,19},{19,3},{4,20},{20... | collective-permute-start | bytes 25165832 | tf_op jit(solution)/shard_map/ppermute | solution.py:465
  470.7 24.1 %collective-permute-start.7 = (bf16[128,2048]{1,0:T(8,128)(2,1)S(1)}, bf16[128,2048]{1,0:T(8,128)(2,1)S(1)}, u32[]{:S(2)}, u32[]{:S(2)}) collective-permute-start(bf16[128,2048]{1,0:T(8,128)(2,1)S(1)} %get-tuple-element.233), channel_id=1, source_target_pairs={{0,8},{4,12},{8,0},{12,4},{1,9},{5,13},{9,1},{13,5},{2,10},{6,14},... | collective-permute-start | bytes 1572872 | tf_op jit(solution)/shard_map/ppermute | solution.py:546
  471.9 22.0 %collective-permute-start.11 = (bf16[128,2048]{1,0:T(8,128)(2,1)S(1)}, bf16[128,2048]{1,0:T(8,128)(2,1)S(1)}, u32[]{:S(2)}, u32[]{:S(2)}) collective-permute-start(bf16[128,2048]{1,0:T(8,128)(2,1)S(1)} %get-tuple-element.231), channel_id=1, source_target_pairs={{0,8},{4,12},{8,0},{12,4},{1,9},{5,13},{9,1},{13,5},{2,10},{6,14},... | collective-permute-start | bytes 1572872 | tf_op jit(solution)/shard_map/ppermute | solution.py:546
  481.5 23.5 %collective-permute-start.9 = (bf16[128,2048]{1,0:T(8,128)(2,1)S(1)}, bf16[128,2048]{1,0:T(8,128)(2,1)S(1)}, u32[]{:S(2)}, u32[]{:S(2)}) collective-permute-start(bf16[128,2048]{1,0:T(8,128)(2,1)S(1)} %collective-permute-done.8), channel_id=1, source_target_pairs={{0,8},{4,12},{8,0},{12,4},{1,9},{5,13},{9,1},{13,5},{2,10},{6,14},... | collective-permute-start | bytes 1572872 | tf_op jit(solution)/shard_map/ppermute | solution.py:546
  484.6 22.1 %collective-permute-start.10 = (bf16[128,2048]{1,0:T(8,128)(2,1)S(1)}, bf16[128,2048]{1,0:T(8,128)(2,1)S(1)}, u32[]{:S(2)}, u32[]{:S(2)}) collective-permute-start(bf16[128,2048]{1,0:T(8,128)(2,1)S(1)} %get-tuple-element.231), channel_id=1, source_target_pairs={{0,4},{4,0},{8,12},{12,8},{1,5},{5,1},{9,13},{13,9},{2,6},{6,2},{1... | collective-permute-start | bytes 1572872 | tf_op jit(solution)/shard_map/ppermute | solution.py:546
  509.2 22.2 %collective-permute-start.14 = (bf16[1024,2048]{1,0:T(8,128)(2,1)}, bf16[1024,2048]{1,0:T(8,128)(2,1)S(1)}, u32[]{:S(2)}, u32[]{:S(2)}) collective-permute-start(bf16[1024,2048]{1,0:T(8,128)(2,1)} %all-gather.11.cloned.1.call-done.down_ref.refs_10_), channel_id=1, source_target_pairs={{0,16},{16,0},{1,17},{17,1},{2,18},{18,2},{3,19},{19,3},{4,20},{20... | collective-permute-start | bytes 12582920 | tf_op jit(solution)/shard_map/ppermute | solution.py:465
  637.8 207.9 %reduce-scatter.10.cloned.1.call-start = ((), (), s32[]{:S(2)}) async-start(), calls=%async_computation.14 | async-start | bytes 5242880 | tf_op jit(solution)/shard_map/reduce_scatter | solution.py:1453
  637.9 76.3 %collective-permute-start.16 = (bf16[1024,2048]{1,0:T(8,128)(2,1)}, bf16[1024,2048]{1,0:T(8,128)(2,1)S(1)}, u32[]{:S(2)}, u32[]{:S(2)}) collective-permute-start(bf16[1024,2048]{1,0:T(8,128)(2,1)} %weight_pass.10), channel_id=1, source_target_pairs={{0,16},{16,0},{1,17},{17,1},{2,18},{18,2},{3,19},{19,3},{4,20},{20... | collective-permute-start | bytes 12582920 | tf_op jit(solution)/shard_map/ppermute | solution.py:465
  731.0 182.2 %reduce-scatter.8.cloned.1.call-start = ((), (), s32[]{:S(2)}) async-start(), calls=%async_computation.13 | async-start | bytes 5242880 | tf_op jit(solution)/shard_map/reduce_scatter | solution.py:1538
  798.3 73.1 %collective-permute-start.17 = (bf16[1024,2048]{1,0:T(8,128)(2,1)}, bf16[1024,2048]{1,0:T(8,128)(2,1)}, u32[]{:S(2)}, u32[]{:S(2)}) collective-permute-start(bf16[1024,2048]{1,0:T(8,128)(2,1)} %weight_pass.12), channel_id=1, source_target_pairs={{0,16},{16,0},{1,17},{17,1},{2,18},{18,2},{3,19},{19,3},{4,20},{20... | collective-permute-start | bytes 12582920 | tf_op jit(solution)/shard_map/ppermute | solution.py:465
  806.3 33.9 %all-to-all-start.2 = ((bf16[8,256,256]{2,1,0:T(8,128)(2,1)}), bf16[8,256,256]{2,1,0:T(8,128)(2,1)S(1)}, u32[]{:S(2)}, u32[]{:S(2)}) async-start(bf16[8,256,256]{2,1,0:T(8,128)(2,1)} %bitcast.136), calls=%async_computation.4 | async-start | bytes 2097152 | tf_op jit(solution)/shard_map/all_to_all | solution.py:1492
  840.2 31.2 %all-to-all-start.3 = ((bf16[8,256,256]{2,1,0:T(8,128)(2,1)}), bf16[8,256,256]{2,1,0:T(8,128)(2,1)S(1)}, u32[]{:S(2)}, u32[]{:S(2)}) async-start(bf16[8,256,256]{2,1,0:T(8,128)(2,1)} %bitcast.153), calls=%async_computation.6 | async-start | bytes 2097152 | tf_op jit(solution)/shard_map/all_to_all | solution.py:1492
  845.7 142.3 %reduce-scatter.14.cloned.1.call-start = ((), (), s32[]{:S(2)}) async-start(), calls=%async_computation.16 | async-start | bytes 5242880 | tf_op jit(solution)/shard_map/reduce_scatter | solution.py:1453
  886.7 138.5 %reduce-scatter.12.cloned.1.call-start = ((), (), s32[]{:S(2)}) async-start(), calls=%async_computation.15 | async-start | bytes 5242880 | tf_op jit(solution)/shard_map/reduce_scatter | solution.py:1538
  887.4 391.5 %all-gather.13.cloned.1.call-start = ((), (), s32[]{:S(2)}) async-start(), calls=%async_computation.17 | async-start | bytes 2162688 | tf_op jit(solution)/shard_map/all_gather | solution.py:1597
  896.3 48.7 %collective-permute-start.20 = (bf16[2048,1024]{1,0:T(8,128)(2,1)}, bf16[2048,1024]{1,0:T(8,128)(2,1)}, u32[]{:S(2)}, u32[]{:S(2)}) collective-permute-start(bf16[2048,1024]{1,0:T(8,128)(2,1)} %weight_pass.16), channel_id=1, source_target_pairs={{0,16},{16,0},{1,17},{17,1},{2,18},{18,2},{3,19},{19,3},{4,20},{20... | collective-permute-start | bytes 12582920 | tf_op jit(solution)/shard_map/ppermute | solution.py:465
  904.0 50.2 %collective-permute-start.18 = (bf16[1024,2048]{1,0:T(8,128)(2,1)}, bf16[1024,2048]{1,0:T(8,128)(2,1)}, u32[]{:S(2)}, u32[]{:S(2)}) collective-permute-start(bf16[1024,2048]{1,0:T(8,128)(2,1)} %get-tuple-element.138), channel_id=1, source_target_pairs={{0,16},{16,0},{1,17},{17,1},{2,18},{18,2},{3,19},{19,3},{4,20},{20... | collective-permute-start | bytes 12582920 | tf_op jit(solution)/shard_map/ppermute | solution.py:465
  907.4 34.7 %collective-permute-start.22 = (bf16[256,2048]{1,0:T(8,128)(2,1)}, bf16[256,2048]{1,0:T(8,128)(2,1)}, u32[]{:S(2)}, u32[]{:S(2)}) collective-permute-start(bf16[256,2048]{1,0:T(8,128)(2,1)} %reduce-scatter.6.cloned.1.call-done), channel_id=1, source_target_pairs={{0,16},{16,0},{1,17},{17,1},{2,18},{18,2},{3,19},{19,3},{4,20},{20... | collective-permute-start | bytes 3145736 | tf_op jit(solution)/shard_map/ppermute | solution.py:465
  940.9 88.0 %collective-permute-start.19 = (bf16[1024,2048]{1,0:T(8,128)(2,1)}, bf16[1024,2048]{1,0:T(8,128)(2,1)}, u32[]{:S(2)}, u32[]{:S(2)}) collective-permute-start(bf16[1024,2048]{1,0:T(8,128)(2,1)} %get-tuple-element.145), channel_id=1, source_target_pairs={{0,16},{16,0},{1,17},{17,1},{2,18},{18,2},{3,19},{19,3},{4,20},{20... | collective-permute-start | bytes 12582920 | tf_op jit(solution)/shard_map/ppermute | solution.py:465
  990.3 56.3 %collective-permute-start.21 = (bf16[256,4096]{1,0:T(8,128)(2,1)}, bf16[256,4096]{1,0:T(8,128)(2,1)}, u32[]{:S(2)}, u32[]{:S(2)}) collective-permute-start(bf16[256,4096]{1,0:T(8,128)(2,1)} %constant_dynamic-update-slice_fusion.16), channel_id=1, source_target_pairs={{0,16},{16,0},{1,17},{17,1},{2,18},{18,2},{3,19},{19,3},{4,20},{20... | collective-permute-start | bytes 6291464 | tf_op jit(solution)/shard_map/ppermute | solution.py:465
  (84 other events, 2096.6 us)
Sparse Core Ops, SparseCore 0:
  10.6 94.3 all-gather.14
  107.2 102.7 all-gather.6
  218.7 193.4 all-gather.8
  413.6 80.2 all-gather.10
  638.0 78.4 reduce-scatter.5
  731.1 79.6 reduce-scatter.9
  813.8 52.6 reduce-scatter.7
  886.8 82.6 reduce-scatter.13
  972.4 52.6 reduce-scatter.11
  1039.8 98.5 all-gather.12

commit v5 on v4

--- a/solution.py
+++ b/solution.py
@@ -872,35 +872,46 @@
 
 def row_kernel(count, *refs):
     hidden, gates, ups, gate_w, up_w, down_w = (refs[2 * i : 2 * i + 2] for i in range(6))
-    out_ref, grad_ref, parts, landed, sent, here = refs[12:]
+    out_ref, grad_ref, parts, sent, here = refs[12:17]
+    landed = refs[17:]
+    stages = len(landed)
     step, steps = pl.program_id(0), pl.num_programs(0)
     core, column, place = lax.axis_index("rep"), lax.axis_index("dp"), lax.axis_index("seq")
-    cube = [(core, flipped(column, k), place) for k in range(1, count)]
+    width = parts.shape[2]
+    size = out_ref.shape[0] // (2 * count)
 
     @pl.when(step == 0)
     def _():
-        greet(cube)
-
-    size = out_ref.shape[0] // (2 * count)
-    spots = [
-        (side, at, order_k)
-        for side, bits in enumerate(cube_bits(count))
-        for at, order_k in enumerate(cube_order(bits))
-    ]
-
-    def piece(side, at):
-        return pl.ds((side * count + at) * size, size)
-
-    def leaving(t, side, at, k):
-        number = side * (count - 1) + k - 1
-        flat = t * (2 * (count - 1)) + number
+        greet([(core, flipped(column, bit), place) for bit in cube_bits(count)[0]])
+
+    def copy(t, stage, side):
+        keep = (count >> (stage + 1)) * size
+        flat = (t * stages + stage) * 2 + side
         return remote(
-            parts.at[t, piece(side, at)],
-            landed.at[t, number],
+            parts.at[t, pl.ds(side * count * size + keep, keep)],
+            landed[stage].at[t, side],
             sent.at[flat],
             here.at[flat],
-            cube[k - 1],
-        )
+            (core, flipped(column, cube_bits(count)[side][stage]), place),
+        )
+
+    def send(t, stage):
+        for side in range(2):
+            copy(t, stage, side).start()
+
+    def take(t, stage):
+        keep = (count >> (stage + 1)) * size
+        for side in range(2):
+            copy(t, stage, side).wait()
+            rows = pl.ds(side * count * size, keep)
+            total = parts[t, rows, :].astype(F32) + landed[stage][t, side].astype(F32)
+            if stage + 1 < stages:
+                parts[t, rows, :] = total.astype(BF16)
+            else:
+                columns = pl.ds(pl.multiple_of(t * width, width), width)
+                grad_ref[side * size : (side + 1) * size, columns] = total
+        if stage + 1 < stages:
+            send(t, stage + 1)
 
     parts[step] = (
         nn(gates[0][...], gate_w[0][...])
@@ -908,34 +919,27 @@
         + nn(ups[0][...], up_w[0][...])
         + nn(ups[1][...], up_w[1][...])
     ).astype(BF16)
-    for side, at, k in spots:
-        if k:
-            leaving(step, side, at, k).start()
+    send(step, 0)
     out = (
         nn(hidden[0][...], down_w[0][...]) + nn(hidden[1][...], down_w[1][...])
     ).astype(BF16)
-    for side, at, k in spots:
-        owner = flipped(column, k) if k else column
-        start = pl.multiple_of((2 * owner + side) * size, size)
-        out_ref[pl.ds(start, size), :] = out[(side * count + at) * size :][:size]
+    for side, bits in enumerate(cube_bits(count)):
+        for at, k in enumerate(cube_order(bits)):
+            owner = flipped(column, k) if k else column
+            start = pl.multiple_of((2 * owner + side) * size, size)
+            out_ref[pl.ds(start, size), :] = out[(side * count + at) * size :][:size]
+
+    for stage in reversed(range(stages)):
+
+        @pl.when(step >= 2 * (stage + 1))
+        def _():
+            take(step - 2 * (stage + 1), stage)
 
     @pl.when(step == steps - 1)
     def _():
-        width = parts.shape[2]
-
-        def finish(t, _):
-            for side, at, k in spots:
-                if k:
-                    leaving(t, side, at, k).wait()
-            columns = pl.ds(pl.multiple_of(t * width, width), width)
-            for side in range(2):
-                total = parts[t, piece(side, 0), :].astype(F32)
-                for k in range(1, count):
-                    total += landed[t, side * (count - 1) + k - 1].astype(F32)
-                grad_ref[side * size : (side + 1) * size, columns] = total
-            return 0
-
-        lax.fori_loop(0, steps, finish, 0)
+        for stage in range(stages):
+            for back in reversed(range(2 * (stage + 1))):
+                take(steps - 1 - back, stage)
 
 
 def row_pass(hidden, grad_gates, grad_ups, inner, down, dp_count):
@@ -943,8 +947,8 @@
     width = down[0].shape[1]
     tile = min(256, width)
     tiles = width // tile
-    pieces = 2 * (dp_count - 1)
     size = count // (2 * dp_count)
+    stages = dp_count.bit_length() - 1
     resident = pl.BlockSpec((count, units), lambda t: (0, 0), pipeline_mode=pl.Buffered(1))
     low = pl.BlockSpec((units, tile), lambda t: (0, t))
     high = pl.BlockSpec((units, tile), lambda t: (0, tiles + t))
@@ -963,9 +967,12 @@
         ],
         scratch_shapes=[
             pltpu.VMEM((tiles, count, tile), BF16),
-            pltpu.VMEM((tiles, pieces, size, tile), BF16),
-            dma((tiles * pieces,)),
-            dma((tiles * pieces,)),
+            dma((tiles * stages * 2,)),
+            dma((tiles * stages * 2,)),
+        ]
+        + [
+            pltpu.VMEM((tiles, 2, (dp_count >> (j + 1)) * size, tile), BF16)
+            for j in range(stages)
         ],
         compiler_params=pltpu.CompilerParams(
             collective_id=4, has_side_effects=True, vmem_limit_bytes=56 << 20
@@ -1569,6 +1576,7 @@
     grad_qkv = qkv_done.astype(F32)
     grad_out = jnp.swapaxes(out_done, 0, 1).reshape(shard_out, width).astype(F32)
     for s, mlp_out in zip(saved, mlp_outs):
+        mlp_out = after(mlp_out, grad_ones)
         outputs.append((s["after_attn"] + mlp_out.astype(F32)).astype(BF16))
 
     def joined(name):

time: 1300 us -> 1280 us (0.985)
  waiting for transfers between devices: 187 us -> 141 us
  Pallas kernels: 869 us -> 899 us
    reduce_scatter x2, waiting for transfers between devices: 34.3 us -> 0.02 us  [spread_out(): lax.psum_scatter(after(s['mlp_part'], *earlier), 'dp', scatter_dimension=...]
    pallas_call x2, Pallas kernels: 35.1 us -> 50.3 us  [attend_back(): pl.pallas_call(functools.partial(attend_back_kernel, block), grid=(heads,...]
    unnamed x172 -> x188, local copies, waits for them, and re-layouts: 63.1 us -> 75.1 us
  transfers between devices with their start and end apart: 37 -> 37, of which waited for: 11 -> 10; matrix products, arithmetic and copies ran while one was open for 9% -> 8% of each run, Pallas kernels for 60% -> 64%
where the time goes in v5:
time: 1280 us
  Pallas kernels  899 us (70%)
  waiting for transfers between devices  141 us (11%)
  local copies, waits for them, and re-layouts  108 us (8%)
  starting transfers between devices  48.5 us (4%)
  other arithmetic  42.4 us (3%)
  matrix products  20.5 us (2%)
  between operations  15.5 us (1%)
    pallas_call x1, Pallas kernels, spread_sums(): pl.pallas_call(functools.partial(spread_kernel, sizes, micros), in_specs=...  212 us
    pallas_call x9, Pallas kernels, weight_pass(): pl.pallas_call(functools.partial(weight_kernel, len(pairs)), grid=(size /...  127 us
    pallas_call x2, Pallas kernels, row_pass(): pl.pallas_call(functools.partial(row_kernel, dp_count), grid=(tiles,), in...  124 us
    pallas_call x1, Pallas kernels, gather_rest(): pl.pallas_call(functools.partial(rest_kernel, sizes), in_specs=[anywhere]...  104 us
    pallas_call x4, Pallas kernels, unit_pass(): pl.pallas_call(unit_kernel, grid=(units // tile,), in_specs=[resident, re...  78.5 us
    unnamed x188, local copies, waits for them, and re-layouts  75.1 us
    pallas_call x1, Pallas kernels, gather_heads(): pl.pallas_call(functools.partial(heads_kernel, sizes), in_specs=[anywhere...  59.7 us
    pallas_call x2, Pallas kernels, attend_back(): pl.pallas_call(functools.partial(attend_back_kernel, block), grid=(heads,...  50.3 us
  transfers between devices with their start and end apart: 37, of which 10 were waited for; matrix products, arithmetic and copies ran while one was open for 8% of the time, Pallas kernels for 64%

profile of v5, /device:TPU:17, one launch (start us, length us, event | category | flops | bytes accessed | tf_op | source)
XLA Modules:
  0.0 1275.0 jit_solution(3406951607275854512)
XLA Ops:
  12.1 59.7 %gather_heads.1 = (bf16[768,2048]{1,0:T(8,128)(2,1)S(1)}, f32[16,8,128]{2,1,0:T(8,128)S(1)}) custom-call(bf16[384,2048]{1,0:T(8,128)(2,1)S(1)} %copy-done.13, f32[8,128]{1,0:T(8,128)S(1)} %pad_convert_fusion.gain_ref), custom_call_target="tpu_custom_call" | custom-call | bytes 33554432 | tf_op jit(solution)/shard_map/gather_heads/pallas_call | solution.py:715
  73.4 31.6 %all-gather.15.cloned.1.call-done = bf16[1,1,2048,2048]{3,2,1,0:T(8,128)(2,1)} async-done(((bf16[1,1,256,2048]{3,2,1,0:T(8,128)(2,1)}), bf16[1,1,2048,2048]{3,2,1,0:T(8,128)(2,1)}) %all-gather.15.cloned.1.call-update) | async-done | bytes 8388624 | tf_op jit(solution)/shard_map/all_gather | solution.py:1328
  114.2 104.1 %gather_rest.1 = (bf16[2048,1024]{1,0:T(8,128)(2,1)}, bf16[1024,2048]{1,0:T(8,128)(2,1)}) custom-call(bf16[128,1024]{1,0:T(8,128)(2,1)} %constant_dynamic-slice_fusion.9.refs_0_, bf16[256,2048]{1,0:T(8,128)(2,1)} %get-tuple-element.222.refs_1_), custom_call_target="tpu_custom_call" | custom-call | bytes 4194304 | tf_op jit(solution)/shard_map/gather_rest/pallas_call | solution.py:846
  221.4 47.4 %gather_cot.1.grad_ref.refs_3_ = bf16[1024,2048]{1,0:T(8,128)(2,1)} custom-call(bf16[256,2048]{1,0:T(8,128)(2,1)} %get-tuple-element.91.cot_ref), custom_call_target="tpu_custom_call" | custom-call | bytes 4194304 | tf_op jit(solution)/shard_map/gather_cot/pallas_call | solution.py:786
  270.7 11.3 project.2
  285.4 21.6 %attend.2 = (bf16[2048,256]{1,0:T(8,128)(2,1)}, f32[2048,256]{1,0:T(8,128)S(1)}, f32[2,1,2048]{2,1,0:T(1,128)S(1)}, f32[2,128,128]{2,1,0:T(8,128)S(1)}, f32[2,1,128]{2,1,0:T(1,128)S(1)}) custom-call(s32[1]{0:T(128)} %bitcast.1.length_ref, f32[2]{0:T(128)S(1)} %dynamic_slice.43.gate_ref, bf16[2048,768]{1,0:T(8,128)(2,1)S(1)} %get-tuple-element.94.q_ref.k_ref.v_ref, ...), custom_call_target="tpu_custom_call" | custom-call | flops 4294967296 | bytes 6291456 | tf_op jit(solution)/shard_map/attend/pallas_call | solution.py:156
  319.0 11.3 project.3
  333.7 21.6 %attend.3 = (bf16[2048,256]{1,0:T(8,128)(2,1)}, f32[2048,256]{1,0:T(8,128)S(1)}, f32[2,1,2048]{2,1,0:T(1,128)S(1)}, f32[2,128,128]{2,1,0:T(8,128)S(1)}, f32[2,1,128]{2,1,0:T(1,128)S(1)}) custom-call(s32[1]{0:T(128)} %bitcast.15.length_ref, f32[2]{0:T(128)S(1)} %dynamic_slice.43.gate_ref, bf16[2048,768]{1,0:T(8,128)(2,1)S(1)} %get-tuple-element.99.q_ref.k_ref.v_ref, ...), custom_call_target="tpu_custom_call" | custom-call | flops 4294967296 | bytes 6291456 | tf_op jit(solution)/shard_map/attend/pallas_call | solution.py:156
  358.9 10.0 all-to-all-done
  378.2 33.6 %all-to-all-done.1 = bf16[8,256,256]{2,1,0:T(8,128)(2,1)} async-done(((bf16[8,256,256]{2,1,0:T(8,128)(2,1)}), bf16[8,256,256]{2,1,0:T(8,128)(2,1)}, u32[]{:S(2)}, u32[]{:S(2)}) %all-to-all-start.1) | async-done | bytes 1048608 | tf_op jit(solution)/shard_map/all_to_all | solution.py:1398
  432.0 10.8 collective-permute-done.2
  484.0 8.9 collective-permute-done.11
  510.9 20.0 %unit_pass.4 = (bf16[1024,1024]{1,0:T(8,128)(2,1)}, bf16[1024,1024]{1,0:T(8,128)(2,1)}, bf16[1024,1024]{1,0:T(8,128)(2,1)}) custom-call(bf16[1024,2048]{1,0:T(8,128)(2,1)} %constant_dynamic-update-slice_fusion.rows_ref.refs_1_, bf16[1024,2048]{1,0:T(8,128)(2,1)} %get-tuple-element.90.grad_ref.refs_1_, ...), custom_call_target="tpu_custom_call" | custom-call | flops 12884901888 | bytes 27262976 | tf_op jit(solution)/shard_map/unit_pass/pallas_call | solution.py:348
  532.9 19.5 %unit_pass.5 = (bf16[1024,1024]{1,0:T(8,128)(2,1)}, bf16[1024,1024]{1,0:T(8,128)(2,1)}, bf16[1024,1024]{1,0:T(8,128)(2,1)}) custom-call(bf16[1024,2048]{1,0:T(8,128)(2,1)} %constant_dynamic-update-slice_fusion.rows_ref.refs_1_, bf16[1024,2048]{1,0:T(8,128)(2,1)} %get-tuple-element.90.grad_ref.refs_1_, ...), custom_call_target="tpu_custom_call" | custom-call | flops 12884901888 | bytes 27262976 | tf_op jit(solution)/shard_map/unit_pass/pallas_call | solution.py:348
  552.4 19.5 %unit_pass.6 = (bf16[1024,1024]{1,0:T(8,128)(2,1)}, bf16[1024,1024]{1,0:T(8,128)(2,1)}, bf16[1024,1024]{1,0:T(8,128)(2,1)}) custom-call(bf16[1024,2048]{1,0:T(8,128)(2,1)} %constant_dynamic-update-slice_fusion.8.rows_ref.refs_3_, bf16[1024,2048]{1,0:T(8,128)(2,1)} %gather_cot.1.grad_ref.refs_3_, ...), custom_call_target="tpu_custom_call" | custom-call | flops 12884901888 | bytes 27262976 | tf_op jit(solution)/shard_map/unit_pass/pallas_call | solution.py:348
  571.9 19.6 %unit_pass.7 = (bf16[1024,1024]{1,0:T(8,128)(2,1)}, bf16[1024,1024]{1,0:T(8,128)(2,1)}, bf16[1024,1024]{1,0:T(8,128)(2,1)}) custom-call(bf16[1024,2048]{1,0:T(8,128)(2,1)} %constant_dynamic-update-slice_fusion.8.rows_ref.refs_3_, bf16[1024,2048]{1,0:T(8,128)(2,1)} %gather_cot.1.grad_ref.refs_3_, ...), custom_call_target="tpu_custom_call" | custom-call | flops 12884901888 | bytes 27262976 | tf_op jit(solution)/shard_map/unit_pass/pallas_call | solution.py:348
  591.5 14.5 %weight_pass.9 = bf16[1024,2048]{1,0:T(8,128)(2,1)} custom-call(bf16[1024,1024]{1,0:T(8,128)(2,1)} %get-tuple-element.112.refs_0_.refs_1_, bf16[1024,2048]{1,0:T(8,128)(2,1)} %get-tuple-element.90.grad_ref.refs_1_, bf16[1024,1024]{1,0:T(8,128)(2,1)} %get-tuple-element.111.refs_2_.refs_1_, bf16[1024,2048]{1,0:T(8,128)(2,1)} %gather_cot.1.grad_ref.refs_3_), custom_call_target="tpu_custom_call" | custom-call | flops 8589934592 | bytes 16777216 | tf_op jit(solution)/shard_map/weight_pass/pallas_call | solution.py:396
  606.1 14.3 %weight_pass.10 = bf16[1024,2048]{1,0:T(8,128)(2,1)} custom-call(bf16[1024,1024]{1,0:T(8,128)(2,1)} %get-tuple-element.113.refs_0_.refs_3_, bf16[1024,2048]{1,0:T(8,128)(2,1)} %constant_dynamic-update-slice_fusion.rows_ref.refs_1_, bf16[1024,1024]{1,0:T(8,128)(2,1)} %get-tuple-element.114.refs_2_.refs_3_, ...), custom_call_target="tpu_custom_call" | custom-call | flops 8589934592 | bytes 16777216 | tf_op jit(solution)/shard_map/weight_pass/pallas_call | solution.py:396
  622.3 14.7 %weight_pass.11 = bf16[1024,2048]{1,0:T(8,128)(2,1)} custom-call(bf16[1024,1024]{1,0:T(8,128)(2,1)} %get-tuple-element.115.refs_0_, bf16[1024,2048]{1,0:T(8,128)(2,1)} %get-tuple-element.90.grad_ref.refs_1_, bf16[1024,1024]{1,0:T(8,128)(2,1)} %get-tuple-element.109.refs_2_.refs_0_, bf16[1024,2048]{1,0:T(8,128)(2,1)} %gather_cot.1.grad_ref.refs_3_, ...), custom_call_target="tpu_custom_call" | custom-call | flops 8589934592 | bytes 20971520 | tf_op jit(solution)/shard_map/weight_pass/pallas_call | solution.py:396
  637.7 61.8 %row_pass.2 = (bf16[1024,2048]{1,0:T(8,128)(2,1)}, f32[256,2048]{1,0:T(8,128)}) custom-call(bf16[1024,1024]{1,0:T(8,128)(2,1)} %get-tuple-element.115.refs_0_, bf16[1024,1024]{1,0:T(8,128)(2,1)} %get-tuple-element.112.refs_0_.refs_1_, bf16[1024,1024]{1,0:T(8,128)(2,1)} %get-tuple-element.124.refs_2_.refs_0_, ...), custom_call_target="tpu_custom_call" | custom-call | flops 25769803776 | bytes 46137344 | tf_op jit(solution)/shard_map/row_pass/pallas_call | solution.py:956
  699.5 14.4 %weight_pass.12 = bf16[1024,2048]{1,0:T(8,128)(2,1)} custom-call(bf16[1024,1024]{1,0:T(8,128)(2,1)} %get-tuple-element.122.refs_5_.refs_0_, bf16[1024,2048]{1,0:T(8,128)(2,1)} %constant_dynamic-update-slice_fusion.rows_ref.refs_1_, bf16[1024,1024]{1,0:T(8,128)(2,1)} %get-tuple-element.123.refs_2_.refs_5_, ...), custom_call_target="tpu_custom_call" | custom-call | flops 8589934592 | bytes 16777216 | tf_op jit(solution)/shard_map/weight_pass/pallas_call | solution.py:396
  715.9 14.8 %weight_pass.13 = bf16[1024,2048]{1,0:T(8,128)(2,1)} custom-call(bf16[1024,1024]{1,0:T(8,128)(2,1)} %get-tuple-element.124.refs_2_.refs_0_, bf16[1024,2048]{1,0:T(8,128)(2,1)} %constant_dynamic-update-slice_fusion.rows_ref.refs_1_, bf16[1024,1024]{1,0:T(8,128)(2,1)} %get-tuple-element.125.refs_2_, ...), custom_call_target="tpu_custom_call" | custom-call | flops 8589934592 | bytes 20971520 | tf_op jit(solution)/shard_map/weight_pass/pallas_call | solution.py:396
  730.8 62.1 %row_pass.3 = (bf16[1024,2048]{1,0:T(8,128)(2,1)}, f32[256,2048]{1,0:T(8,128)}) custom-call(bf16[1024,1024]{1,0:T(8,128)(2,1)} %get-tuple-element.109.refs_2_.refs_0_, bf16[1024,1024]{1,0:T(8,128)(2,1)} %get-tuple-element.111.refs_2_.refs_1_, bf16[1024,1024]{1,0:T(8,128)(2,1)} %get-tuple-element.125.refs_2_, ...), custom_call_target="tpu_custom_call" | custom-call | flops 25769803776 | bytes 46137344 | tf_op jit(solution)/shard_map/row_pass/pallas_call | solution.py:956
  807.4 9.3 all-to-all-start.2
  823.2 17.6 %all-to-all-done.2 = bf16[8,256,256]{2,1,0:T(8,128)(2,1)S(1)} async-done(((bf16[8,256,256]{2,1,0:T(8,128)(2,1)}), bf16[8,256,256]{2,1,0:T(8,128)(2,1)S(1)}, u32[]{:S(2)}, u32[]{:S(2)}) %all-to-all-start.2) | async-done | bytes 1048608 | tf_op jit(solution)/shard_map/all_to_all | solution.py:1499
  849.8 25.1 %attend_back.2 = (bf16[2048,768]{1,0:T(8,128)(2,1)S(1)}, f32[2,1,128]{2,1,0:T(1,128)S(1)}) custom-call(s32[1]{0:T(128)} %bitcast.1.length_ref, f32[2]{0:T(128)S(1)} %dynamic_slice.43.gate_ref, bf16[2048,768]{1,0:T(8,128)(2,1)S(1)} %copy-done.27, bf16[2048,768]{1,0:T(8,128)(2,1)S(1)} %copy-done.27, bf16[2048,768]{1,0:T(8,128)(2,1)S(1)} %copy-done.27, ...), custom_call_target="tpu_custom_call" | custom-call | flops 10737418240 | bytes 10485760 | tf_op jit(solution)/shard_map/attend_back/pallas_call | solution.py:286
  876.7 15.2 %weight_pass.14 = bf16[1024,2048]{1,0:T(8,128)(2,1)} custom-call(bf16[1024,1024]{1,0:T(8,128)(2,1)} %get-tuple-element.135.refs_4_.refs_0_, bf16[1024,2048]{1,0:T(8,128)(2,1)} %constant_dynamic-update-slice_fusion.rows_ref.refs_1_, bf16[1024,1024]{1,0:T(8,128)(2,1)} %get-tuple-element.126.refs_4_.refs_2_, ...), custom_call_target="tpu_custom_call" | custom-call | flops 8589934592 | bytes 20971520 | tf_op jit(solution)/shard_map/weight_pass/pallas_call | solution.py:396
  891.9 8.4 weight_pass.16
  925.0 25.1 %attend_back.3 = (bf16[2048,768]{1,0:T(8,128)(2,1)S(1)}, f32[2,1,128]{2,1,0:T(1,128)S(1)}) custom-call(s32[1]{0:T(128)} %bitcast.15.length_ref, f32[2]{0:T(128)S(1)} %copy-done.23, bf16[2048,768]{1,0:T(8,128)(2,1)S(1)} %copy-done.25, bf16[2048,768]{1,0:T(8,128)(2,1)S(1)} %copy-done.25, bf16[2048,768]{1,0:T(8,128)(2,1)S(1)} %copy-done.25, ...), custom_call_target="tpu_custom_call" | custom-call | flops 10737418240 | bytes 10485760 | tf_op jit(solution)/shard_map/attend_back/pallas_call | solution.py:286
  966.8 9.1 weight_pass.17
  985.5 21.6 %weight_pass.15 = bf16[768,2048]{1,0:T(8,128)(2,1)} custom-call(bf16[2048,768]{1,0:T(8,128)(2,1)} %copy-done.6, bf16[2048,2048]{1,0:T(8,128)(2,1)} %copy-done.28, bf16[2048,768]{1,0:T(8,128)(2,1)} %copy-done.9, bf16[2048,2048]{1,0:T(8,128)(2,1)} %copy-done.29), custom_call_target="tpu_custom_call" | custom-call | flops 12884901888 | bytes 26214400 | tf_op jit(solution)/shard_map/weight_pass/pallas_call | solution.py:396
  1029.9 212.4 %spread_sums.1 = (f32[2,256,2048]{2,1,0:T(8,128)}, bf16[384,2048]{1,0:T(8,128)(2,1)}, bf16[2,128,1024]{2,1,0:T(8,128)(2,1)}) custom-call(bf16[4,256,2048]{2,1,0:T(8,128)(2,1)} %bitcast.137, bf16[4,256,2048]{2,1,0:T(8,128)(2,1)} %bitcast.138, bf16[3,256,2048]{2,1,0:T(8,128)(2,1)} %bitcast.159, bf16[4,4,128,1024]{3,2,1,0:T(8,128)(2,1)} %bitcast.152), custom_call_target="tpu_custom_call" | custom-call | bytes 134217728 | tf_op jit(solution)/shard_map/spread_sums/pallas_call | solution.py:1253
  (348 shorter events, 268.7 us)
Async XLA Ops:
  7.2 97.9 %all-gather.15.cloned.1.call-start = ((), (), s32[]{:S(2)}) async-start(), calls=%async_computation.18 | async-start | bytes 9437184 | tf_op jit(solution)/shard_map/all_gather | solution.py:1328
  10.5 207.8 %all-gather.7.cloned.1.call-start = ((), (), s32[]{:S(2)}) async-start(), calls=%async_computation.9 | async-start | bytes 9437184 | tf_op jit(solution)/shard_map/all_gather | solution.py:1328
  105.1 340.3 %all-gather.9.cloned.1.call-start = ((), (), s32[]{:S(2)}) async-start(), calls=%async_computation.10 | async-start | bytes 10485760 | tf_op jit(solution)/shard_map/all_gather | solution.py:1390
  308.3 60.6 %all-to-all-start = ((bf16[8,256,256]{2,1,0:T(8,128)(2,1)}), bf16[8,256,256]{2,1,0:T(8,128)(2,1)}, u32[]{:S(2)}, u32[]{:S(2)}) async-start(bf16[8,256,256]{2,1,0:T(8,128)(2,1)} %bitcast.12), calls=%async_computation | async-start | bytes 2097152 | tf_op jit(solution)/shard_map/all_to_all | solution.py:1398
  316.7 101.9 %collective-permute-start = (bf16[2048,1024]{1,0:T(8,128)(2,1)}, bf16[2048,1024]{1,0:T(8,128)(2,1)}, u32[]{:S(2)}, u32[]{:S(2)}) collective-permute-start(bf16[2048,1024]{1,0:T(8,128)(2,1)} %get-tuple-element.96), channel_id=1, source_target_pairs={{0,16},{16,0},{1,17},{17,1},{2,18},{18,2},{3,19},{19,3},{4,20},{20... | collective-permute-start | bytes 12582920 | tf_op jit(solution)/shard_map/ppermute | solution.py:465
  368.9 43.0 %all-to-all-start.1 = ((bf16[8,256,256]{2,1,0:T(8,128)(2,1)}), bf16[8,256,256]{2,1,0:T(8,128)(2,1)}, u32[]{:S(2)}, u32[]{:S(2)}) async-start(bf16[8,256,256]{2,1,0:T(8,128)(2,1)} %bitcast.18), calls=%async_computation.1 | async-start | bytes 2097152 | tf_op jit(solution)/shard_map/all_to_all | solution.py:1398
  375.5 132.6 %all-gather.11.cloned.1.call-start = ((), (), s32[]{:S(2)}) async-start(), calls=%async_computation.11 | async-start | bytes 5242880 | tf_op jit(solution)/shard_map/all_gather | solution.py:1441
  376.6 354.1 %reduce-scatter.6.cloned.1.call-start = ((), (), s32[]{:S(2)}) async-start(), calls=%async_computation.12 | async-start | bytes 5242880 | tf_op jit(solution)/shard_map/reduce_scatter | solution.py:1460
  430.5 24.1 %collective-permute-start.1 = (bf16[128,2048]{1,0:T(8,128)(2,1)}, bf16[128,2048]{1,0:T(8,128)(2,1)}, u32[]{:S(2)}, u32[]{:S(2)}) collective-permute-start(bf16[128,2048]{1,0:T(8,128)(2,1)} %get-tuple-element.232), channel_id=1, source_target_pairs={{0,8},{4,12},{8,0},{12,4},{1,9},{5,13},{9,1},{13,5},{2,10},{6,14},... | collective-permute-start | bytes 1572872 | tf_op jit(solution)/shard_map/ppermute | solution.py:546
  442.8 23.1 %collective-permute-start.3 = (bf16[128,2048]{1,0:T(8,128)(2,1)}, bf16[128,2048]{1,0:T(8,128)(2,1)}, u32[]{:S(2)}, u32[]{:S(2)}) collective-permute-start(bf16[128,2048]{1,0:T(8,128)(2,1)} %collective-permute-done.2), channel_id=1, source_target_pairs={{0,8},{4,12},{8,0},{12,4},{1,9},{5,13},{9,1},{13,5},{2,10},{6,14},... | collective-permute-start | bytes 1572872 | tf_op jit(solution)/shard_map/ppermute | solution.py:546
  443.9 27.2 %collective-permute-start.4 = (bf16[128,2048]{1,0:T(8,128)(2,1)S(1)}, bf16[128,2048]{1,0:T(8,128)(2,1)}, u32[]{:S(2)}, u32[]{:S(2)}) collective-permute-start(bf16[128,2048]{1,0:T(8,128)(2,1)S(1)} %get-tuple-element.230), channel_id=1, source_target_pairs={{0,4},{4,0},{8,12},{12,8},{1,5},{5,1},{9,13},{13,9},{2,6},{6,2},{1... | collective-permute-start | bytes 1572872 | tf_op jit(solution)/shard_map/ppermute | solution.py:546
  444.3 37.1 %collective-permute-start.6 = (bf16[128,2048]{1,0:T(8,128)(2,1)}, bf16[128,2048]{1,0:T(8,128)(2,1)}, u32[]{:S(2)}, u32[]{:S(2)}) collective-permute-start(bf16[128,2048]{1,0:T(8,128)(2,1)} %collective-permute-done.5), channel_id=1, source_target_pairs={{0,4},{4,0},{8,12},{12,8},{1,5},{5,1},{9,13},{13,9},{2,6},{6,2},{1... | collective-permute-start | bytes 1572872 | tf_op jit(solution)/shard_map/ppermute | solution.py:546
  445.4 85.5 %collective-permute-start.13 = (bf16[1024,4096]{1,0:T(8,128)(2,1)}, bf16[1024,4096]{1,0:T(8,128)(2,1)}, u32[]{:S(2)}, u32[]{:S(2)}) collective-permute-start(bf16[1024,4096]{1,0:T(8,128)(2,1)} %all-gather.9.cloned.1.call-done.inner_ref.refs_6_.refs_8_), channel_id=1, source_target_pairs={{0,16},{16,0},{1,17},{17,1},{2,18},{18,2},{3,19},{19,3},{4,20},{20... | collective-permute-start | bytes 25165832 | tf_op jit(solution)/shard_map/ppermute | solution.py:465
  469.9 24.1 %collective-permute-start.7 = (bf16[128,2048]{1,0:T(8,128)(2,1)S(1)}, bf16[128,2048]{1,0:T(8,128)(2,1)S(1)}, u32[]{:S(2)}, u32[]{:S(2)}) collective-permute-start(bf16[128,2048]{1,0:T(8,128)(2,1)S(1)} %get-tuple-element.237), channel_id=1, source_target_pairs={{0,8},{4,12},{8,0},{12,4},{1,9},{5,13},{9,1},{13,5},{2,10},{6,14},... | collective-permute-start | bytes 1572872 | tf_op jit(solution)/shard_map/ppermute | solution.py:546
  471.1 21.8 %collective-permute-start.11 = (bf16[128,2048]{1,0:T(8,128)(2,1)S(1)}, bf16[128,2048]{1,0:T(8,128)(2,1)S(1)}, u32[]{:S(2)}, u32[]{:S(2)}) collective-permute-start(bf16[128,2048]{1,0:T(8,128)(2,1)S(1)} %get-tuple-element.235), channel_id=1, source_target_pairs={{0,8},{4,12},{8,0},{12,4},{1,9},{5,13},{9,1},{13,5},{2,10},{6,14},... | collective-permute-start | bytes 1572872 | tf_op jit(solution)/shard_map/ppermute | solution.py:546
  480.7 23.2 %collective-permute-start.9 = (bf16[128,2048]{1,0:T(8,128)(2,1)S(1)}, bf16[128,2048]{1,0:T(8,128)(2,1)S(1)}, u32[]{:S(2)}, u32[]{:S(2)}) collective-permute-start(bf16[128,2048]{1,0:T(8,128)(2,1)S(1)} %collective-permute-done.8), channel_id=1, source_target_pairs={{0,8},{4,12},{8,0},{12,4},{1,9},{5,13},{9,1},{13,5},{2,10},{6,14},... | collective-permute-start | bytes 1572872 | tf_op jit(solution)/shard_map/ppermute | solution.py:546
  483.2 22.4 %collective-permute-start.10 = (bf16[128,2048]{1,0:T(8,128)(2,1)S(1)}, bf16[128,2048]{1,0:T(8,128)(2,1)S(1)}, u32[]{:S(2)}, u32[]{:S(2)}) collective-permute-start(bf16[128,2048]{1,0:T(8,128)(2,1)S(1)} %get-tuple-element.235), channel_id=1, source_target_pairs={{0,4},{4,0},{8,12},{12,8},{1,5},{5,1},{9,13},{13,9},{2,6},{6,2},{1... | collective-permute-start | bytes 1572872 | tf_op jit(solution)/shard_map/ppermute | solution.py:546
  508.1 22.7 %collective-permute-start.14 = (bf16[1024,2048]{1,0:T(8,128)(2,1)}, bf16[1024,2048]{1,0:T(8,128)(2,1)S(1)}, u32[]{:S(2)}, u32[]{:S(2)}) collective-permute-start(bf16[1024,2048]{1,0:T(8,128)(2,1)} %all-gather.11.cloned.1.call-done.down_ref.refs_10_), channel_id=1, source_target_pairs={{0,16},{16,0},{1,17},{17,1},{2,18},{18,2},{3,19},{19,3},{4,20},{20... | collective-permute-start | bytes 12582920 | tf_op jit(solution)/shard_map/ppermute | solution.py:465
  637.1 209.2 %reduce-scatter.10.cloned.1.call-start = ((), (), s32[]{:S(2)}) async-start(), calls=%async_computation.14 | async-start | bytes 5242880 | tf_op jit(solution)/shard_map/reduce_scatter | solution.py:1460
  637.2 76.7 %collective-permute-start.16 = (bf16[1024,2048]{1,0:T(8,128)(2,1)}, bf16[1024,2048]{1,0:T(8,128)(2,1)S(1)}, u32[]{:S(2)}, u32[]{:S(2)}) collective-permute-start(bf16[1024,2048]{1,0:T(8,128)(2,1)} %weight_pass.10), channel_id=1, source_target_pairs={{0,16},{16,0},{1,17},{17,1},{2,18},{18,2},{3,19},{19,3},{4,20},{20... | collective-permute-start | bytes 12582920 | tf_op jit(solution)/shard_map/ppermute | solution.py:465
  730.7 188.3 %reduce-scatter.8.cloned.1.call-start = ((), (), s32[]{:S(2)}) async-start(), calls=%async_computation.13 | async-start | bytes 5242880 | tf_op jit(solution)/shard_map/reduce_scatter | solution.py:1545
  799.8 76.8 %collective-permute-start.18 = (bf16[1024,2048]{1,0:T(8,128)(2,1)}, bf16[1024,2048]{1,0:T(8,128)(2,1)}, u32[]{:S(2)}, u32[]{:S(2)}) collective-permute-start(bf16[1024,2048]{1,0:T(8,128)(2,1)} %weight_pass.12), channel_id=1, source_target_pairs={{0,16},{16,0},{1,17},{17,1},{2,18},{18,2},{3,19},{19,3},{4,20},{20... | collective-permute-start | bytes 12582920 | tf_op jit(solution)/shard_map/ppermute | solution.py:465
  807.4 33.4 %all-to-all-start.2 = ((bf16[8,256,256]{2,1,0:T(8,128)(2,1)}), bf16[8,256,256]{2,1,0:T(8,128)(2,1)S(1)}, u32[]{:S(2)}, u32[]{:S(2)}) async-start(bf16[8,256,256]{2,1,0:T(8,128)(2,1)} %bitcast.136), calls=%async_computation.4 | async-start | bytes 2097152 | tf_op jit(solution)/shard_map/all_to_all | solution.py:1499
  840.8 35.9 %all-to-all-start.3 = ((bf16[8,256,256]{2,1,0:T(8,128)(2,1)}), bf16[8,256,256]{2,1,0:T(8,128)(2,1)S(1)}, u32[]{:S(2)}, u32[]{:S(2)}) async-start(bf16[8,256,256]{2,1,0:T(8,128)(2,1)} %bitcast.153), calls=%async_computation.6 | async-start | bytes 2097152 | tf_op jit(solution)/shard_map/all_to_all | solution.py:1499
  846.3 160.7 %reduce-scatter.12.cloned.1.call-start = ((), (), s32[]{:S(2)}) async-start(), calls=%async_computation.15 | async-start | bytes 5242880 | tf_op jit(solution)/shard_map/reduce_scatter | solution.py:1460
  891.9 350.4 %reduce-scatter.14.cloned.1.call-start = ((), (), s32[]{:S(2)}) async-start(), calls=%async_computation.16 | async-start | bytes 5242880 | tf_op jit(solution)/shard_map/reduce_scatter | solution.py:1545
  900.3 66.4 %collective-permute-start.20 = (bf16[2048,1024]{1,0:T(8,128)(2,1)}, bf16[2048,1024]{1,0:T(8,128)(2,1)}, u32[]{:S(2)}, u32[]{:S(2)}) collective-permute-start(bf16[2048,1024]{1,0:T(8,128)(2,1)} %weight_pass.16), channel_id=1, source_target_pairs={{0,16},{16,0},{1,17},{17,1},{2,18},{18,2},{3,19},{19,3},{4,20},{20... | collective-permute-start | bytes 12582920 | tf_op jit(solution)/shard_map/ppermute | solution.py:465
  900.7 362.2 %all-gather.13.cloned.1.call-start = ((), (), s32[]{:S(2)}) async-start(), calls=%async_computation.17 | async-start | bytes 2162688 | tf_op jit(solution)/shard_map/all_gather | solution.py:1605
  911.9 64.0 %collective-permute-start.17 = (bf16[1024,2048]{1,0:T(8,128)(2,1)}, bf16[1024,2048]{1,0:T(8,128)(2,1)}, u32[]{:S(2)}, u32[]{:S(2)}) collective-permute-start(bf16[1024,2048]{1,0:T(8,128)(2,1)} %get-tuple-element.133), channel_id=1, source_target_pairs={{0,16},{16,0},{1,17},{17,1},{2,18},{18,2},{3,19},{19,3},{4,20},{20... | collective-permute-start | bytes 12582920 | tf_op jit(solution)/shard_map/ppermute | solution.py:465
  917.5 46.4 %collective-permute-start.22 = (bf16[256,2048]{1,0:T(8,128)(2,1)}, bf16[256,2048]{1,0:T(8,128)(2,1)}, u32[]{:S(2)}, u32[]{:S(2)}) collective-permute-start(bf16[256,2048]{1,0:T(8,128)(2,1)} %reduce-scatter.6.cloned.1.call-done), channel_id=1, source_target_pairs={{0,16},{16,0},{1,17},{17,1},{2,18},{18,2},{3,19},{19,3},{4,20},{20... | collective-permute-start | bytes 3145736 | tf_op jit(solution)/shard_map/ppermute | solution.py:465
  958.4 57.7 %collective-permute-start.19 = (bf16[1024,2048]{1,0:T(8,128)(2,1)}, bf16[1024,2048]{1,0:T(8,128)(2,1)}, u32[]{:S(2)}, u32[]{:S(2)}) collective-permute-start(bf16[1024,2048]{1,0:T(8,128)(2,1)} %get-tuple-element.141), channel_id=1, source_target_pairs={{0,16},{16,0},{1,17},{17,1},{2,18},{18,2},{3,19},{19,3},{4,20},{20... | collective-permute-start | bytes 12582920 | tf_op jit(solution)/shard_map/ppermute | solution.py:465
  1009.4 16.4 %collective-permute-start.21 = (bf16[256,4096]{1,0:T(8,128)(2,1)}, bf16[256,4096]{1,0:T(8,128)(2,1)}, u32[]{:S(2)}, u32[]{:S(2)}) collective-permute-start(bf16[256,4096]{1,0:T(8,128)(2,1)} %constant_dynamic-update-slice_fusion.16), channel_id=1, source_target_pairs={{0,16},{16,0},{1,17},{17,1},{2,18},{18,2},{3,19},{19,3},{4,20},{20... | collective-permute-start | bytes 6291464 | tf_op jit(solution)/shard_map/ppermute | solution.py:465
  (92 other events, 2597.7 us)
Sparse Core Ops, SparseCore 0:
  10.6 94.3 all-gather.14
  107.2 102.6 all-gather.6
  218.5 193.1 all-gather.8
  413.2 80.3 all-gather.10
  637.2 77.3 reduce-scatter.5
  730.8 78.5 reduce-scatter.9
  812.3 52.6 reduce-scatter.7
  892.0 77.1 reduce-scatter.11
  972.1 52.6 reduce-scatter.13
  1028.1 103.1 all-gather.12

commit v6 on v5

--- a/solution.py
+++ b/solution.py
@@ -913,13 +913,16 @@
         if stage + 1 < stages:
             send(t, stage + 1)
 
+    @pl.when(step >= 1)
+    def _():
+        send(step - 1, 0)
+
     parts[step] = (
         nn(gates[0][...], gate_w[0][...])
         + nn(gates[1][...], gate_w[1][...])
         + nn(ups[0][...], up_w[0][...])
         + nn(ups[1][...], up_w[1][...])
     ).astype(BF16)
-    send(step, 0)
     out = (
         nn(hidden[0][...], down_w[0][...]) + nn(hidden[1][...], down_w[1][...])
     ).astype(BF16)
@@ -937,6 +940,7 @@
 
     @pl.when(step == steps - 1)
     def _():
+        send(step, 0)
         for stage in range(stages):
             for back in reversed(range(2 * (stage + 1))):
                 take(steps - 1 - back, stage)

time: 1280 us -> 1260 us (0.984)
  Pallas kernels: 899 us -> 860 us
    pallas_call x2, Pallas kernels: 124 us -> 99.1 us  [row_pass(): pl.pallas_call(functools.partial(row_kernel, dp_count), grid=(tiles,), in...]
    pallas_call x2, Pallas kernels: 50.3 us -> 34.8 us  [attend_back(): pl.pallas_call(functools.partial(attend_back_kernel, block), grid=(heads,...]
    pallas_call x1, Pallas kernels: 212 us -> 227 us  [spread_sums(): pl.pallas_call(functools.partial(spread_kernel, sizes, micros), in_specs=...]
  transfers between devices with their start and end apart: 37 -> 37, of which waited for: 10 -> 10; matrix products, arithmetic and copies ran while one was open for 8% -> 9% of each run, Pallas kernels for 64% -> 62%
where the time goes in v6:
time: 1260 us; the launch traced here: 1250 us
  Pallas kernels  860 us (68%)
  waiting for transfers between devices  152 us (12%)
  local copies, waits for them, and re-layouts  108 us (9%)
  starting transfers between devices  53 us (4%)
  other arithmetic  42.8 us (3%)
  matrix products  20.6 us (2%)
  between operations  15.5 us (1%)
    pallas_call x1, Pallas kernels, spread_sums(): pl.pallas_call(functools.partial(spread_kernel, sizes, micros), in_specs=...  227 us
    pallas_call x9, Pallas kernels, weight_pass(): pl.pallas_call(functools.partial(weight_kernel, len(pairs)), grid=(size /...  127 us
    pallas_call x1, Pallas kernels, gather_rest(): pl.pallas_call(functools.partial(rest_kernel, sizes), in_specs=[anywhere]...  104 us
    pallas_call x2, Pallas kernels, row_pass(): pl.pallas_call(functools.partial(row_kernel, dp_count), grid=(tiles,), in...  99.1 us
    pallas_call x4, Pallas kernels, unit_pass(): pl.pallas_call(unit_kernel, grid=(units // tile,), in_specs=[resident, re...  78.5 us
    unnamed x188, local copies, waits for them, and re-layouts  75.1 us
    pallas_call x1, Pallas kernels, gather_heads(): pl.pallas_call(functools.partial(heads_kernel, sizes), in_specs=[anywhere...  59.7 us
    all_to_all x2, waiting for transfers between devices, shards(): lax.all_to_all(mixed_heads.reshape(span_count, span_rows, block_rows), ('...  53.4 us
  transfers between devices with their start and end apart: 37, of which 10 were waited for; matrix products, arithmetic and copies ran while one was open for 9% of the time, Pallas kernels for 62%

profile of v6, /device:TPU:17, one launch (start us, length us, event | category | flops | bytes accessed | tf_op | source)
XLA Modules:
  0.0 1251.2 jit_solution(15786954471749457122)
XLA Ops:
  12.1 59.7 %gather_heads.1 = (bf16[768,2048]{1,0:T(8,128)(2,1)S(1)}, f32[16,8,128]{2,1,0:T(8,128)S(1)}) custom-call(bf16[384,2048]{1,0:T(8,128)(2,1)S(1)} %copy-done.13, f32[8,128]{1,0:T(8,128)S(1)} %pad_convert_fusion.gain_ref), custom_call_target="tpu_custom_call" | custom-call | bytes 33554432 | tf_op jit(solution)/shard_map/gather_heads/pallas_call | solution.py:715
  73.4 31.6 %all-gather.15.cloned.1.call-done = bf16[1,1,2048,2048]{3,2,1,0:T(8,128)(2,1)} async-done(((bf16[1,1,256,2048]{3,2,1,0:T(8,128)(2,1)}), bf16[1,1,2048,2048]{3,2,1,0:T(8,128)(2,1)}) %all-gather.15.cloned.1.call-update) | async-done | bytes 8388624 | tf_op jit(solution)/shard_map/all_gather | solution.py:1332
  114.2 104.1 %gather_rest.1 = (bf16[2048,1024]{1,0:T(8,128)(2,1)}, bf16[1024,2048]{1,0:T(8,128)(2,1)}) custom-call(bf16[128,1024]{1,0:T(8,128)(2,1)} %constant_dynamic-slice_fusion.9.refs_0_, bf16[256,2048]{1,0:T(8,128)(2,1)} %get-tuple-element.222.refs_1_), custom_call_target="tpu_custom_call" | custom-call | bytes 4194304 | tf_op jit(solution)/shard_map/gather_rest/pallas_call | solution.py:846
  221.4 47.4 %gather_cot.1.grad_ref.refs_3_ = bf16[1024,2048]{1,0:T(8,128)(2,1)} custom-call(bf16[256,2048]{1,0:T(8,128)(2,1)} %get-tuple-element.91.cot_ref), custom_call_target="tpu_custom_call" | custom-call | bytes 4194304 | tf_op jit(solution)/shard_map/gather_cot/pallas_call | solution.py:786
  270.7 11.3 project.2
  285.4 17.5 %attend.2 = (bf16[2048,256]{1,0:T(8,128)(2,1)}, f32[2048,256]{1,0:T(8,128)S(1)}, f32[2,1,2048]{2,1,0:T(1,128)S(1)}, f32[2,128,128]{2,1,0:T(8,128)S(1)}, f32[2,1,128]{2,1,0:T(1,128)S(1)}) custom-call(s32[1]{0:T(128)} %bitcast.1.length_ref, f32[2]{0:T(128)S(1)} %dynamic_slice.43.gate_ref, bf16[2048,768]{1,0:T(8,128)(2,1)S(1)} %get-tuple-element.94.q_ref.k_ref.v_ref, ...), custom_call_target="tpu_custom_call" | custom-call | flops 4294967296 | bytes 6291456 | tf_op jit(solution)/shard_map/attend/pallas_call | solution.py:156
  314.9 11.3 project.3
  329.6 13.0 %attend.3 = (bf16[2048,256]{1,0:T(8,128)(2,1)}, f32[2048,256]{1,0:T(8,128)S(1)}, f32[2,1,2048]{2,1,0:T(1,128)S(1)}, f32[2,128,128]{2,1,0:T(8,128)S(1)}, f32[2,1,128]{2,1,0:T(1,128)S(1)}) custom-call(s32[1]{0:T(128)} %bitcast.15.length_ref, f32[2]{0:T(128)S(1)} %dynamic_slice.43.gate_ref, bf16[2048,768]{1,0:T(8,128)(2,1)S(1)} %get-tuple-element.99.q_ref.k_ref.v_ref, ...), custom_call_target="tpu_custom_call" | custom-call | flops 4294967296 | bytes 6291456 | tf_op jit(solution)/shard_map/attend/pallas_call | solution.py:156
  346.2 15.1 %all-to-all-done = bf16[8,256,256]{2,1,0:T(8,128)(2,1)} async-done(((bf16[8,256,256]{2,1,0:T(8,128)(2,1)}), bf16[8,256,256]{2,1,0:T(8,128)(2,1)}, u32[]{:S(2)}, u32[]{:S(2)}) %all-to-all-start) | async-done | bytes 1048608 | tf_op jit(solution)/shard_map/all_to_all | solution.py:1402
  371.9 38.3 %all-to-all-done.1 = bf16[8,256,256]{2,1,0:T(8,128)(2,1)} async-done(((bf16[8,256,256]{2,1,0:T(8,128)(2,1)}), bf16[8,256,256]{2,1,0:T(8,128)(2,1)}, u32[]{:S(2)}, u32[]{:S(2)}) %all-to-all-start.1) | async-done | bytes 1048608 | tf_op jit(solution)/shard_map/all_to_all | solution.py:1402
  430.6 10.3 collective-permute-done.2
  484.1 9.1 collective-permute-done.11
  494.8 9.5 collective-permute-done.9
  510.9 20.0 %unit_pass.4 = (bf16[1024,1024]{1,0:T(8,128)(2,1)}, bf16[1024,1024]{1,0:T(8,128)(2,1)}, bf16[1024,1024]{1,0:T(8,128)(2,1)}) custom-call(bf16[1024,2048]{1,0:T(8,128)(2,1)} %constant_dynamic-update-slice_fusion.rows_ref.refs_1_, bf16[1024,2048]{1,0:T(8,128)(2,1)} %get-tuple-element.90.grad_ref.refs_1_, ...), custom_call_target="tpu_custom_call" | custom-call | flops 12884901888 | bytes 27262976 | tf_op jit(solution)/shard_map/unit_pass/pallas_call | solution.py:348
  533.0 19.5 %unit_pass.5 = (bf16[1024,1024]{1,0:T(8,128)(2,1)}, bf16[1024,1024]{1,0:T(8,128)(2,1)}, bf16[1024,1024]{1,0:T(8,128)(2,1)}) custom-call(bf16[1024,2048]{1,0:T(8,128)(2,1)} %constant_dynamic-update-slice_fusion.rows_ref.refs_1_, bf16[1024,2048]{1,0:T(8,128)(2,1)} %get-tuple-element.90.grad_ref.refs_1_, ...), custom_call_target="tpu_custom_call" | custom-call | flops 12884901888 | bytes 27262976 | tf_op jit(solution)/shard_map/unit_pass/pallas_call | solution.py:348
  552.4 19.5 %unit_pass.6 = (bf16[1024,1024]{1,0:T(8,128)(2,1)}, bf16[1024,1024]{1,0:T(8,128)(2,1)}, bf16[1024,1024]{1,0:T(8,128)(2,1)}) custom-call(bf16[1024,2048]{1,0:T(8,128)(2,1)} %constant_dynamic-update-slice_fusion.8.rows_ref.refs_3_, bf16[1024,2048]{1,0:T(8,128)(2,1)} %gather_cot.1.grad_ref.refs_3_, ...), custom_call_target="tpu_custom_call" | custom-call | flops 12884901888 | bytes 27262976 | tf_op jit(solution)/shard_map/unit_pass/pallas_call | solution.py:348
  571.9 19.6 %unit_pass.7 = (bf16[1024,1024]{1,0:T(8,128)(2,1)}, bf16[1024,1024]{1,0:T(8,128)(2,1)}, bf16[1024,1024]{1,0:T(8,128)(2,1)}) custom-call(bf16[1024,2048]{1,0:T(8,128)(2,1)} %constant_dynamic-update-slice_fusion.8.rows_ref.refs_3_, bf16[1024,2048]{1,0:T(8,128)(2,1)} %gather_cot.1.grad_ref.refs_3_, ...), custom_call_target="tpu_custom_call" | custom-call | flops 12884901888 | bytes 27262976 | tf_op jit(solution)/shard_map/unit_pass/pallas_call | solution.py:348
  591.5 14.5 %weight_pass.9 = bf16[1024,2048]{1,0:T(8,128)(2,1)} custom-call(bf16[1024,1024]{1,0:T(8,128)(2,1)} %get-tuple-element.112.refs_0_.refs_1_, bf16[1024,2048]{1,0:T(8,128)(2,1)} %get-tuple-element.90.grad_ref.refs_1_, bf16[1024,1024]{1,0:T(8,128)(2,1)} %get-tuple-element.111.refs_2_.refs_1_, bf16[1024,2048]{1,0:T(8,128)(2,1)} %gather_cot.1.grad_ref.refs_3_), custom_call_target="tpu_custom_call" | custom-call | flops 8589934592 | bytes 16777216 | tf_op jit(solution)/shard_map/weight_pass/pallas_call | solution.py:396
  606.0 14.3 %weight_pass.10 = bf16[1024,2048]{1,0:T(8,128)(2,1)} custom-call(bf16[1024,1024]{1,0:T(8,128)(2,1)} %get-tuple-element.113.refs_0_.refs_3_, bf16[1024,2048]{1,0:T(8,128)(2,1)} %constant_dynamic-update-slice_fusion.rows_ref.refs_1_, bf16[1024,1024]{1,0:T(8,128)(2,1)} %get-tuple-element.114.refs_2_.refs_3_, ...), custom_call_target="tpu_custom_call" | custom-call | flops 8589934592 | bytes 16777216 | tf_op jit(solution)/shard_map/weight_pass/pallas_call | solution.py:396
  622.3 14.7 %weight_pass.11 = bf16[1024,2048]{1,0:T(8,128)(2,1)} custom-call(bf16[1024,1024]{1,0:T(8,128)(2,1)} %get-tuple-element.115.refs_0_, bf16[1024,2048]{1,0:T(8,128)(2,1)} %get-tuple-element.90.grad_ref.refs_1_, bf16[1024,1024]{1,0:T(8,128)(2,1)} %get-tuple-element.109.refs_2_.refs_0_, bf16[1024,2048]{1,0:T(8,128)(2,1)} %gather_cot.1.grad_ref.refs_3_, ...), custom_call_target="tpu_custom_call" | custom-call | flops 8589934592 | bytes 20971520 | tf_op jit(solution)/shard_map/weight_pass/pallas_call | solution.py:396
  637.7 49.6 %row_pass.2 = (bf16[1024,2048]{1,0:T(8,128)(2,1)}, f32[256,2048]{1,0:T(8,128)}) custom-call(bf16[1024,1024]{1,0:T(8,128)(2,1)} %get-tuple-element.115.refs_0_, bf16[1024,1024]{1,0:T(8,128)(2,1)} %get-tuple-element.112.refs_0_.refs_1_, bf16[1024,1024]{1,0:T(8,128)(2,1)} %get-tuple-element.124.refs_2_.refs_0_, ...), custom_call_target="tpu_custom_call" | custom-call | flops 25769803776 | bytes 46137344 | tf_op jit(solution)/shard_map/row_pass/pallas_call | solution.py:960
  687.3 14.5 %weight_pass.12 = bf16[1024,2048]{1,0:T(8,128)(2,1)} custom-call(bf16[1024,1024]{1,0:T(8,128)(2,1)} %get-tuple-element.122.refs_5_.refs_0_, bf16[1024,2048]{1,0:T(8,128)(2,1)} %constant_dynamic-update-slice_fusion.rows_ref.refs_1_, bf16[1024,1024]{1,0:T(8,128)(2,1)} %get-tuple-element.123.refs_2_.refs_5_, ...), custom_call_target="tpu_custom_call" | custom-call | flops 8589934592 | bytes 16777216 | tf_op jit(solution)/shard_map/weight_pass/pallas_call | solution.py:396
  703.7 14.8 %weight_pass.13 = bf16[1024,2048]{1,0:T(8,128)(2,1)} custom-call(bf16[1024,1024]{1,0:T(8,128)(2,1)} %get-tuple-element.124.refs_2_.refs_0_, bf16[1024,2048]{1,0:T(8,128)(2,1)} %constant_dynamic-update-slice_fusion.rows_ref.refs_1_, bf16[1024,1024]{1,0:T(8,128)(2,1)} %get-tuple-element.125.refs_2_, ...), custom_call_target="tpu_custom_call" | custom-call | flops 8589934592 | bytes 20971520 | tf_op jit(solution)/shard_map/weight_pass/pallas_call | solution.py:396
  718.6 49.5 %row_pass.3 = (bf16[1024,2048]{1,0:T(8,128)(2,1)}, f32[256,2048]{1,0:T(8,128)}) custom-call(bf16[1024,1024]{1,0:T(8,128)(2,1)} %get-tuple-element.109.refs_2_.refs_0_, bf16[1024,1024]{1,0:T(8,128)(2,1)} %get-tuple-element.111.refs_2_.refs_1_, bf16[1024,1024]{1,0:T(8,128)(2,1)} %get-tuple-element.125.refs_2_, ...), custom_call_target="tpu_custom_call" | custom-call | flops 25769803776 | bytes 46137344 | tf_op jit(solution)/shard_map/row_pass/pallas_call | solution.py:960
  783.2 9.3 all-to-all-start.2
  798.5 19.6 %all-to-all-done.2 = bf16[8,256,256]{2,1,0:T(8,128)(2,1)S(1)} async-done(((bf16[8,256,256]{2,1,0:T(8,128)(2,1)}), bf16[8,256,256]{2,1,0:T(8,128)(2,1)S(1)}, u32[]{:S(2)}, u32[]{:S(2)}) %all-to-all-start.2) | async-done | bytes 1048608 | tf_op jit(solution)/shard_map/all_to_all | solution.py:1503
  827.3 20.3 %attend_back.2 = (bf16[2048,768]{1,0:T(8,128)(2,1)S(1)}, f32[2,1,128]{2,1,0:T(1,128)S(1)}) custom-call(s32[1]{0:T(128)} %bitcast.1.length_ref, f32[2]{0:T(128)S(1)} %dynamic_slice.43.gate_ref, bf16[2048,768]{1,0:T(8,128)(2,1)S(1)} %copy-done.27, bf16[2048,768]{1,0:T(8,128)(2,1)S(1)} %copy-done.27, bf16[2048,768]{1,0:T(8,128)(2,1)S(1)} %copy-done.27, ...), custom_call_target="tpu_custom_call" | custom-call | flops 10737418240 | bytes 10485760 | tf_op jit(solution)/shard_map/attend_back/pallas_call | solution.py:286
  849.3 15.3 %weight_pass.14 = bf16[1024,2048]{1,0:T(8,128)(2,1)} custom-call(bf16[1024,1024]{1,0:T(8,128)(2,1)} %get-tuple-element.135.refs_4_.refs_0_, bf16[1024,2048]{1,0:T(8,128)(2,1)} %constant_dynamic-update-slice_fusion.rows_ref.refs_1_, bf16[1024,1024]{1,0:T(8,128)(2,1)} %get-tuple-element.126.refs_4_.refs_2_, ...), custom_call_target="tpu_custom_call" | custom-call | flops 8589934592 | bytes 20971520 | tf_op jit(solution)/shard_map/weight_pass/pallas_call | solution.py:396
  898.1 14.5 %attend_back.3 = (bf16[2048,768]{1,0:T(8,128)(2,1)S(1)}, f32[2,1,128]{2,1,0:T(1,128)S(1)}) custom-call(s32[1]{0:T(128)} %bitcast.15.length_ref, f32[2]{0:T(128)S(1)} %copy-done.23, bf16[2048,768]{1,0:T(8,128)(2,1)S(1)} %copy-done.25, bf16[2048,768]{1,0:T(8,128)(2,1)S(1)} %copy-done.25, bf16[2048,768]{1,0:T(8,128)(2,1)S(1)} %copy-done.25, ...), custom_call_target="tpu_custom_call" | custom-call | flops 10737418240 | bytes 10485760 | tf_op jit(solution)/shard_map/attend_back/pallas_call | solution.py:286
  929.5 9.2 weight_pass.17
  947.8 21.0 %weight_pass.15 = bf16[768,2048]{1,0:T(8,128)(2,1)} custom-call(bf16[2048,768]{1,0:T(8,128)(2,1)} %copy-done.6, bf16[2048,2048]{1,0:T(8,128)(2,1)} %copy-done.28, bf16[2048,768]{1,0:T(8,128)(2,1)} %copy-done.9, bf16[2048,2048]{1,0:T(8,128)(2,1)} %copy-done.29), custom_call_target="tpu_custom_call" | custom-call | flops 12884901888 | bytes 26214400 | tf_op jit(solution)/shard_map/weight_pass/pallas_call | solution.py:396
  991.5 226.9 %spread_sums.1 = (f32[2,256,2048]{2,1,0:T(8,128)}, bf16[384,2048]{1,0:T(8,128)(2,1)}, bf16[2,128,1024]{2,1,0:T(8,128)(2,1)}) custom-call(bf16[4,256,2048]{2,1,0:T(8,128)(2,1)} %bitcast.137, bf16[4,256,2048]{2,1,0:T(8,128)(2,1)} %bitcast.138, bf16[3,256,2048]{2,1,0:T(8,128)(2,1)} %bitcast.159, bf16[4,4,128,1024]{3,2,1,0:T(8,128)(2,1)} %bitcast.152), custom_call_target="tpu_custom_call" | custom-call | bytes 134217728 | tf_op jit(solution)/shard_map/spread_sums/pallas_call | solution.py:1257
  (348 shorter events, 270.9 us)
Async XLA Ops:
  7.2 97.9 %all-gather.15.cloned.1.call-start = ((), (), s32[]{:S(2)}) async-start(), calls=%async_computation.18 | async-start | bytes 9437184 | tf_op jit(solution)/shard_map/all_gather | solution.py:1332
  10.5 207.8 %all-gather.7.cloned.1.call-start = ((), (), s32[]{:S(2)}) async-start(), calls=%async_computation.9 | async-start | bytes 9437184 | tf_op jit(solution)/shard_map/all_gather | solution.py:1332
  105.1 340.3 %all-gather.9.cloned.1.call-start = ((), (), s32[]{:S(2)}) async-start(), calls=%async_computation.10 | async-start | bytes 10485760 | tf_op jit(solution)/shard_map/all_gather | solution.py:1394
  304.2 57.1 %all-to-all-start = ((bf16[8,256,256]{2,1,0:T(8,128)(2,1)}), bf16[8,256,256]{2,1,0:T(8,128)(2,1)}, u32[]{:S(2)}, u32[]{:S(2)}) async-start(bf16[8,256,256]{2,1,0:T(8,128)(2,1)} %bitcast.12), calls=%async_computation | async-start | bytes 2097152 | tf_op jit(solution)/shard_map/all_to_all | solution.py:1402
  312.6 104.3 %collective-permute-start = (bf16[2048,1024]{1,0:T(8,128)(2,1)}, bf16[2048,1024]{1,0:T(8,128)(2,1)}, u32[]{:S(2)}, u32[]{:S(2)}) collective-permute-start(bf16[2048,1024]{1,0:T(8,128)(2,1)} %get-tuple-element.96), channel_id=1, source_target_pairs={{0,16},{16,0},{1,17},{17,1},{2,18},{18,2},{3,19},{19,3},{4,20},{20... | collective-permute-start | bytes 12582920 | tf_op jit(solution)/shard_map/ppermute | solution.py:465
  361.3 48.8 %all-to-all-start.1 = ((bf16[8,256,256]{2,1,0:T(8,128)(2,1)}), bf16[8,256,256]{2,1,0:T(8,128)(2,1)}, u32[]{:S(2)}, u32[]{:S(2)}) async-start(bf16[8,256,256]{2,1,0:T(8,128)(2,1)} %bitcast.18), calls=%async_computation.1 | async-start | bytes 2097152 | tf_op jit(solution)/shard_map/all_to_all | solution.py:1402
  369.1 139.3 %all-gather.11.cloned.1.call-start = ((), (), s32[]{:S(2)}) async-start(), calls=%async_computation.11 | async-start | bytes 5242880 | tf_op jit(solution)/shard_map/all_gather | solution.py:1445
  370.3 348.3 %reduce-scatter.6.cloned.1.call-start = ((), (), s32[]{:S(2)}) async-start(), calls=%async_computation.12 | async-start | bytes 5242880 | tf_op jit(solution)/shard_map/reduce_scatter | solution.py:1464
  430.5 22.6 %collective-permute-start.1 = (bf16[128,2048]{1,0:T(8,128)(2,1)}, bf16[128,2048]{1,0:T(8,128)(2,1)}, u32[]{:S(2)}, u32[]{:S(2)}) collective-permute-start(bf16[128,2048]{1,0:T(8,128)(2,1)} %get-tuple-element.232), channel_id=1, source_target_pairs={{0,8},{4,12},{8,0},{12,4},{1,9},{5,13},{9,1},{13,5},{2,10},{6,14},... | collective-permute-start | bytes 1572872 | tf_op jit(solution)/shard_map/ppermute | solution.py:546
  440.9 23.5 %collective-permute-start.3 = (bf16[128,2048]{1,0:T(8,128)(2,1)}, bf16[128,2048]{1,0:T(8,128)(2,1)}, u32[]{:S(2)}, u32[]{:S(2)}) collective-permute-start(bf16[128,2048]{1,0:T(8,128)(2,1)} %collective-permute-done.2), channel_id=1, source_target_pairs={{0,8},{4,12},{8,0},{12,4},{1,9},{5,13},{9,1},{13,5},{2,10},{6,14},... | collective-permute-start | bytes 1572872 | tf_op jit(solution)/shard_map/ppermute | solution.py:546
  443.9 27.2 %collective-permute-start.4 = (bf16[128,2048]{1,0:T(8,128)(2,1)S(1)}, bf16[128,2048]{1,0:T(8,128)(2,1)}, u32[]{:S(2)}, u32[]{:S(2)}) collective-permute-start(bf16[128,2048]{1,0:T(8,128)(2,1)S(1)} %get-tuple-element.230), channel_id=1, source_target_pairs={{0,4},{4,0},{8,12},{12,8},{1,5},{5,1},{9,13},{13,9},{2,6},{6,2},{1... | collective-permute-start | bytes 1572872 | tf_op jit(solution)/shard_map/ppermute | solution.py:546
  444.2 37.0 %collective-permute-start.6 = (bf16[128,2048]{1,0:T(8,128)(2,1)}, bf16[128,2048]{1,0:T(8,128)(2,1)}, u32[]{:S(2)}, u32[]{:S(2)}) collective-permute-start(bf16[128,2048]{1,0:T(8,128)(2,1)} %collective-permute-done.5), channel_id=1, source_target_pairs={{0,4},{4,0},{8,12},{12,8},{1,5},{5,1},{9,13},{13,9},{2,6},{6,2},{1... | collective-permute-start | bytes 1572872 | tf_op jit(solution)/shard_map/ppermute | solution.py:546
  445.4 85.5 %collective-permute-start.13 = (bf16[1024,4096]{1,0:T(8,128)(2,1)}, bf16[1024,4096]{1,0:T(8,128)(2,1)}, u32[]{:S(2)}, u32[]{:S(2)}) collective-permute-start(bf16[1024,4096]{1,0:T(8,128)(2,1)} %all-gather.9.cloned.1.call-done.inner_ref.refs_6_.refs_8_), channel_id=1, source_target_pairs={{0,16},{16,0},{1,17},{17,1},{2,18},{18,2},{3,19},{19,3},{4,20},{20... | collective-permute-start | bytes 25165832 | tf_op jit(solution)/shard_map/ppermute | solution.py:465
  469.9 23.2 %collective-permute-start.7 = (bf16[128,2048]{1,0:T(8,128)(2,1)S(1)}, bf16[128,2048]{1,0:T(8,128)(2,1)S(1)}, u32[]{:S(2)}, u32[]{:S(2)}) collective-permute-start(bf16[128,2048]{1,0:T(8,128)(2,1)S(1)} %get-tuple-element.237), channel_id=1, source_target_pairs={{0,8},{4,12},{8,0},{12,4},{1,9},{5,13},{9,1},{13,5},{2,10},{6,14},... | collective-permute-start | bytes 1572872 | tf_op jit(solution)/shard_map/ppermute | solution.py:546
  471.1 22.1 %collective-permute-start.11 = (bf16[128,2048]{1,0:T(8,128)(2,1)S(1)}, bf16[128,2048]{1,0:T(8,128)(2,1)S(1)}, u32[]{:S(2)}, u32[]{:S(2)}) collective-permute-start(bf16[128,2048]{1,0:T(8,128)(2,1)S(1)} %get-tuple-element.235), channel_id=1, source_target_pairs={{0,8},{4,12},{8,0},{12,4},{1,9},{5,13},{9,1},{13,5},{2,10},{6,14},... | collective-permute-start | bytes 1572872 | tf_op jit(solution)/shard_map/ppermute | solution.py:546
  479.9 24.4 %collective-permute-start.9 = (bf16[128,2048]{1,0:T(8,128)(2,1)S(1)}, bf16[128,2048]{1,0:T(8,128)(2,1)S(1)}, u32[]{:S(2)}, u32[]{:S(2)}) collective-permute-start(bf16[128,2048]{1,0:T(8,128)(2,1)S(1)} %collective-permute-done.8), channel_id=1, source_target_pairs={{0,8},{4,12},{8,0},{12,4},{1,9},{5,13},{9,1},{13,5},{2,10},{6,14},... | collective-permute-start | bytes 1572872 | tf_op jit(solution)/shard_map/ppermute | solution.py:546
  483.1 22.9 %collective-permute-start.10 = (bf16[128,2048]{1,0:T(8,128)(2,1)S(1)}, bf16[128,2048]{1,0:T(8,128)(2,1)S(1)}, u32[]{:S(2)}, u32[]{:S(2)}) collective-permute-start(bf16[128,2048]{1,0:T(8,128)(2,1)S(1)} %get-tuple-element.235), channel_id=1, source_target_pairs={{0,4},{4,0},{8,12},{12,8},{1,5},{5,1},{9,13},{13,9},{2,6},{6,2},{1... | collective-permute-start | bytes 1572872 | tf_op jit(solution)/shard_map/ppermute | solution.py:546
  508.5 22.4 %collective-permute-start.14 = (bf16[1024,2048]{1,0:T(8,128)(2,1)}, bf16[1024,2048]{1,0:T(8,128)(2,1)S(1)}, u32[]{:S(2)}, u32[]{:S(2)}) collective-permute-start(bf16[1024,2048]{1,0:T(8,128)(2,1)} %all-gather.11.cloned.1.call-done.down_ref.refs_10_), channel_id=1, source_target_pairs={{0,16},{16,0},{1,17},{17,1},{2,18},{18,2},{3,19},{19,3},{4,20},{20... | collective-permute-start | bytes 12582920 | tf_op jit(solution)/shard_map/ppermute | solution.py:465
  637.1 186.5 %reduce-scatter.10.cloned.1.call-start = ((), (), s32[]{:S(2)}) async-start(), calls=%async_computation.14 | async-start | bytes 5242880 | tf_op jit(solution)/shard_map/reduce_scatter | solution.py:1464
  637.2 64.6 %collective-permute-start.16 = (bf16[1024,2048]{1,0:T(8,128)(2,1)}, bf16[1024,2048]{1,0:T(8,128)(2,1)S(1)}, u32[]{:S(2)}, u32[]{:S(2)}) collective-permute-start(bf16[1024,2048]{1,0:T(8,128)(2,1)} %weight_pass.10), channel_id=1, source_target_pairs={{0,16},{16,0},{1,17},{17,1},{2,18},{18,2},{3,19},{19,3},{4,20},{20... | collective-permute-start | bytes 12582920 | tf_op jit(solution)/shard_map/ppermute | solution.py:465
  718.5 173.5 %reduce-scatter.8.cloned.1.call-start = ((), (), s32[]{:S(2)}) async-start(), calls=%async_computation.13 | async-start | bytes 5242880 | tf_op jit(solution)/shard_map/reduce_scatter | solution.py:1549
  775.2 74.1 %collective-permute-start.18 = (bf16[1024,2048]{1,0:T(8,128)(2,1)}, bf16[1024,2048]{1,0:T(8,128)(2,1)}, u32[]{:S(2)}, u32[]{:S(2)}) collective-permute-start(bf16[1024,2048]{1,0:T(8,128)(2,1)} %weight_pass.12), channel_id=1, source_target_pairs={{0,16},{16,0},{1,17},{17,1},{2,18},{18,2},{3,19},{19,3},{4,20},{20... | collective-permute-start | bytes 12582920 | tf_op jit(solution)/shard_map/ppermute | solution.py:465
  783.2 34.9 %all-to-all-start.2 = ((bf16[8,256,256]{2,1,0:T(8,128)(2,1)}), bf16[8,256,256]{2,1,0:T(8,128)(2,1)S(1)}, u32[]{:S(2)}, u32[]{:S(2)}) async-start(bf16[8,256,256]{2,1,0:T(8,128)(2,1)} %bitcast.136), calls=%async_computation.4 | async-start | bytes 2097152 | tf_op jit(solution)/shard_map/all_to_all | solution.py:1503
  818.1 31.2 %all-to-all-start.3 = ((bf16[8,256,256]{2,1,0:T(8,128)(2,1)}), bf16[8,256,256]{2,1,0:T(8,128)(2,1)S(1)}, u32[]{:S(2)}, u32[]{:S(2)}) async-start(bf16[8,256,256]{2,1,0:T(8,128)(2,1)} %bitcast.153), calls=%async_computation.6 | async-start | bytes 2097152 | tf_op jit(solution)/shard_map/all_to_all | solution.py:1503
  823.6 145.2 %reduce-scatter.12.cloned.1.call-start = ((), (), s32[]{:S(2)}) async-start(), calls=%async_computation.15 | async-start | bytes 5242880 | tf_op jit(solution)/shard_map/reduce_scatter | solution.py:1464
  864.6 353.7 %reduce-scatter.14.cloned.1.call-start = ((), (), s32[]{:S(2)}) async-start(), calls=%async_computation.16 | async-start | bytes 5242880 | tf_op jit(solution)/shard_map/reduce_scatter | solution.py:1549
  873.0 56.5 %collective-permute-start.20 = (bf16[2048,1024]{1,0:T(8,128)(2,1)}, bf16[2048,1024]{1,0:T(8,128)(2,1)}, u32[]{:S(2)}, u32[]{:S(2)}) collective-permute-start(bf16[2048,1024]{1,0:T(8,128)(2,1)} %weight_pass.16), channel_id=1, source_target_pairs={{0,16},{16,0},{1,17},{17,1},{2,18},{18,2},{3,19},{19,3},{4,20},{20... | collective-permute-start | bytes 12582920 | tf_op jit(solution)/shard_map/ppermute | solution.py:465
  873.1 366.0 %all-gather.13.cloned.1.call-start = ((), (), s32[]{:S(2)}) async-start(), calls=%async_computation.17 | async-start | bytes 2162688 | tf_op jit(solution)/shard_map/all_gather | solution.py:1609
  884.9 53.7 %collective-permute-start.17 = (bf16[1024,2048]{1,0:T(8,128)(2,1)}, bf16[1024,2048]{1,0:T(8,128)(2,1)}, u32[]{:S(2)}, u32[]{:S(2)}) collective-permute-start(bf16[1024,2048]{1,0:T(8,128)(2,1)} %get-tuple-element.133), channel_id=1, source_target_pairs={{0,16},{16,0},{1,17},{17,1},{2,18},{18,2},{3,19},{19,3},{4,20},{20... | collective-permute-start | bytes 12582920 | tf_op jit(solution)/shard_map/ppermute | solution.py:465
  890.7 35.8 %collective-permute-start.22 = (bf16[256,2048]{1,0:T(8,128)(2,1)}, bf16[256,2048]{1,0:T(8,128)(2,1)}, u32[]{:S(2)}, u32[]{:S(2)}) collective-permute-start(bf16[256,2048]{1,0:T(8,128)(2,1)} %reduce-scatter.6.cloned.1.call-done), channel_id=1, source_target_pairs={{0,16},{16,0},{1,17},{17,1},{2,18},{18,2},{3,19},{19,3},{4,20},{20... | collective-permute-start | bytes 3145736 | tf_op jit(solution)/shard_map/ppermute | solution.py:465
  920.8 56.3 %collective-permute-start.19 = (bf16[1024,2048]{1,0:T(8,128)(2,1)}, bf16[1024,2048]{1,0:T(8,128)(2,1)}, u32[]{:S(2)}, u32[]{:S(2)}) collective-permute-start(bf16[1024,2048]{1,0:T(8,128)(2,1)} %get-tuple-element.141), channel_id=1, source_target_pairs={{0,16},{16,0},{1,17},{17,1},{2,18},{18,2},{3,19},{19,3},{4,20},{20... | collective-permute-start | bytes 12582920 | tf_op jit(solution)/shard_map/ppermute | solution.py:465
  971.2 15.7 %collective-permute-start.21 = (bf16[256,4096]{1,0:T(8,128)(2,1)}, bf16[256,4096]{1,0:T(8,128)(2,1)}, u32[]{:S(2)}, u32[]{:S(2)}) collective-permute-start(bf16[256,4096]{1,0:T(8,128)(2,1)} %constant_dynamic-update-slice_fusion.16), channel_id=1, source_target_pairs={{0,16},{16,0},{1,17},{17,1},{2,18},{18,2},{3,19},{19,3},{4,20},{20... | collective-permute-start | bytes 6291464 | tf_op jit(solution)/shard_map/ppermute | solution.py:465
  (92 other events, 2492.3 us)
Sparse Core Ops, SparseCore 0:
  10.6 94.3 all-gather.14
  107.2 102.6 all-gather.6
  218.5 193.2 all-gather.8
  413.2 80.2 all-gather.10
  637.2 77.3 reduce-scatter.5
  718.6 80.4 reduce-scatter.9
  802.1 54.2 reduce-scatter.7
  864.8 81.6 reduce-scatter.11
  949.5 52.6 reduce-scatter.13
  1005.4 103.6 all-gather.12
